TPU v7x, 32 devices: a whole 2x2x4 slice. The times are simulated.
32 devices in a mesh: sub: 4 (over z), blk: 8 (over y, x, core).
Axes of the slice: x: 2, y: 2, z: 4, core: 2. Of those that a mesh axis runs over, the one named last changes fastest.
Arguments:
- mode_blocks: float32 [36864, 1024], P(('sub', 'blk')), may hold values from -6 to 6
- stiffness: bfloat16 [8192, 5760], P(('sub', 'blk')), may hold values from -0.078125 to 0.078125
- mass_tiles: bfloat16 [8192, 5760], P(('sub', 'blk')), may hold values from -0.078125 to 0.078125
- reader_ids: int32 [32, 5], P(('sub', 'blk')), may hold values from 0 to 31, as said below
- owner_slot: int32 [32], replicated, may hold values from 0 to 31, as said below
- tile_mask: int32 [64, 45], P(('sub', 'blk')), may hold values 0 or 1
- tree_order: int32 [8192], P(('sub', 'blk')), may hold values from 0 to 255, as said below
Outputs:
- stiff_tree: bfloat16 [8192, 1024], P(('sub', 'blk'))
- mass_tree: bfloat16 [8192, 1024], P(('sub', 'blk'))
Inputs may be any that keep to these rules, and one draw needn't show every extreme that they name: A permutation: interface i is held at slot owner_slot[i]. `reader_ids`: the 5 interfaces of a row block are distinct, include the one held at its own slot, and are held at slots no more than 4 away from its own index. `tree_order`: within each row block a permutation of 0 to 255.
All inputs are finite; a program needn't handle non-finite values. No bound on the sum of `tile_mask` on one device may be relied on, other than what follows from the above.
Results may differ from a plain program's by a relative error of at most 0.001.
Values may be sent and summed in bfloat16 or wider, within the bound.
No kernel may reach another device: no remote copies, remote signals or barrier semaphores. Data moves between devices by JAX's collectives and lax.ppermute only.
A program may use at most 192 MiB of HBM per device.

v0:
```python
import jax
import jax.numpy as jnp
from jax import lax
from jax.sharding import PartitionSpec as P

TILE = 128
REACH = 4


def from_behind(shard, axis, by):
    count = lax.axis_size(axis)
    pairs = [(i, i + by) for i in range(count) if 0 <= i + by < count]
    return lax.ppermute(shard, axis, pairs)


def masked_tiles(block, mask):
    shaped = block.astype(jnp.float32).reshape(mask.shape[0], TILE, mask.shape[1], TILE)
    return (shaped * mask.astype(jnp.float32)[:, None, :, None]).reshape(block.shape)


def full_dot(left, right):
    return jnp.dot(left, right, precision=lax.Precision.HIGHEST, preferred_element_type=jnp.float32)


def per_device(mode_blocks, stiffness, mass_tiles, reader_ids, owner_slot, tile_mask, tree_order):
    iface_rows, modes = mode_blocks.shape
    row_count = stiffness.shape[0]
    reads = reader_ids.shape[1]
    span = 2 * REACH + 1
    own_index = lax.axis_index(("sub", "blk"))
    matches = reader_ids[0][:, None] == jnp.arange(owner_slot.shape[0], dtype=jnp.int32)[None, :]
    slots = jnp.sum(jnp.where(matches, owner_slot[None, :], 0), axis=1)
    position = slots - own_index + REACH
    stacked = jnp.concatenate(
        [masked_tiles(stiffness, tile_mask), masked_tiles(mass_tiles, tile_mask)], axis=0
    )
    stacked = stacked.reshape(2 * row_count, reads, iface_rows)
    total = jnp.zeros((2 * row_count, modes), jnp.float32)
    for offset in range(span):
        if offset == REACH:
            block = mode_blocks
        else:
            block = from_behind(mode_blocks, ("sub", "blk"), REACH - offset)
        pick = (position == offset).astype(jnp.float32)
        total = total + full_dot(jnp.sum(stacked * pick[None, :, None], axis=1), block)
    stiff_proj = total[:row_count].astype(jnp.bfloat16)
    mass_proj = total[row_count:].astype(jnp.bfloat16)
    stiff_rows, mass_rows = (
        lax.all_to_all(stiff_proj, "blk", split_axis=0, concat_axis=0, tiled=True),
        lax.all_to_all(mass_proj, "blk", split_axis=0, concat_axis=0, tiled=True),
    )
    stiff_tree = jnp.take(stiff_rows, tree_order, axis=0)
    mass_tree = jnp.take(mass_rows, tree_order, axis=0)
    return (stiff_tree, mass_tree)


def solution(mesh):
    return jax.shard_map(
        per_device,
        mesh=mesh,
        in_specs=(
            P(("sub", "blk"), None),
            P(("sub", "blk"), None),
            P(("sub", "blk"), None),
            P(("sub", "blk"), None),
            P(),
            P(("sub", "blk"), None),
            P(("sub", "blk")),
        ),
        out_specs=(P(("sub", "blk"), None), P(("sub", "blk"), None)),
        check_vma=False,
    )
```

profile of v0, /device:TPU:15, one launch (start us, length us, event | category | flops | bytes accessed | tf_op | source)
XLA Modules:
  0.0 730.7 jit_solution(5756581089626071181)
XLA Ops:
  0.6 3.2 collective-permute-start
  3.8 4.0 collective-permute-start.1
  7.8 3.1 collective-permute-start.2
  10.9 2.8 collective-permute-start.3
  13.7 1.9 collective-permute-start.4
  15.7 0.7 convert_element_type.76
  16.4 0.1 copy.16
  16.5 4.2 copy.15
  20.7 4.7 copy.17
  25.4 1.6 mul.93
  27.0 0.0 copy-start.7
  27.0 0.0 copy-start.8
  27.0 7.3 bitcast_multiply_fusion.1
  34.3 0.0 copy-done.7
  34.3 0.2 select_reduce_fusion
  34.5 121.6 %collective-permute-done = f32[1152,1024]{1,0:T(8,128)} collective-permute-done((f32[1152,1024]{1,0:T(8,128)}, f32[1152,1024]{1,0:T(8,128)}, u32[]{:S(2)}, u32[]{:S(2)}) %collective-permute-start) | collective-permute-done | bytes 4718624 | tf_op jit(solution)/shard_map/ppermute | solution.py:13
  156.1 153.8 %collective-permute-start.5 = (f32[1152,1024]{1,0:T(8,128)}, f32[1152,1024]{1,0:T(8,128)}, u32[]{:S(2)}, u32[]{:S(2)}) collective-permute-start(f32[1152,1024]{1,0:T(8,128)} %param.9), channel_id=1, source_target_pairs={{2,0},{3,1},{4,2},{5,3},{6,4},{7,5},{8,6},{9,7},{10,8},{11,9},{12,... | collective-permute-start | bytes 14155784 | tf_op jit(solution)/shard_map/ppermute | solution.py:13
  309.9 0.0 collective-permute-done.1
  309.9 52.0 %collective-permute-start.6 = (f32[1152,1024]{1,0:T(8,128)}, f32[1152,1024]{1,0:T(8,128)}, u32[]{:S(2)}, u32[]{:S(2)}) collective-permute-start(f32[1152,1024]{1,0:T(8,128)} %param.9), channel_id=1, source_target_pairs={{3,0},{4,1},{5,2},{6,3},{7,4},{8,5},{9,6},{10,7},{11,8},{12,9},{13... | collective-permute-start | bytes 14155784 | tf_op jit(solution)/shard_map/ppermute | solution.py:13
  361.9 0.0 collective-permute-done.2
  361.9 2.2 collective-permute-start.7
  364.1 36.7 %multiply_reduce_fusion.7 = (f32[512,1152]{0,1:T(8,128)}, f32[512,1152]{0,1:T(8,128)}, f32[512,1152]{0,1:T(8,128)}, f32[512,1152]{0,1:T(8,128)}, f32[512,1152]{0...) fusion(f32[5]{0:T(128)S(1)} %get-tuple-element.29, ...), kind=kLoop, calls=%fused_computation.10 | loop fusion | flops 50724864 | bytes 33030324 | tf_op jit(solution)/shard_map/reduce_sum | solution.py:45
  400.8 11.3 %fusion.5 = f32[512,1024]{1,0:T(8,128)S(1)} fusion(f32[512,1152]{0,1:T(8,128)} %get-tuple-element.6, f32[1152,1024]{1,0:T(8,128)} %param.9), kind=kOutput, calls=%fused_computation.37 | convolution fusion | flops 7247757312 | bytes 9175040 | tf_op jit(solution)/shard_map/dot_general | solution.py:22
  412.1 0.0 copy-done.5
  412.1 0.0 copy-start.4
  412.2 11.5 %fusion.1 = f32[512,1024]{1,0:T(8,128)S(1)} fusion(f32[512,1152]{0,1:T(8,128)S(1)} %copy-done.5, f32[1152,1024]{1,0:T(8,128)} %collective-permute-done), kind=kOutput, calls=%fused_computation.33 | convolution fusion | flops 7247757312 | bytes 9175040 | tf_op jit(solution)/shard_map/dot_general | solution.py:22
  423.6 10.9 %fusion.2 = f32[512,1024]{1,0:T(8,128)S(1)} fusion(f32[512,1152]{0,1:T(8,128)S(1)} %copy-done.4, f32[1152,1024]{1,0:T(8,128)} %collective-permute-done.1), kind=kOutput, calls=%fused_computation.34 | convolution fusion | flops 7247757312 | bytes 9175040 | tf_op jit(solution)/shard_map/dot_general | solution.py:22
  434.6 11.1 %fusion.3 = f32[512,1024]{1,0:T(8,128)S(1)} fusion(f32[512,1152]{0,1:T(8,128)S(1)} %copy-done.3, f32[1152,1024]{1,0:T(8,128)} %collective-permute-done.2), kind=kOutput, calls=%fused_computation.35 | convolution fusion | flops 7247757312 | bytes 9175040 | tf_op jit(solution)/shard_map/dot_general | solution.py:22
  445.7 0.0 collective-permute-done.3
  445.7 0.0 copy-done.2
  445.7 0.0 copy-start.1
  445.7 10.9 %fusion.4 = f32[512,1024]{1,0:T(8,128)S(1)} fusion(f32[512,1152]{0,1:T(8,128)S(1)} %copy-done.2, f32[1152,1024]{1,0:T(8,128)} %collective-permute-done.3), kind=kOutput, calls=%fused_computation.36 | convolution fusion | flops 7247757312 | bytes 9175040 | tf_op jit(solution)/shard_map/dot_general | solution.py:22
  456.6 0.0 collective-permute-done.4
  456.6 11.1 %fusion.6 = f32[512,1024]{1,0:T(8,128)S(1)} fusion(f32[512,1152]{0,1:T(8,128)S(1)} %copy-done.1, f32[1152,1024]{1,0:T(8,128)} %collective-permute-done.4), kind=kOutput, calls=%fused_computation.38 | convolution fusion | flops 7247757312 | bytes 9175040 | tf_op jit(solution)/shard_map/dot_general | solution.py:22
  467.7 16.5 %collective-permute-done.5 = f32[1152,1024]{1,0:T(8,128)} collective-permute-done((f32[1152,1024]{1,0:T(8,128)}, f32[1152,1024]{1,0:T(8,128)}, u32[]{:S(2)}, u32[]{:S(2)}) %collective-permute-start.5) | collective-permute-done | bytes 4718624 | tf_op jit(solution)/shard_map/ppermute | solution.py:13
  484.3 10.8 %fusion.7 = f32[512,1024]{1,0:T(8,128)S(1)} fusion(f32[512,1152]{0,1:T(8,128)S(1)} %copy-done, f32[1152,1024]{1,0:T(8,128)} %collective-permute-done.5), kind=kOutput, calls=%fused_computation.39 | convolution fusion | flops 7247757312 | bytes 9175040 | tf_op jit(solution)/shard_map/dot_general | solution.py:22
  495.0 15.0 %collective-permute-done.6 = f32[1152,1024]{1,0:T(8,128)} collective-permute-done((f32[1152,1024]{1,0:T(8,128)}, f32[1152,1024]{1,0:T(8,128)}, u32[]{:S(2)}, u32[]{:S(2)}) %collective-permute-start.6) | collective-permute-done | bytes 4718624 | tf_op jit(solution)/shard_map/ppermute | solution.py:13
  510.1 11.0 %fusion.8 = f32[512,1024]{1,0:T(8,128)S(1)} fusion(f32[512,1152]{0,1:T(8,128)S(1)} %get-tuple-element.15, f32[1152,1024]{1,0:T(8,128)} %collective-permute-done.6), kind=kOutput, calls=%fused_computation.40 | convolution fusion | flops 7247757312 | bytes 9175040 | tf_op jit(solution)/shard_map/dot_general | solution.py:22
  521.1 64.2 %collective-permute-done.7 = f32[1152,1024]{1,0:T(8,128)} collective-permute-done((f32[1152,1024]{1,0:T(8,128)}, f32[1152,1024]{1,0:T(8,128)}, u32[]{:S(2)}, u32[]{:S(2)}) %collective-permute-start.7) | collective-permute-done | bytes 4718624 | tf_op jit(solution)/shard_map/ppermute | solution.py:13
  585.3 11.1 %add_convert_fusion = bf16[512,1024]{1,0:T(8,128)(2,1)S(1)} fusion(f32[512,1024]{1,0:T(8,128)S(1)} %fusion.8, f32[512,1024]{1,0:T(8,128)S(1)} %fusion.7, f32[512,1024]{1,0:T(8,128)S(1)} %fusion.6, f32[512,1024]{1,0:T(8,128)S(1)} %fusion.5, f32[512,1024]{1,0:T(8,128)S(1)} %fusion.4, f32[512,1024]{1,0:T(8,128)S(1)} %fusion.3, f32[512,1024]{1,0:T(8,128)S(1)} %fusion.1, ...), kind=kOutput, calls=%fused_computation.14 | convolution fusion | flops 7252475904 | bytes 24903680 | tf_op jit(solution)/shard_map/dot_general | solution.py:22
  596.3 0.0 copy-start.6
  596.3 0.9 fusion
  597.2 117.7 %all_to_all.24 = bf16[8,32,1024]{2,1,0:T(8,128)(2,1)S(1)} all-to-all(bf16[8,32,1024]{2,1,0:T(8,128)(2,1)S(1)} %bitcast.37), channel_id=1, replica_groups=mesh['sub'=4,'blk'=8] {'blk'}, dimensions={0} | all-to-all | bytes 1048576 | tf_op jit(solution)/shard_map/all_to_all | solution.py:49
  714.9 6.1 all-to-all-start.1
  721.1 1.2 gather_fusion
  722.3 5.9 all-to-all-done.1
  728.1 1.2 gather_fusion.1
  729.3 1.1 broadcast_select_fusion
  (15 shorter events, 0.1 us)
Async XLA Ops:
  0.6 155.4 %collective-permute-start = (f32[1152,1024]{1,0:T(8,128)}, f32[1152,1024]{1,0:T(8,128)}, u32[]{:S(2)}, u32[]{:S(2)}) collective-permute-start(f32[1152,1024]{1,0:T(8,128)} %param.9), channel_id=1, source_target_pairs={{0,4},{1,5},{2,6},{3,7},{4,8},{5,9},{6,10},{7,11},{8,12},{9,13},{1... | collective-permute-start | bytes 14155784 | tf_op jit(solution)/shard_map/ppermute | solution.py:13
  3.8 306.1 %collective-permute-start.1 = (f32[1152,1024]{1,0:T(8,128)}, f32[1152,1024]{1,0:T(8,128)}, u32[]{:S(2)}, u32[]{:S(2)}) collective-permute-start(f32[1152,1024]{1,0:T(8,128)} %param.9), channel_id=1, source_target_pairs={{0,3},{1,4},{2,5},{3,6},{4,7},{5,8},{6,9},{7,10},{8,11},{9,12},{10... | collective-permute-start | bytes 14155784 | tf_op jit(solution)/shard_map/ppermute | solution.py:13
  7.8 354.1 %collective-permute-start.2 = (f32[1152,1024]{1,0:T(8,128)}, f32[1152,1024]{1,0:T(8,128)}, u32[]{:S(2)}, u32[]{:S(2)}) collective-permute-start(f32[1152,1024]{1,0:T(8,128)} %param.9), channel_id=1, source_target_pairs={{0,2},{1,3},{2,4},{3,5},{4,6},{5,7},{6,8},{7,9},{8,10},{9,11},{10,... | collective-permute-start | bytes 14155784 | tf_op jit(solution)/shard_map/ppermute | solution.py:13
  10.9 434.7 %collective-permute-start.3 = (f32[1152,1024]{1,0:T(8,128)}, f32[1152,1024]{1,0:T(8,128)}, u32[]{:S(2)}, u32[]{:S(2)}) collective-permute-start(f32[1152,1024]{1,0:T(8,128)} %param.9), channel_id=1, source_target_pairs={{0,1},{1,2},{2,3},{3,4},{4,5},{5,6},{6,7},{7,8},{8,9},{9,10},{10,1... | collective-permute-start | bytes 14155784 | tf_op jit(solution)/shard_map/ppermute | solution.py:13
  13.7 442.9 %collective-permute-start.4 = (f32[1152,1024]{1,0:T(8,128)}, f32[1152,1024]{1,0:T(8,128)}, u32[]{:S(2)}, u32[]{:S(2)}) collective-permute-start(f32[1152,1024]{1,0:T(8,128)} %param.9), channel_id=1, source_target_pairs={{1,0},{2,1},{3,2},{4,3},{5,4},{6,5},{7,6},{8,7},{9,8},{10,9},{11,1... | collective-permute-start | bytes 14155784 | tf_op jit(solution)/shard_map/ppermute | solution.py:13
  27.0 7.3 %copy-start.7 = (s32[32]{0:T(128)S(1)}, s32[32]{0:T(128)}, u32[]{:S(2)}) copy-start(s32[32]{0:T(128)} %param.13) | copy-start | bytes 388
  27.0 7.3 copy-start.8
  156.1 328.2 %collective-permute-start.5 = (f32[1152,1024]{1,0:T(8,128)}, f32[1152,1024]{1,0:T(8,128)}, u32[]{:S(2)}, u32[]{:S(2)}) collective-permute-start(f32[1152,1024]{1,0:T(8,128)} %param.9), channel_id=1, source_target_pairs={{2,0},{3,1},{4,2},{5,3},{6,4},{7,5},{8,6},{9,7},{10,8},{11,9},{12,... | collective-permute-start | bytes 14155784 | tf_op jit(solution)/shard_map/ppermute | solution.py:13
  309.9 200.1 %collective-permute-start.6 = (f32[1152,1024]{1,0:T(8,128)}, f32[1152,1024]{1,0:T(8,128)}, u32[]{:S(2)}, u32[]{:S(2)}) collective-permute-start(f32[1152,1024]{1,0:T(8,128)} %param.9), channel_id=1, source_target_pairs={{3,0},{4,1},{5,2},{6,3},{7,4},{8,5},{9,6},{10,7},{11,8},{12,9},{13... | collective-permute-start | bytes 14155784 | tf_op jit(solution)/shard_map/ppermute | solution.py:13
  361.9 223.3 %collective-permute-start.7 = (f32[1152,1024]{1,0:T(8,128)}, f32[1152,1024]{1,0:T(8,128)}, u32[]{:S(2)}, u32[]{:S(2)}) collective-permute-start(f32[1152,1024]{1,0:T(8,128)} %param.9), channel_id=1, source_target_pairs={{4,0},{5,1},{6,2},{7,3},{8,4},{9,5},{10,6},{11,7},{12,8},{13,9},{1... | collective-permute-start | bytes 14155784 | tf_op jit(solution)/shard_map/ppermute | solution.py:13
  400.8 11.3 %copy-start.5 = (f32[512,1152]{0,1:T(8,128)S(1)}, f32[512,1152]{0,1:T(8,128)}, u32[]{:S(2)}) copy-start(f32[512,1152]{0,1:T(8,128)} %get-tuple-element.16) | copy-start | bytes 7077892
  412.1 11.5 %copy-start.4 = (f32[512,1152]{0,1:T(8,128)S(1)}, f32[512,1152]{0,1:T(8,128)}, u32[]{:S(2)}) copy-start(f32[512,1152]{0,1:T(8,128)} %get-tuple-element.3) | copy-start | bytes 7077892
  423.6 10.9 %copy-start.3 = (f32[512,1152]{0,1:T(8,128)S(1)}, f32[512,1152]{0,1:T(8,128)}, u32[]{:S(2)}) copy-start(f32[512,1152]{0,1:T(8,128)} %get-tuple-element.4) | copy-start | bytes 7077892
  434.6 11.1 %copy-start.2 = (f32[512,1152]{0,1:T(8,128)S(1)}, f32[512,1152]{0,1:T(8,128)}, u32[]{:S(2)}) copy-start(f32[512,1152]{0,1:T(8,128)} %get-tuple-element.5) | copy-start | bytes 7077892
  445.7 10.9 %copy-start.1 = (f32[512,1152]{0,1:T(8,128)S(1)}, f32[512,1152]{0,1:T(8,128)}, u32[]{:S(2)}) copy-start(f32[512,1152]{0,1:T(8,128)} %get-tuple-element.7) | copy-start | bytes 7077892
  456.6 27.6 %copy-start = (f32[512,1152]{0,1:T(8,128)S(1)}, f32[512,1152]{0,1:T(8,128)}, u32[]{:S(2)}) copy-start(f32[512,1152]{0,1:T(8,128)} %get-tuple-element.8) | copy-start | bytes 7077892
  596.3 124.7 %copy-start.6 = (s32[256]{0:T(256)S(1)}, s32[256]{0:T(256)}, u32[]{:S(2)}) copy-start(s32[256]{0:T(256)} %param.15) | copy-start | bytes 3076
  714.9 13.2 %all-to-all-start.1 = ((bf16[8,32,1024]{2,1,0:T(8,128)(2,1)}), bf16[8,32,1024]{2,1,0:T(8,128)(2,1)S(1)}, u32[]{:S(2)}, u32[]{:S(2)}) async-start(bf16[8,32,1024]{2,1,0:T(8,128)(2,1)} %bitcast.5), calls=%async_computation.1 | async-start | bytes 1048576 | tf_op jit(solution)/shard_map/all_to_all | solution.py:50
where the time goes:
time: 738 us; the launch traced here: 731 us
  starting transfers between devices  229 us (31%)
  waiting for transfers between devices  223 us (30%)
  blocking collectives  118 us (16%)
  matrix products  99.6 us (13%)
  other arithmetic  46 us (6%)
  local copies, waits for them, and re-layouts  13.9 us (2%)
    ppermute x8, starting transfers between devices, from_behind(): return lax.ppermute(shard, axis, pairs)  223 us
    ppermute x8, waiting for transfers between devices, from_behind(): return lax.ppermute(shard, axis, pairs)  217 us
    all_to_all x1, blocking collectives, per_device(): lax.all_to_all(stiff_proj, 'blk', split_axis=0, concat_axis=0, tiled=True)  118 us
    dot_general x9, matrix products, full_dot(): jnp.dot(left, right, precision=lax.Precision.HIGHEST, preferred_element_t...  99.6 us
    reduce_sum x1, other arithmetic, per_device(): jnp.sum(stacked * pick[None, :, None], axis=1)  36.7 us
  transfers between devices with their start and end apart: 9, of which 5 were waited for; matrix products, arithmetic and copies ran while one was open for 20% of the time, Pallas kernels for 0%

commit v1 on v0

v1 whole, which is shorter than its diff:
```python
import functools

import jax
import jax.numpy as jnp
from jax import lax
from jax.experimental import pallas as pl
from jax.experimental.pallas import tpu as pltpu
from jax.sharding import PartitionSpec as P

TILE = 128
REACH = 4
AXES = ("sub", "blk")
STEPS = 64.0
TOP = 32760.0
CODE_ROWS = 16


def quantize(x_ref, q_ref):
    tiles = x_ref.shape[0] // TILE
    codes = []
    for t in range(tiles):
        rows = pl.ds(t * TILE, TILE)
        x = x_ref[rows, :]
        top = jnp.maximum(jnp.max(jnp.abs(x), axis=0, keepdims=True), 2.0**-120)
        code = jnp.ceil(jnp.log2(top) * STEPS + 0.5)
        q = x * (jnp.exp2(code * (-1.0 / STEPS)) * TOP)
        q = jnp.minimum(jnp.maximum(q, -32767.0), 32767.0)
        q_ref[rows, :] = jnp.round(q).astype(jnp.int32).astype(jnp.int16)
        codes.append(code.astype(jnp.int32))
    codes.append(jnp.zeros((CODE_ROWS - tiles, x_ref.shape[1]), jnp.int32))
    q_ref[pl.ds(tiles * TILE, CODE_ROWS), :] = jnp.concatenate(codes, axis=0).astype(jnp.int16)


def pack_kernel(place_ref, keep_in, send_in, keep_ref, send_ref):
    quantize(keep_in, keep_ref)
    quantize(send_in, send_ref)


def pack(place, mode_blocks, width):
    rows, modes = mode_blocks.shape
    half = modes // 2
    per_half = half // width
    out = jax.ShapeDtypeStruct((rows + CODE_ROWS, half), jnp.int16)
    return pl.pallas_call(
        pack_kernel,
        grid_spec=pltpu.PrefetchScalarGridSpec(
            num_scalar_prefetch=1,
            grid=(per_half,),
            in_specs=[
                pl.BlockSpec((rows, width), lambda i, place: (0, (place[0] % 2) * per_half + i)),
                pl.BlockSpec((rows, width), lambda i, place: (0, (1 - place[0] % 2) * per_half + i)),
            ],
            out_specs=[pl.BlockSpec((rows + CODE_ROWS, width), lambda i, place: (0, i))] * 2,
        ),
        out_shape=(out, out),
        compiler_params=pltpu.CompilerParams(vmem_limit_bytes=32 << 20),
        name="pack",
    )(place, mode_blocks, mode_blocks)


def project_kernel(reads, pieces, place_ref, owner_ref, *refs):
    ids, masks = refs[0:2], refs[2:4]
    stiff, mass = refs[4:6], refs[6:8]
    held = refs[8 : 8 + pieces]
    out_ref, total, left, high, low = refs[8 + pieces :]
    read = pl.program_id(0)
    core = place_ref[0] % 2
    first = place_ref[0] - core - REACH
    rows = stiff[0].shape[0]
    depth = high.shape[0]
    tiles = depth // TILE

    @pl.when(read == 0)
    def _():
        total[...] = jnp.zeros_like(total)

    for who in range(2):
        offset = owner_ref[ids[who][0, read]] - first
        piece = (offset // 2) * 2 + (offset % 2 + core) % 2
        for k in range(pieces):

            @pl.when(piece == k)
            def _(k=k):
                codes = held[k][pl.ds(depth, CODE_ROWS), :].astype(jnp.int32).astype(jnp.float32)
                scale = jnp.exp2(codes * (1.0 / STEPS)) * (1.0 / TOP)
                for t in range(tiles):
                    span = pl.ds(t * TILE, TILE)
                    value = held[k][span, :].astype(jnp.int32).astype(jnp.float32) * scale[t : t + 1, :]
                    top = value.astype(jnp.bfloat16)
                    high[span, :] = top
                    low[span, :] = (value - top.astype(jnp.float32)).astype(jnp.bfloat16)

        for kind, source in enumerate((stiff[who], mass[who])):
            for r in range(rows // TILE):
                for t in range(tiles):
                    keep = masks[who][r, read * tiles + t] != 0
                    tile = source[pl.ds(r * TILE, TILE), pl.ds(t * TILE, TILE)]
                    left[pl.ds(kind * rows + r * TILE, TILE), pl.ds(t * TILE, TILE)] = jnp.where(keep, tile, jnp.zeros_like(tile))
        total[who] += jnp.dot(left[...], high[...], preferred_element_type=jnp.float32) + jnp.dot(
            left[...], low[...], preferred_element_type=jnp.float32
        )

    @pl.when(read == reads - 1)
    def _():
        devices, _, _, part, _ = out_ref.shape
        for who in range(2):
            for kind in range(2):
                for j in range(devices):
                    out_ref[j, who, kind] = total[who, pl.ds(kind * rows + j * part, part), :].astype(jnp.bfloat16)


def project(place, owner_slot, ids, masks, stiff, mass, held, devices):
    rows, reads = stiff[0].shape[0], ids[0].shape[1]
    depth = stiff[0].shape[1] // reads
    width = held[0].shape[1]
    whole = pl.BlockSpec(held[0].shape, lambda r, *_: (0, 0), pipeline_mode=pl.Buffered(1))
    part = rows // devices
    return pl.pallas_call(
        functools.partial(project_kernel, reads, len(held)),
        grid_spec=pltpu.PrefetchScalarGridSpec(
            num_scalar_prefetch=6,
            grid=(reads,),
            in_specs=[pl.BlockSpec((rows, depth), lambda r, *_: (0, r))] * 4 + [whole] * len(held),
            out_specs=pl.BlockSpec((devices, 2, 2, part, width), lambda r, *_: (0, 0, 0, 0, 0)),
            scratch_shapes=[
                pltpu.VMEM((2, 2 * rows, width), jnp.float32),
                pltpu.VMEM((2 * rows, depth), jnp.bfloat16),
                pltpu.VMEM((depth, width), jnp.bfloat16),
                pltpu.VMEM((depth, width), jnp.bfloat16),
            ],
        ),
        out_shape=jax.ShapeDtypeStruct((devices, 2, 2, part, width), jnp.bfloat16),
        compiler_params=pltpu.CompilerParams(vmem_limit_bytes=48 << 20),
        cost_estimate=pl.CostEstimate(
            flops=2 * 2 * 2 * 2 * rows * depth * reads * width,
            bytes_accessed=4 * rows * depth * reads * 2 + len(held) * depth * width * 2,
            transcendentals=0,
        ),
        name="project",
    )(place, owner_slot, *ids, *masks, *stiff, *mass, *held)


def order_kernel(order_ref, rows_ref, stiff_ref, mass_ref):
    source = pl.program_id(0)
    chips, _, _, _, part, width = rows_ref.shape
    count = order_ref.shape[0]
    at = lax.broadcasted_iota(jnp.int32, (count, chips * 2 * part), 1)
    block = at // part
    owner = (block // 2) * 2 + (block % 2 + source) % 2
    pick = (order_ref[...] == owner * part + at % part).astype(jnp.bfloat16)
    for kind, ref in enumerate((stiff_ref, mass_ref)):
        rows = rows_ref[:, 0, :, kind]
        if part % 16:
            rows = rows.astype(jnp.float32).reshape(count, width).astype(jnp.bfloat16)
        else:
            rows = rows.reshape(count, width)
        ref[...] = jnp.dot(pick, rows, preferred_element_type=jnp.float32).astype(jnp.bfloat16)


def order_rows(tree_order, rows):
    chips, _, _, _, part, width = rows.shape
    count = tree_order.shape[0]
    out = jax.ShapeDtypeStruct((count, 2 * width), jnp.bfloat16)
    return pl.pallas_call(
        order_kernel,
        grid=(2,),
        in_specs=[
            pl.BlockSpec((count, 1), lambda s: (0, 0)),
            pl.BlockSpec((chips, 1, 2, 2, part, width), lambda s: (0, s, 0, 0, 0, 0)),
        ],
        out_specs=[pl.BlockSpec((count, width), lambda s: (0, s))] * 2,
        out_shape=(out, out),
        name="order",
    )(tree_order[:, None], rows)


def per_device(mode_blocks, stiffness, mass_tiles, reader_ids, owner_slot, tile_mask, tree_order):
    devices = lax.axis_size("blk")
    count = lax.axis_size("sub") * devices
    place = lax.axis_index(AXES).astype(jnp.int32).reshape(1)
    swap = [(i, i ^ 1) for i in range(count)]

    def partner(x):
        return lax.ppermute(x, AXES, swap)

    def shift(x, chips):
        by = 2 * chips
        return lax.ppermute(x, AXES, [(i, i + by) for i in range(count) if 0 <= i + by < count])

    keep, send = pack(place, mode_blocks, TILE)
    pair = (keep, partner(send))
    held = []
    for chips in range(-(REACH // 2), REACH // 2 + 1):
        for x in pair:
            held.append(shift(x, -chips) if chips else x)
    ids = (reader_ids, partner(reader_ids))
    masks = (tile_mask, partner(tile_mask))
    stiff = (stiffness, partner(stiffness))
    mass = (mass_tiles, partner(mass_tiles))
    rows = project(place, owner_slot, ids, masks, stiff, mass, held, devices)
    rows = lax.all_to_all(rows, "blk", split_axis=0, concat_axis=0, tiled=True)
    return order_rows(tree_order, rows.reshape(devices // 2, 2, *rows.shape[1:]))


def solution(mesh):
    spec = P(AXES, None)
    return jax.shard_map(
        per_device,
        mesh=mesh,
        in_specs=(spec, spec, spec, spec, P(), spec, P(AXES)),
        out_specs=(spec, spec),
        check_vma=False,
    )
```

time: 738 us -> 260 us (0.35)
  starting transfers between devices: 229 us -> 65.7 us
  blocking collectives: 118 us -> 0 us
  matrix products: 99.6 us -> 0 us
  waiting for transfers between devices: 223 us -> 153 us
  other arithmetic: 46 us -> 0 us
  Pallas kernels: 0 us -> 31.9 us
  local copies, waits for them, and re-layouts: 13.9 us -> 5.73 us
    ppermute x8 -> x13, starting transfers between devices: 223 us -> 48 us  [the longest x8 46 us: shift(): lax.ppermute(x, AXES, [(i, i + by) for i in range(count) if 0 <= i + by <...]
    all_to_all x1 -> x0, blocking collectives: 118 us -> none  [per_device(): lax.all_to_all(stiff_proj, 'blk', split_axis=0, concat_axis=0, tiled=True)]
    dot_general x9 -> x0, matrix products: 99.6 us -> none  [full_dot(): jnp.dot(left, right, precision=lax.Precision.HIGHEST, preferred_element_t...]
    ppermute x8 -> x13, waiting for transfers between devices: 217 us -> 141 us  [the longest x8 140 us: shift(): lax.ppermute(x, AXES, [(i, i + by) for i in range(count) if 0 <= i + by <...]
    reduce_sum x2 -> x0, other arithmetic: 36.9 us -> none  [the longest x1 36.7 us: per_device(): jnp.sum(stacked * pick[None, :, None], axis=1)]
    pallas_call x0 -> x3, Pallas kernels: none -> 31.9 us  [the longest x1 27.1 us: project(): pl.pallas_call(functools.partial(project_kernel, reads, len(held)), grid_...]
    all_to_all x1, starting transfers between devices: 6.15 us -> 17.7 us  [per_device(): rows = lax.all_to_all(rows, 'blk', split_axis=0, concat_axis=0, tiled=True)]
  transfers between devices with their start and end apart: 9 -> 14, of which waited for: 5 -> 8; matrix products, arithmetic and copies ran while one was open for 20% -> 0% of each run, Pallas kernels for 0% -> 0%
where the time goes in v1:
time: 260 us; the launch traced here: 257 us
  waiting for transfers between devices  153 us (59%)
  starting transfers between devices  65.7 us (25%)
  Pallas kernels  31.9 us (12%)
  local copies, waits for them, and re-layouts  5.73 us (2%)
    ppermute x8, waiting for transfers between devices, shift(): lax.ppermute(x, AXES, [(i, i + by) for i in range(count) if 0 <= i + by <...  140 us
    ppermute x8, starting transfers between devices, shift(): lax.ppermute(x, AXES, [(i, i + by) for i in range(count) if 0 <= i + by <...  46 us
    pallas_call x1, Pallas kernels, project(): pl.pallas_call(functools.partial(project_kernel, reads, len(held)), grid_...  27.1 us
    all_to_all x1, starting transfers between devices, per_device(): rows = lax.all_to_all(rows, 'blk', split_axis=0, concat_axis=0, tiled=True)  17.7 us
    all_to_all x1, waiting for transfers between devices, per_device(): rows = lax.all_to_all(rows, 'blk', split_axis=0, concat_axis=0, tiled=True)  11.9 us
  transfers between devices with their start and end apart: 14, of which 8 were waited for; matrix products, arithmetic and copies ran while one was open for 0% of the time, Pallas kernels for 0%

profile of v1, /device:TPU:15, one launch (start us, length us, event | category | flops | bytes accessed | tf_op | source)
XLA Modules:
  0.0 257.5 jit_solution(1363724868656210234)
XLA Ops:
  0.6 0.0 copy-start
  0.6 2.3 copy-done
  3.0 0.0 copy-start.3
  3.0 2.2 pack.1
  5.2 0.0 copy-start.1
  5.2 0.7 collective-permute-start.5
  6.0 2.1 collective-permute-start.11
  8.1 4.0 %collective-permute-start.4 = (s16[1168,512]{1,0:T(8,128)(2,1)S(1)}, s16[1168,512]{1,0:T(8,128)(2,1)S(1)}, u32[]{:S(2)}, u32[]{:S(2)}) collective-permute-start(s16[1168,512]{1,0:T(8,128)(2,1)S(1)} %get-tuple-element.4.refs_12_), channel_id=1, source_target_pairs={{0,4},{1,5},{2,6},{3,7},{4,8},{5,9},{6,10},{7,11},{8,12},{9,13},{1... | collective-permute-start | bytes 3588104 | tf_op jit(solution)/shard_map/ppermute | solution.py:188
  12.2 0.0 copy-done.2
  12.2 0.7 collective-permute-start.1
  12.8 0.0 copy-done.4
  12.8 0.1 collective-permute-start
  12.9 1.0 collective-permute-done.refs_1_
  13.9 0.0 copy-done.7
  14.0 0.2 collective-permute-start.2
  14.2 0.0 collective-permute-done.1.refs_3_
  14.2 0.0 copy-done.8
  14.2 0.3 collective-permute-start.3
  14.5 0.0 collective-permute-done.5.refs_13_
  14.5 2.2 collective-permute-start.7
  16.7 42.8 %collective-permute-done.11.refs_16_ = s16[1168,512]{1,0:T(8,128)(2,1)S(1)} collective-permute-done((s16[1168,512]{1,0:T(8,128)(2,1)S(1)}, s16[1168,512]{1,0:T(8,128)(2,1)S(1)}, u32[]{:S(2)}, u32[]{:S(2)}) %collective-permute-start.11) | collective-permute-done | bytes 1196064 | tf_op jit(solution)/shard_map/ppermute | solution.py:188
  59.4 27.8 %collective-permute-start.9 = (s16[1168,512]{1,0:T(8,128)(2,1)S(1)}, s16[1168,512]{1,0:T(8,128)(2,1)S(1)}, u32[]{:S(2)}, u32[]{:S(2)}) collective-permute-start(s16[1168,512]{1,0:T(8,128)(2,1)S(1)} %get-tuple-element.4.refs_12_), channel_id=1, source_target_pairs={{2,0},{3,1},{4,2},{5,3},{6,4},{7,5},{8,6},{9,7},{10,8},{11,9},{12,... | collective-permute-start | bytes 3588104 | tf_op jit(solution)/shard_map/ppermute | solution.py:188
  87.2 0.0 collective-permute-done.4.refs_8_
  87.2 3.2 %collective-permute-start.10 = (s16[1168,512]{1,0:T(8,128)(2,1)S(1)}, s16[1168,512]{1,0:T(8,128)(2,1)}, u32[]{:S(2)}, u32[]{:S(2)}) collective-permute-start(s16[1168,512]{1,0:T(8,128)(2,1)S(1)} %collective-permute-done.5.refs_13_), channel_id=1, source_target_pairs={{2,0},{3,1},{4,2},{5,3},{6,4},{7,5},{8,6},{9,7},{10,8},{11,9},{12,... | collective-permute-start | bytes 3588104 | tf_op jit(solution)/shard_map/ppermute | solution.py:188
  90.4 0.0 collective-permute-done.7.refs_10_
  90.5 2.8 %collective-permute-start.12 = (s16[1168,512]{1,0:T(8,128)(2,1)S(1)}, s16[1168,512]{1,0:T(8,128)(2,1)S(1)}, u32[]{:S(2)}, u32[]{:S(2)}) collective-permute-start(s16[1168,512]{1,0:T(8,128)(2,1)S(1)} %collective-permute-done.5.refs_13_), channel_id=1, source_target_pairs={{4,0},{5,1},{6,2},{7,3},{8,4},{9,5},{10,6},{11,7},{12,8},{13,9},{1... | collective-permute-start | bytes 3588104 | tf_op jit(solution)/shard_map/ppermute | solution.py:188
  93.3 38.8 %collective-permute-done.9.refs_14_ = s16[1168,512]{1,0:T(8,128)(2,1)S(1)} collective-permute-done((s16[1168,512]{1,0:T(8,128)(2,1)S(1)}, s16[1168,512]{1,0:T(8,128)(2,1)S(1)}, u32[]{:S(2)}, u32[]{:S(2)}) %collective-permute-start.9) | collective-permute-done | bytes 1196064 | tf_op jit(solution)/shard_map/ppermute | solution.py:188
  132.1 1.9 collective-permute-start.6
  134.0 33.4 %collective-permute-done.10.refs_15_ = s16[1168,512]{1,0:T(8,128)(2,1)} collective-permute-done((s16[1168,512]{1,0:T(8,128)(2,1)S(1)}, s16[1168,512]{1,0:T(8,128)(2,1)}, u32[]{:S(2)}, u32[]{:S(2)}) %collective-permute-start.10) | collective-permute-done | bytes 1196064 | tf_op jit(solution)/shard_map/ppermute | solution.py:188
  167.4 1.9 collective-permute-start.8
  169.3 20.6 %collective-permute-done.12.refs_17_ = s16[1168,512]{1,0:T(8,128)(2,1)S(1)} collective-permute-done((s16[1168,512]{1,0:T(8,128)(2,1)S(1)}, s16[1168,512]{1,0:T(8,128)(2,1)S(1)}, u32[]{:S(2)}, u32[]{:S(2)}) %collective-permute-start.12) | collective-permute-done | bytes 1196064 | tf_op jit(solution)/shard_map/ppermute | solution.py:188
  189.9 3.9 %collective-permute-done.6.refs_9_ = s16[1168,512]{1,0:T(8,128)(2,1)S(1)} collective-permute-done((s16[1168,512]{1,0:T(8,128)(2,1)S(1)}, s16[1168,512]{1,0:T(8,128)(2,1)S(1)}, u32[]{:S(2)}, u32[]{:S(2)}) %collective-permute-start.6) | collective-permute-done | bytes 1196064 | tf_op jit(solution)/shard_map/ppermute | solution.py:188
  193.8 0.9 collective-permute-done.8.refs_11_
  194.7 0.0 collective-permute-done.2.refs_5_
  194.7 0.0 copy-done.12
  194.7 0.0 copy-done.13
  194.8 0.0 copy-start.9
  194.8 1.6 copy-done.9
  196.3 0.0 collective-permute-done.3.refs_7_
  196.3 0.0 copy-done.1
  196.4 0.0 copy-done.10
  196.4 0.0 copy-done.11
  196.4 27.1 %project.1 = bf16[8,2,2,32,512]{4,3,2,1,0:T(8,128)(2,1)} custom-call(s32[1]{0:T(128)} %bitcast.1.place_ref, s32[32]{0:T(128)S(1)} %copy-done.3, s32[1,5]{1,0:T(1,128)S(1)} %copy-done.4, s32[1,5]{1,0:T(1,128)S(1)} %collective-permute-done.refs_1_, s32[2,45]{1,0:T(2,128)S(1)} %copy-done.2, s32[2,45]{1,0:T(2,128)S(1)} %collective-permute-done.1.refs_3_, ...), custom_call_target="tpu_custom_call" | custom-call | flops 12079595520 | bytes 23592960 | tf_op jit(solution)/shard_map/project/pallas_call | solution.py:118
  223.5 17.7 %all-to-all-start = ((bf16[8,2,2,32,512]{4,3,2,1,0:T(8,128)(2,1)}), bf16[8,2,2,32,512]{4,3,2,1,0:T(8,128)(2,1)S(1)}, u32[]{:S(2)}, u32[]{:S(2)}) async-start(bf16[8,2,2,32,512]{4,3,2,1,0:T(8,128)(2,1)} %project.1), calls=%async_computation | async-start | bytes 2097152 | tf_op jit(solution)/shard_map/all_to_all | solution.py:201
  241.3 0.8 copy.9.order_ref
  242.1 11.9 %all-to-all-done = bf16[8,2,2,32,512]{4,3,2,1,0:T(8,128)(2,1)S(1)} async-done(((bf16[8,2,2,32,512]{4,3,2,1,0:T(8,128)(2,1)}), bf16[8,2,2,32,512]{4,3,2,1,0:T(8,128)(2,1)S(1)}, u32[]{:S(2)}, u32[]{:S(2)}) %all-to-all-start) | async-done | bytes 1048608 | tf_op jit(solution)/shard_map/all_to_all | solution.py:201
  254.0 1.0 copy-done.5
  255.0 2.5 order.1
  (12 shorter events, 0.0 us)
Async XLA Ops:
  0.6 2.3 copy-start
  3.0 9.2 %copy-start.2 = (s32[2,45]{1,0:T(2,128)S(1)}, s32[2,45]{1,0:T(2,128)}, u32[]{:S(2)}) copy-start(s32[2,45]{1,0:T(2,128)} %refs_2_.1) | copy-start | bytes 1084
  3.0 9.9 %copy-start.4 = (s32[1,5]{1,0:T(1,128)S(1)}, s32[1,5]{1,0:T(1,128)}, u32[]{:S(2)}) copy-start(s32[1,5]{1,0:T(1,128)} %refs_0_.1) | copy-start | bytes 64
  3.0 11.0 %copy-start.7 = (bf16[256,5760]{1,0:T(8,128)(2,1)S(1)}, bf16[256,5760]{1,0:T(8,128)(2,1)}, u32[]{:S(2)}) copy-start(bf16[256,5760]{1,0:T(8,128)(2,1)} %refs_4_.1) | copy-start | bytes 8847364
  3.0 11.2 %copy-start.8 = (bf16[256,5760]{1,0:T(8,128)(2,1)S(1)}, bf16[256,5760]{1,0:T(8,128)(2,1)}, u32[]{:S(2)}) copy-start(bf16[256,5760]{1,0:T(8,128)(2,1)} %refs_6_.1) | copy-start | bytes 8847364
  3.0 193.4 %copy-start.3 = (s32[32]{0:T(128)S(1)}, s32[32]{0:T(128)}, u32[]{:S(2)}) copy-start(s32[32]{0:T(128)} %owner_ref.1) | copy-start | bytes 388
  5.2 191.1 %copy-start.1 = (s16[1168,512]{1,0:T(8,128)(2,1)}, s16[1168,512]{1,0:T(8,128)(2,1)S(1)}, u32[]{:S(2)}) copy-start(s16[1168,512]{1,0:T(8,128)(2,1)S(1)} %get-tuple-element.4.refs_12_) | copy-start | bytes 3588100
  5.2 9.2 %collective-permute-start.5 = (s16[1168,512]{1,0:T(8,128)(2,1)S(1)}, s16[1168,512]{1,0:T(8,128)(2,1)S(1)}, u32[]{:S(2)}, u32[]{:S(2)}) collective-permute-start(s16[1168,512]{1,0:T(8,128)(2,1)S(1)} %get-tuple-element.5), channel_id=1, source_target_pairs={{0,1},{1,0},{2,3},{3,2},{4,5},{5,4},{6,7},{7,6},{8,9},{9,8},{10,11... | collective-permute-start | bytes 3588104 | tf_op jit(solution)/shard_map/ppermute | solution.py:184
  6.0 53.5 %collective-permute-start.11 = (s16[1168,512]{1,0:T(8,128)(2,1)S(1)}, s16[1168,512]{1,0:T(8,128)(2,1)S(1)}, u32[]{:S(2)}, u32[]{:S(2)}) collective-permute-start(s16[1168,512]{1,0:T(8,128)(2,1)S(1)} %get-tuple-element.4.refs_12_), channel_id=1, source_target_pairs={{4,0},{5,1},{6,2},{7,3},{8,4},{9,5},{10,6},{11,7},{12,8},{13,9},{1... | collective-permute-start | bytes 3588104 | tf_op jit(solution)/shard_map/ppermute | solution.py:188
  8.1 79.1 %collective-permute-start.4 = (s16[1168,512]{1,0:T(8,128)(2,1)S(1)}, s16[1168,512]{1,0:T(8,128)(2,1)S(1)}, u32[]{:S(2)}, u32[]{:S(2)}) collective-permute-start(s16[1168,512]{1,0:T(8,128)(2,1)S(1)} %get-tuple-element.4.refs_12_), channel_id=1, source_target_pairs={{0,4},{1,5},{2,6},{3,7},{4,8},{5,9},{6,10},{7,11},{8,12},{9,13},{1... | collective-permute-start | bytes 3588104 | tf_op jit(solution)/shard_map/ppermute | solution.py:188
  12.2 2.0 collective-permute-start.1
  12.8 1.1 collective-permute-start
  14.0 180.8 %collective-permute-start.2 = (bf16[256,5760]{1,0:T(8,128)(2,1)S(1)}, bf16[256,5760]{1,0:T(8,128)(2,1)S(1)}, u32[]{:S(2)}, u32[]{:S(2)}) collective-permute-start(bf16[256,5760]{1,0:T(8,128)(2,1)S(1)} %copy-done.7), channel_id=1, source_target_pairs={{0,1},{1,0},{2,3},{3,2},{4,5},{5,4},{6,7},{7,6},{8,9},{9,8},{10,11... | collective-permute-start | bytes 8847368 | tf_op jit(solution)/shard_map/ppermute | solution.py:184
  14.2 182.2 %collective-permute-start.3 = (bf16[256,5760]{1,0:T(8,128)(2,1)S(1)}, bf16[256,5760]{1,0:T(8,128)(2,1)}, u32[]{:S(2)}, u32[]{:S(2)}) collective-permute-start(bf16[256,5760]{1,0:T(8,128)(2,1)S(1)} %copy-done.8), channel_id=1, source_target_pairs={{0,1},{1,0},{2,3},{3,2},{4,5},{5,4},{6,7},{7,6},{8,9},{9,8},{10,11... | collective-permute-start | bytes 8847368 | tf_op jit(solution)/shard_map/ppermute | solution.py:184
  14.5 181.9 %copy-start.10 = (s16[1168,512]{1,0:T(8,128)(2,1)}, s16[1168,512]{1,0:T(8,128)(2,1)S(1)}, u32[]{:S(2)}) copy-start(s16[1168,512]{1,0:T(8,128)(2,1)S(1)} %collective-permute-done.5.refs_13_) | copy-start | bytes 3588100
  14.5 76.0 %collective-permute-start.7 = (s16[1168,512]{1,0:T(8,128)(2,1)S(1)}, s16[1168,512]{1,0:T(8,128)(2,1)S(1)}, u32[]{:S(2)}, u32[]{:S(2)}) collective-permute-start(s16[1168,512]{1,0:T(8,128)(2,1)S(1)} %get-tuple-element.4.refs_12_), channel_id=1, source_target_pairs={{0,2},{1,3},{2,4},{3,5},{4,6},{5,7},{6,8},{7,9},{8,10},{9,11},{10,... | collective-permute-start | bytes 3588104 | tf_op jit(solution)/shard_map/ppermute | solution.py:188
  59.4 136.9 %copy-start.11 = (s16[1168,512]{1,0:T(8,128)(2,1)}, s16[1168,512]{1,0:T(8,128)(2,1)S(1)}, u32[]{:S(2)}) copy-start(s16[1168,512]{1,0:T(8,128)(2,1)S(1)} %collective-permute-done.11.refs_16_) | copy-start | bytes 3588100
  59.4 72.7 %collective-permute-start.9 = (s16[1168,512]{1,0:T(8,128)(2,1)S(1)}, s16[1168,512]{1,0:T(8,128)(2,1)S(1)}, u32[]{:S(2)}, u32[]{:S(2)}) collective-permute-start(s16[1168,512]{1,0:T(8,128)(2,1)S(1)} %get-tuple-element.4.refs_12_), channel_id=1, source_target_pairs={{2,0},{3,1},{4,2},{5,3},{6,4},{7,5},{8,6},{9,7},{10,8},{11,9},{12,... | collective-permute-start | bytes 3588104 | tf_op jit(solution)/shard_map/ppermute | solution.py:188
  87.2 80.2 %collective-permute-start.10 = (s16[1168,512]{1,0:T(8,128)(2,1)S(1)}, s16[1168,512]{1,0:T(8,128)(2,1)}, u32[]{:S(2)}, u32[]{:S(2)}) collective-permute-start(s16[1168,512]{1,0:T(8,128)(2,1)S(1)} %collective-permute-done.5.refs_13_), channel_id=1, source_target_pairs={{2,0},{3,1},{4,2},{5,3},{6,4},{7,5},{8,6},{9,7},{10,8},{11,9},{12,... | collective-permute-start | bytes 3588104 | tf_op jit(solution)/shard_map/ppermute | solution.py:188
  90.5 99.4 %collective-permute-start.12 = (s16[1168,512]{1,0:T(8,128)(2,1)S(1)}, s16[1168,512]{1,0:T(8,128)(2,1)S(1)}, u32[]{:S(2)}, u32[]{:S(2)}) collective-permute-start(s16[1168,512]{1,0:T(8,128)(2,1)S(1)} %collective-permute-done.5.refs_13_), channel_id=1, source_target_pairs={{4,0},{5,1},{6,2},{7,3},{8,4},{9,5},{10,6},{11,7},{12,8},{13,9},{1... | collective-permute-start | bytes 3588104 | tf_op jit(solution)/shard_map/ppermute | solution.py:188
  132.1 62.6 %copy-start.12 = (s16[1168,512]{1,0:T(8,128)(2,1)}, s16[1168,512]{1,0:T(8,128)(2,1)S(1)}, u32[]{:S(2)}) copy-start(s16[1168,512]{1,0:T(8,128)(2,1)S(1)} %collective-permute-done.9.refs_14_) | copy-start | bytes 3588100
  132.1 61.7 %collective-permute-start.6 = (s16[1168,512]{1,0:T(8,128)(2,1)S(1)}, s16[1168,512]{1,0:T(8,128)(2,1)S(1)}, u32[]{:S(2)}, u32[]{:S(2)}) collective-permute-start(s16[1168,512]{1,0:T(8,128)(2,1)S(1)} %collective-permute-done.5.refs_13_), channel_id=1, source_target_pairs={{0,4},{1,5},{2,6},{3,7},{4,8},{5,9},{6,10},{7,11},{8,12},{9,13},{1... | collective-permute-start | bytes 3588104 | tf_op jit(solution)/shard_map/ppermute | solution.py:188
  167.4 27.3 %collective-permute-start.8 = (s16[1168,512]{1,0:T(8,128)(2,1)S(1)}, s16[1168,512]{1,0:T(8,128)(2,1)S(1)}, u32[]{:S(2)}, u32[]{:S(2)}) collective-permute-start(s16[1168,512]{1,0:T(8,128)(2,1)S(1)} %collective-permute-done.5.refs_13_), channel_id=1, source_target_pairs={{0,2},{1,3},{2,4},{3,5},{4,6},{5,7},{6,8},{7,9},{8,10},{9,11},{10,... | collective-permute-start | bytes 3588104 | tf_op jit(solution)/shard_map/ppermute | solution.py:188
  189.9 4.9 %copy-start.13 = (s16[1168,512]{1,0:T(8,128)(2,1)}, s16[1168,512]{1,0:T(8,128)(2,1)S(1)}, u32[]{:S(2)}) copy-start(s16[1168,512]{1,0:T(8,128)(2,1)S(1)} %collective-permute-done.12.refs_17_) | copy-start | bytes 3588100
  194.8 1.6 copy-start.9
  223.5 17.7 %copy-start.6 = (s32[256]{0:T(256)S(1)}, s32[256]{0:T(256)}, u32[]{:S(2)}) copy-start(s32[256]{0:T(256)} %param.13) | copy-start | bytes 3076
  223.5 30.5 %all-to-all-start = ((bf16[8,2,2,32,512]{4,3,2,1,0:T(8,128)(2,1)}), bf16[8,2,2,32,512]{4,3,2,1,0:T(8,128)(2,1)S(1)}, u32[]{:S(2)}, u32[]{:S(2)}) async-start(bf16[8,2,2,32,512]{4,3,2,1,0:T(8,128)(2,1)} %project.1), calls=%async_computation | async-start | bytes 2097152 | tf_op jit(solution)/shard_map/all_to_all | solution.py:201
  254.0 1.0 copy-start.5

commit v2 on v0

v2 whole, which is shorter than its diff:
```python
import functools

import jax
import jax.numpy as jnp
from jax import lax
from jax.experimental import pallas as pl
from jax.experimental.pallas import tpu as pltpu
from jax.sharding import PartitionSpec as P

TILE = 128
REACH = 4
AXES = ("sub", "blk")
STEPS = 64.0
TOP = 32760.0
CODE_ROWS = 16
PACK_LIMIT = 60
VMEM = pl.BlockSpec(memory_space=pltpu.VMEM)


def quantize(x_ref, q_ref):
    tiles = x_ref.shape[0] // TILE
    codes = []
    for t in range(tiles):
        rows = pl.ds(t * TILE, TILE)
        x = x_ref[rows, :]
        top = jnp.maximum(jnp.max(jnp.abs(x), axis=0, keepdims=True), 2.0**-120)
        code = jnp.ceil(jnp.log2(top) * STEPS + 0.5)
        q = x * (jnp.exp2(code * (-1.0 / STEPS)) * TOP)
        q = jnp.minimum(jnp.maximum(q, -32767.0), 32767.0)
        q_ref[rows, :] = jnp.round(q).astype(jnp.int32).astype(jnp.int16)
        codes.append(code.astype(jnp.int32))
    codes.append(jnp.zeros((CODE_ROWS - tiles, x_ref.shape[1]), jnp.int32))
    q_ref[pl.ds(tiles * TILE, CODE_ROWS), :] = jnp.concatenate(codes, axis=0).astype(jnp.int16)


def pack_kernel(place_ref, *refs):
    for x_ref, q_ref in zip(refs[: len(refs) // 2], refs[len(refs) // 2 :], strict=True):
        quantize(x_ref, q_ref)


def pack(place, mode_blocks):
    rows, modes = mode_blocks.shape
    width = modes // 4
    steps = width // TILE
    out = jax.ShapeDtypeStruct((rows + CODE_ROWS, width), jnp.int16)

    def columns(piece):
        return lambda i, place: (0, (((place[0] + piece // 2) % 2) * 2 + piece % 2) * steps + i)

    return pl.pallas_call(
        pack_kernel,
        grid_spec=pltpu.PrefetchScalarGridSpec(
            num_scalar_prefetch=1,
            grid=(steps,),
            in_specs=[pl.BlockSpec((rows, TILE), columns(piece)) for piece in range(4)],
            out_specs=[pl.BlockSpec((rows + CODE_ROWS, TILE), lambda i, place: (0, i))] * 4,
        ),
        out_shape=(out,) * 4,
        compiler_params=pltpu.CompilerParams(vmem_limit_bytes=PACK_LIMIT << 20),
        cost_estimate=pl.CostEstimate(flops=rows * modes * 16, bytes_accessed=rows * modes * 6, transcendentals=0),
        name="pack",
    )(place, *[mode_blocks] * 4)


def slot_kernel(away, other, first, last, place_ref, owner_ref, own_ids, other_ids, own_mask, other_mask, *refs):
    own_rows, other_rows = refs[0:2], refs[2:4]
    a_ref, b_ref = refs[4:6]
    total = refs[6] if last or first else refs[7]
    high, low, left, landed = refs[-4:]
    outs = refs[7:-4]
    depth = high.shape[0]
    width = a_ref.shape[1]
    tiles = depth // TILE
    reads = own_ids.shape[1]
    index = place_ref[0]
    core = index % 2
    slot = index - core + 2 * away(index) + (core + other) % 2
    found, copies, at = [], [], []
    for who, (ids, rows) in enumerate(((own_ids, own_rows), (other_ids, other_rows))):
        read = jnp.int32(-1)
        for r in range(reads):
            read = jnp.where(owner_ref[ids[0, r]] == slot, jnp.int32(r), read)
        at.append(jnp.maximum(read, 0))
        span = pl.ds(pl.multiple_of(at[who] * depth, TILE), depth)
        height = rows[0].shape[0]
        copies.append(
            [
                pltpu.make_async_copy(x.at[:, span], left.at[who, pl.ds(kind * height, height)], landed.at[who, kind])
                for kind, x in enumerate(rows)
            ]
        )
        found.append(read >= 0)

        @pl.when(found[who])
        def _(who=who):
            for copy in copies[who]:
                copy.start()

    if first:
        total[...] = jnp.zeros_like(total)

    @pl.when(found[0] | found[1])
    def _():
        for piece, q_ref in enumerate((a_ref, b_ref)):
            columns = pl.ds(piece * width, width)
            codes = q_ref[pl.ds(depth, CODE_ROWS), :].astype(jnp.int32).astype(jnp.float32)
            scale = jnp.exp2(codes * (1.0 / STEPS)) * (1.0 / TOP)
            for t in range(tiles):
                span = pl.ds(t * TILE, TILE)
                value = q_ref[span, :].astype(jnp.int32).astype(jnp.float32) * scale[t : t + 1, :]
                top = value.astype(jnp.bfloat16)
                high[span, columns] = top
                low[span, columns] = (value - top.astype(jnp.float32)).astype(jnp.bfloat16)

    for who, mask in enumerate((own_mask, other_mask)):

        @pl.when(found[who])
        def _(who=who, mask=mask):
            for copy in copies[who]:
                copy.wait()
            row_tiles = mask.shape[0]
            for r in range(row_tiles):
                for t in range(tiles):

                    @pl.when(mask[r, at[who] * tiles + t] == 0)
                    def _(r=r, t=t):
                        for kind in range(2):
                            left[who, pl.ds((kind * row_tiles + r) * TILE, TILE), pl.ds(t * TILE, TILE)] = jnp.zeros(
                                (TILE, TILE), left.dtype
                            )

            step = 2 * TILE

            @pl.loop(0, high.shape[1] // step)
            def _(i):
                span = pl.ds(pl.multiple_of(i * step, step), step)
                total[who, :, span] += jnp.dot(left[who], high[:, span], preferred_element_type=jnp.float32) + jnp.dot(
                    left[who], low[:, span], preferred_element_type=jnp.float32
                )

    if last:
        _, kinds, part, _ = outs[0].shape
        for by, out_ref in enumerate(outs):
            for kind in range(kinds):
                to = index % len(outs) ^ by
                span = pl.ds(pl.multiple_of((kind * len(outs) + to) * part, part), part)
                for who in range(2):
                    out_ref[who, kind] = total[who, span, :].astype(jnp.bfloat16)
    else:
        refs[-5][...] = jnp.zeros_like(refs[-5])


def add_slot(place, away, other, owner_slot, ids, masks, rows, pieces, total, devices=None):
    height = rows[0][0].shape[0]
    depth = rows[0][0].shape[1] // ids[0].shape[1]
    width = 2 * pieces[0].shape[1]
    first, last = total is None, devices is not None
    if last:
        out_shape = [jax.ShapeDtypeStruct((2, 2, height // devices, width), jnp.bfloat16)] * devices
    else:
        out_shape = [jax.ShapeDtypeStruct((2, 2 * height, width), jnp.float32), jax.ShapeDtypeStruct((8, TILE), jnp.int32)]
    hbm = pl.BlockSpec(memory_space=pl.ANY)
    return pl.pallas_call(
        functools.partial(slot_kernel, away, other, first, last),
        grid_spec=pltpu.PrefetchScalarGridSpec(
            num_scalar_prefetch=6,
            grid=(),
            in_specs=[hbm] * 4 + [VMEM] * (2 if first else 3),
            out_specs=[VMEM] * len(out_shape),
            scratch_shapes=[
                pltpu.VMEM((depth, width), jnp.bfloat16),
                pltpu.VMEM((depth, width), jnp.bfloat16),
                pltpu.VMEM((2, 2 * height, depth), jnp.bfloat16),
                pltpu.SemaphoreType.DMA((2, 2)),
            ],
        ),
        out_shape=out_shape,
        input_output_aliases={} if first or last else {12: 0},
        compiler_params=pltpu.CompilerParams(vmem_limit_bytes=12 << 20),
        cost_estimate=pl.CostEstimate(flops=16 * height * depth * width, bytes_accessed=depth * width * 2, transcendentals=0),
        name="slot",
    )(place, owner_slot, *ids, *masks, *rows[0], *rows[1], *pieces, *(() if first else (total,)))


def order_kernel(place_ref, order_ref, *refs):
    outs, parts = refs[-2:], refs[:-2]
    _, _, part, width = parts[0].shape
    here = place_ref[0] % len(parts)
    count = order_ref.shape[0]
    at = lax.broadcasted_iota(jnp.int32, (count, count), 1)
    slot, who, row = at // (2 * part), at // part % 2, at % part
    for odd in range(2):
        core = (here + odd) % 2
        sender = here ^ (slot * 2 + odd)
        block = sender // 2 * 2 + (who + core) % 2
        pick = (order_ref[...] == block * part + row).astype(jnp.bfloat16)
        columns = pl.ds(pl.multiple_of(core * width, TILE), width)
        for kind, ref in enumerate(outs):
            if part % 16:
                rows = [x[who, kind].astype(jnp.float32) for x in parts[odd::2] for who in range(2)]
            else:
                rows = [x[who, kind] for x in parts[odd::2] for who in range(2)]
            rows = jnp.concatenate(rows, axis=0).astype(jnp.bfloat16)
            ref[:, columns] = jnp.dot(pick, rows, preferred_element_type=jnp.float32).astype(jnp.bfloat16)


def order_rows(place, tree_order, parts):
    count, width = tree_order.shape[0], parts[0].shape[-1]
    out = jax.ShapeDtypeStruct((count, 2 * width), jnp.bfloat16)
    return pl.pallas_call(
        order_kernel,
        grid_spec=pltpu.PrefetchScalarGridSpec(
            num_scalar_prefetch=1, grid=(), in_specs=[VMEM] * (1 + len(parts)), out_specs=[VMEM] * 2
        ),
        out_shape=(out, out),
        compiler_params=pltpu.CompilerParams(vmem_limit_bytes=12 << 20),
        name="order",
    )(place, tree_order[:, None], *parts)


def after(x, *landed):
    return lax.optimization_barrier((x, *landed))[0] if landed else x


def permute(x, count, target):
    pairs = [(i, target(i)) for i in range(count)]
    return lax.ppermute(x, AXES, [(i, t) for i, t in pairs if t is not None and 0 <= t < count])


def direct(own, partners, count, index, add):
    slots = [(lambda index: 0, own)]
    for chips in range(-(REACH // 2), REACH // 2 + 1):
        if chips:
            pieces = {k: permute(x, count, lambda i, by=-2 * chips: i + by) for k, x in own.items()}
            slots.append((lambda index, chips=chips: chips, pieces))
    for n, (away, pieces) in enumerate(slots):
        for other in range(2):
            parts = add(away, other, pieces, last=n == len(slots) - 1 and other == 1)
    return parts


def routed(own, partners, count, index, add):
    x, y, z, half, d = {}, {}, {}, {}, {}

    def beside(k, *landed):
        x[k] = permute(after(own[k], *landed), count, lambda i: i ^ 2)
        y[k] = permute(after(own[k], *landed), count, lambda i: i ^ 4)

    def beyond(k, *landed):
        z[k] = permute(after(y[k], *landed), count, lambda i: i - 8 if i & 4 else i + 8)
        if k[1] == 1:
            target = lambda i: None if (i >> 2 ^ i >> 1) & 1 == 0 else (i + 8 if i & 4 else i - 8)
            half[k] = permute(after(x[k], *landed), count, target)

    def around(k, *landed):
        outer = (index // 4 % 2) == (index // 2 % 2)
        if k[1] == 0:
            d[k] = permute(after(jnp.where(outer, y[k], z[k]), *landed), count, lambda i: i ^ 2)
        else:
            d[k] = permute(after(jnp.where(outer, x[k], half[k]), *landed), count, lambda i: i ^ 4)

    away = {
        "own": lambda index: 0,
        "x": lambda index: 1 - 2 * (index // 2 % 2),
        "y": lambda index: 2 - 4 * (index // 4 % 2),
        "z": lambda index: 4 * (index // 4 % 2) - 2,
        "d": lambda index: 2 * (index // 2 % 2) - 1,
    }
    oa, ob, pa, pb = (0, 0), (0, 1), (1, 0), (1, 1)
    beside(oa)
    beside(ob)
    beside(pa, x[oa], y[oa], *partners)
    beyond(oa)
    add(away["own"], 0, own, x[oa], y[oa])
    done = add(away["own"], 1, own)
    beside(pb, x[ob], y[ob], done)
    beyond(ob)
    add(away["x"], 0, x)
    done = add(away["y"], 0, y)
    around(oa)
    beyond(pa, done)
    around(ob)
    done = add(away["z"], 0, z)
    beyond(pb, done)
    add(away["x"], 1, x)
    done = add(away["y"], 1, y)
    around(pa, done)
    around(pb, done)
    add(away["z"], 1, z)
    add(away["d"], 0, d)
    return add(away["d"], 1, d, last=True)


def per_device(mode_blocks, stiffness, mass_tiles, reader_ids, owner_slot, tile_mask, tree_order):
    devices = lax.axis_size("blk")
    count = lax.axis_size("sub") * devices
    index = lax.axis_index(AXES).astype(jnp.int32)
    place = index.reshape(1)

    def partner(x):
        return permute(x, count, lambda i: i ^ 1)

    packed = pack(place, mode_blocks)
    keys = ((0, 0), (0, 1), (1, 0), (1, 1))
    own = dict(zip(keys, (*packed[:2], *(partner(x) for x in packed[2:])), strict=True))
    partners = [partner(x) for x in (stiffness, mass_tiles, reader_ids, tile_mask)]
    rows = ((stiffness, mass_tiles), tuple(partners[:2]))
    ids, masks = (reader_ids, partners[2]), (tile_mask, partners[3])
    total = [None]

    def add(away, other, pieces, *landed, last=False):
        pair = (pieces[other, 0], pieces[other, 1])
        out = add_slot(after(place, *landed), away, other, owner_slot, ids, masks, rows, pair, total[0], devices if last else None)
        if last:
            return out
        total[0], token = out
        return token

    parts = (routed if devices == 8 else direct)(own, partners, count, index, add)
    parts = [permute(x, count, lambda i, by=by: i ^ by) if by else x for by, x in enumerate(parts)]
    return order_rows(place, tree_order, parts)


def solution(mesh):
    spec = P(AXES, None)
    return jax.shard_map(
        per_device,
        mesh=mesh,
        in_specs=(spec, spec, spec, spec, P(), spec, P(AXES)),
        out_specs=(spec, spec),
        check_vma=False,
    )
```

time: 738 us -> 158 us (0.21)
  the two profiles are of different devices: /device:TPU:15 before, /device:TPU:17 now
where the time goes in v2:
time: 158 us
  starting transfers between devices  57.4 us (36%)
  waiting for transfers between devices  48.1 us (30%)
  Pallas kernels  46 us (29%)
  local copies, waits for them, and re-layouts  3.51 us (2%)
  other arithmetic  1.75 us (1%)
    ppermute x31, starting transfers between devices, permute(): lax.ppermute(x, AXES, [(i, t) for i, t in pairs if t is not None and 0 <=...  57.4 us
    ppermute x31, waiting for transfers between devices, permute(): lax.ppermute(x, AXES, [(i, t) for i, t in pairs if t is not None and 0 <=...  48.1 us
    pallas_call x10, Pallas kernels, add_slot(): pl.pallas_call(functools.partial(slot_kernel, away, other, first, last),...  40.7 us
    pallas_call x1, Pallas kernels, pack(): pl.pallas_call(pack_kernel, grid_spec=pltpu.PrefetchScalarGridSpec(num_sc...  3.94 us
    unnamed x28, local copies, waits for them, and re-layouts  3.38 us
  transfers between devices with their start and end apart: 31, of which 6 were waited for; matrix products, arithmetic and copies ran while one was open for 1% of the time, Pallas kernels for 26%

profile of v2, /device:TPU:17, one launch (start us, length us, event | category | flops | bytes accessed | tf_op | source)
XLA Modules:
  0.0 157.7 jit_solution(6365768875920732597)
XLA Ops:
  0.6 0.7 collective-permute-start.2
  1.5 3.9 %pack.1 = (s16[1168,256]{1,0:T(8,128)(2,1)}, s16[1168,256]{1,0:T(8,128)(2,1)}, s16[1168,256]{1,0:T(8,128)(2,1)}, s16[1168,256]{1,0:T(8,128)(2,1)}) custom-call(s32[1]{0:T(128)} %bitcast.place_ref, f32[1152,1024]{1,0:T(8,128)} %refs_3_.1, f32[1152,1024]{1,0:T(8,128)} %refs_3_.1, f32[1152,1024]{1,0:T(8,128)} %refs_3_.1, f32[1152,1024]{1,0:T(8,128)} %refs_3_.1), custom_call_target="tpu_custom_call" | custom-call | flops 18874368 | bytes 7077888 | tf_op jit(solution)/shard_map/pack/pallas_call | solution.py:50
  5.4 1.2 collective-permute-start.6
  6.6 1.2 collective-permute-start.5
  7.8 1.0 collective-permute-start.9
  8.8 11.5 %collective-permute-done.6.refs_4_ = s16[1168,256]{1,0:T(8,128)(2,1)} collective-permute-done((s16[1168,256]{1,0:T(8,128)(2,1)}, s16[1168,256]{1,0:T(8,128)(2,1)}, u32[]{:S(2)}, u32[]{:S(2)}) %collective-permute-start.6) | collective-permute-done | bytes 598048 | tf_op jit(solution)/shard_map/ppermute | solution.py:227
  20.4 1.2 collective-permute-start.10
  21.6 0.9 copy-done.5
  22.4 1.2 collective-permute-start.11
  23.7 3.2 %collective-permute-start.15 = (s16[1168,256]{1,0:T(8,128)(2,1)}, s16[1168,256]{1,0:T(8,128)(2,1)}, u32[]{:S(2)}, u32[]{:S(2)}) collective-permute-start(s16[1168,256]{1,0:T(8,128)(2,1)} %collective-permute-done.6.refs_4_), channel_id=1, source_target_pairs={{0,8},{1,9},{2,10},{3,11},{8,16},{9,17},{10,18},{11,19},{12,4},{13... | collective-permute-start | bytes 1794056 | tf_op jit(solution)/shard_map/ppermute | solution.py:227
  26.9 7.5 %collective-permute-done.10.refs_5_ = s16[1168,256]{1,0:T(8,128)(2,1)S(1)} collective-permute-done((s16[1168,256]{1,0:T(8,128)(2,1)}, s16[1168,256]{1,0:T(8,128)(2,1)S(1)}, u32[]{:S(2)}, u32[]{:S(2)}) %collective-permute-start.10) | collective-permute-done | bytes 598048 | tf_op jit(solution)/shard_map/ppermute | solution.py:227
  34.4 2.1 %collective-permute-start.4 = (s16[1168,256]{1,0:T(8,128)(2,1)}, s16[1168,256]{1,0:T(8,128)(2,1)}, u32[]{:S(2)}, u32[]{:S(2)}) collective-permute-start(s16[1168,256]{1,0:T(8,128)(2,1)} %get-tuple-element.32), channel_id=1, source_target_pairs={{0,1},{1,0},{2,3},{3,2},{4,5},{5,4},{6,7},{7,6},{8,9},{9,8},{10,11... | collective-permute-start | bytes 1794056 | tf_op jit(solution)/shard_map/ppermute | solution.py:227
  36.5 2.2 %collective-permute-start.1 = (s32[2,45]{1,0:T(2,128)S(1)}, s32[2,45]{1,0:T(2,128)S(1)}, u32[]{:S(2)}, u32[]{:S(2)}) collective-permute-start(s32[2,45]{1,0:T(2,128)S(1)} %copy-done.9), channel_id=1, source_target_pairs={{0,1},{1,0},{2,3},{3,2},{4,5},{5,4},{6,7},{7,6},{8,9},{9,8},{10,11... | collective-permute-start | bytes 1088 | tf_op jit(solution)/shard_map/ppermute | solution.py:227
  38.7 0.4 collective-permute-done.15.refs_4_
  39.0 2.8 %collective-permute-start = (s32[1,5]{1,0:T(1,128)}, s32[1,5]{1,0:T(1,128)S(1)}, u32[]{:S(2)}, u32[]{:S(2)}) collective-permute-start(s32[1,5]{1,0:T(1,128)} %own_ids.19), channel_id=1, source_target_pairs={{0,1},{1,0},{2,3},{3,2},{4,5},{5,4},{6,7},{7,6},{8,9},{9,8},{10,11... | collective-permute-start | bytes 68 | tf_op jit(solution)/shard_map/ppermute | solution.py:227
  41.8 1.3 broadcast_select_fusion.1
  43.4 0.9 collective-permute-start.14
  44.3 2.4 %collective-permute-start.16 = (s16[1168,256]{1,0:T(8,128)(2,1)}, s16[1168,256]{1,0:T(8,128)(2,1)S(1)}, u32[]{:S(2)}, u32[]{:S(2)}) collective-permute-start(s16[1168,256]{1,0:T(8,128)(2,1)} %collective-permute-done.11.refs_5_), channel_id=1, source_target_pairs={{0,8},{1,9},{2,10},{3,11},{8,16},{9,17},{10,18},{11,19},{12,4},{13... | collective-permute-start | bytes 1794056 | tf_op jit(solution)/shard_map/ppermute | solution.py:227
  46.7 0.7 collective-permute-start.21
  47.4 2.8 %collective-permute-start.13 = (s16[1168,256]{1,0:T(8,128)(2,1)}, s16[1168,256]{1,0:T(8,128)(2,1)S(1)}, u32[]{:S(2)}, u32[]{:S(2)}) collective-permute-start(s16[1168,256]{1,0:T(8,128)(2,1)} %collective-permute-done.4.refs_4_), channel_id=1, source_target_pairs={{0,2},{1,3},{2,0},{3,1},{4,6},{5,7},{6,4},{7,5},{8,10},{9,11},{10,... | collective-permute-start | bytes 1794056 | tf_op jit(solution)/shard_map/ppermute | solution.py:227
  50.2 1.8 %copy-done.1 = bf16[256,5760]{1,0:T(8,128)(2,1)S(1)} copy-done((bf16[256,5760]{1,0:T(8,128)(2,1)S(1)}, bf16[256,5760]{1,0:T(8,128)(2,1)}, u32[]{:S(2)}) %copy-start.1) | copy-done | bytes 2949144
  52.1 0.7 copy-done.11
  52.7 5.6 %slot.10 = (f32[2,512,512]{2,1,0:T(8,128)S(1)}, s32[8,128]{1,0:T(8,128)}) custom-call(s32[1]{0:T(128)} %bitcast.place_ref, s32[32]{0:T(128)S(1)} %copy-done.10, s32[1,5]{1,0:T(1,128)S(1)} %copy-done.11, s32[1,5]{1,0:T(1,128)S(1)} %collective-permute-done.other_ids, s32[2,45]{1,0:T(2,128)S(1)} %copy-done.9, s32[2,45]{1,0:T(2,128)S(1)} %collective-permute-done.1.other_mask, ...), custom_call_target="tpu_custom_call" | custom-call | flops 2415919104 | bytes 1179648 | tf_op jit(solution)/shard_map/slot/pallas_call | solution.py:163
  58.4 5.4 %slot.11 = (f32[2,512,512]{2,1,0:T(8,128)S(1)}, s32[8,128]{1,0:T(8,128)}) custom-call(s32[1]{0:T(128)} %bitcast.place_ref, s32[32]{0:T(128)S(1)} %copy-done.10, s32[1,5]{1,0:T(1,128)S(1)} %copy-done.11, s32[1,5]{1,0:T(1,128)S(1)} %collective-permute-done.other_ids, s32[2,45]{1,0:T(2,128)S(1)} %copy-done.9, ...), custom_call_target="tpu_custom_call", output_to_operand_aliasing={{0}: (12, {})} | custom-call | flops 2415919104 | bytes 1179648 | tf_op jit(solution)/shard_map/slot/pallas_call | solution.py:163
  63.8 3.7 %slot.12 = (f32[2,512,512]{2,1,0:T(8,128)S(1)}, s32[8,128]{1,0:T(8,128)}) custom-call(s32[1]{0:T(128)} %bitcast.place_ref, s32[32]{0:T(128)S(1)} %copy-done.10, s32[1,5]{1,0:T(1,128)S(1)} %copy-done.11, s32[1,5]{1,0:T(1,128)S(1)} %collective-permute-done.other_ids, s32[2,45]{1,0:T(2,128)S(1)} %copy-done.9, ...), custom_call_target="tpu_custom_call", output_to_operand_aliasing={{0}: (12, {})} | custom-call | flops 2415919104 | bytes 1179648 | tf_op jit(solution)/shard_map/slot/pallas_call | solution.py:163
  67.5 2.5 %slot.13 = (f32[2,512,512]{2,1,0:T(8,128)S(1)}, s32[8,128]{1,0:T(8,128)}) custom-call(s32[1]{0:T(128)} %bitcast.place_ref, s32[32]{0:T(128)S(1)} %copy-done.10, s32[1,5]{1,0:T(1,128)S(1)} %copy-done.11, s32[1,5]{1,0:T(1,128)S(1)} %collective-permute-done.other_ids, s32[2,45]{1,0:T(2,128)S(1)} %copy-done.9, ...), custom_call_target="tpu_custom_call", output_to_operand_aliasing={{0}: (12, {})} | custom-call | flops 2415919104 | bytes 1179648 | tf_op jit(solution)/shard_map/slot/pallas_call | solution.py:163
  70.0 1.5 collective-permute-start.7
  71.4 2.6 %slot.14 = (f32[2,512,512]{2,1,0:T(8,128)S(1)}, s32[8,128]{1,0:T(8,128)}) custom-call(s32[1]{0:T(128)} %bitcast.place_ref, s32[32]{0:T(128)S(1)} %copy-done.10, s32[1,5]{1,0:T(1,128)S(1)} %copy-done.11, s32[1,5]{1,0:T(1,128)S(1)} %collective-permute-done.other_ids, s32[2,45]{1,0:T(2,128)S(1)} %copy-done.9, ...), custom_call_target="tpu_custom_call", output_to_operand_aliasing={{0}: (12, {})} | custom-call | flops 2415919104 | bytes 1179648 | tf_op jit(solution)/shard_map/slot/pallas_call | solution.py:163
  74.0 5.4 %collective-permute-start.20 = (s16[1168,256]{1,0:T(8,128)(2,1)S(1)}, s16[1168,256]{1,0:T(8,128)(2,1)S(1)}, u32[]{:S(2)}, u32[]{:S(2)}) collective-permute-start(s16[1168,256]{1,0:T(8,128)(2,1)S(1)} %broadcast_select_fusion.1), channel_id=1, source_target_pairs={{0,2},{1,3},{2,0},{3,1},{4,6},{5,7},{6,4},{7,5},{8,10},{9,11},{10,... | collective-permute-start | bytes 1794056 | tf_op jit(solution)/shard_map/ppermute | solution.py:227
  79.4 0.7 collective-permute-start.18
  80.3 3.0 %collective-permute-start.22 = (s16[1168,256]{1,0:T(8,128)(2,1)S(1)}, s16[1168,256]{1,0:T(8,128)(2,1)S(1)}, u32[]{:S(2)}, u32[]{:S(2)}) collective-permute-start(s16[1168,256]{1,0:T(8,128)(2,1)S(1)} %broadcast_select_fusion), channel_id=1, source_target_pairs={{0,4},{1,5},{2,6},{3,7},{4,0},{5,1},{6,2},{7,3},{8,12},{9,13},{10,... | collective-permute-start | bytes 1794056 | tf_op jit(solution)/shard_map/ppermute | solution.py:227
  83.3 5.2 %collective-permute-start.23 = (s16[1168,256]{1,0:T(8,128)(2,1)S(1)}, s16[1168,256]{1,0:T(8,128)(2,1)S(1)}, u32[]{:S(2)}, u32[]{:S(2)}) collective-permute-start(s16[1168,256]{1,0:T(8,128)(2,1)S(1)} %collective-permute-done.12.refs_5_), channel_id=1, source_target_pairs={{0,8},{1,9},{2,10},{3,11},{8,16},{9,17},{10,18},{11,19},{12,4},{13... | collective-permute-start | bytes 1794056 | tf_op jit(solution)/shard_map/ppermute | solution.py:227
  88.5 1.9 %collective-permute-start.8 = (s16[1168,256]{1,0:T(8,128)(2,1)S(1)}, s16[1168,256]{1,0:T(8,128)(2,1)S(1)}, u32[]{:S(2)}, u32[]{:S(2)}) collective-permute-start(s16[1168,256]{1,0:T(8,128)(2,1)S(1)} %collective-permute-done.7.refs_4_), channel_id=1, source_target_pairs={{0,8},{1,9},{2,10},{3,11},{8,16},{9,17},{10,18},{11,19},{12,4},{13... | collective-permute-start | bytes 1794056 | tf_op jit(solution)/shard_map/ppermute | solution.py:227
  90.4 5.6 %slot.15 = (f32[2,512,512]{2,1,0:T(8,128)S(1)}, s32[8,128]{1,0:T(8,128)}) custom-call(s32[1]{0:T(128)} %bitcast.place_ref, s32[32]{0:T(128)S(1)} %copy-done.10, s32[1,5]{1,0:T(1,128)S(1)} %copy-done.12, s32[1,5]{1,0:T(1,128)S(1)} %collective-permute-done.other_ids, s32[2,45]{1,0:T(2,128)S(1)} %copy-done.9, ...), custom_call_target="tpu_custom_call", output_to_operand_aliasing={{0}: (12, {})} | custom-call | flops 2415919104 | bytes 1179648 | tf_op jit(solution)/shard_map/slot/pallas_call | solution.py:163
  96.0 5.6 %slot.16 = (f32[2,512,512]{2,1,0:T(8,128)S(1)}, s32[8,128]{1,0:T(8,128)}) custom-call(s32[1]{0:T(128)} %bitcast.place_ref, s32[32]{0:T(128)S(1)} %copy-done.10, s32[1,5]{1,0:T(1,128)S(1)} %copy-done.12, s32[1,5]{1,0:T(1,128)S(1)} %collective-permute-done.other_ids, s32[2,45]{1,0:T(2,128)S(1)} %copy-done.9, ...), custom_call_target="tpu_custom_call", output_to_operand_aliasing={{0}: (12, {})} | custom-call | flops 2415919104 | bytes 1179648 | tf_op jit(solution)/shard_map/slot/pallas_call | solution.py:163
  101.8 15.5 %collective-permute-done.8.refs_4_ = s16[1168,256]{1,0:T(8,128)(2,1)S(1)} collective-permute-done((s16[1168,256]{1,0:T(8,128)(2,1)S(1)}, s16[1168,256]{1,0:T(8,128)(2,1)S(1)}, u32[]{:S(2)}, u32[]{:S(2)}) %collective-permute-start.8) | collective-permute-done | bytes 598048 | tf_op jit(solution)/shard_map/ppermute | solution.py:227
  117.5 1.3 collective-permute-start.17
  118.8 1.3 slot.17
  120.1 4.6 %slot.18 = (f32[2,512,512]{2,1,0:T(8,128)S(1)}, s32[8,128]{1,0:T(8,128)}) custom-call(s32[1]{0:T(128)} %bitcast.place_ref, s32[32]{0:T(128)S(1)} %copy-done.10, s32[1,5]{1,0:T(1,128)S(1)} %copy-done.12, s32[1,5]{1,0:T(1,128)S(1)} %collective-permute-done.other_ids, s32[2,45]{1,0:T(2,128)S(1)} %copy-done.9, ...), custom_call_target="tpu_custom_call", output_to_operand_aliasing={{0}: (12, {})} | custom-call | flops 2415919104 | bytes 1179648 | tf_op jit(solution)/shard_map/slot/pallas_call | solution.py:163
  124.7 6.8 %collective-permute-done.17.refs_4_ = s16[1168,256]{1,0:T(8,128)(2,1)S(1)} collective-permute-done((s16[1168,256]{1,0:T(8,128)(2,1)S(1)}, s16[1168,256]{1,0:T(8,128)(2,1)S(1)}, u32[]{:S(2)}, u32[]{:S(2)}) %collective-permute-start.17) | collective-permute-done | bytes 598048 | tf_op jit(solution)/shard_map/ppermute | solution.py:227
  131.5 3.9 %slot.19 = (bf16[2,2,32,512]{3,2,1,0:T(8,128)(2,1)S(1)}, bf16[2,2,32,512]{3,2,1,0:T(8,128)(2,1)S(1)}, bf16[2,2,32,512]{3,2,1,0:T(8,128)(2,1)S(1)}, bf16[2,2,32,5...) custom-call(s32[1]{0:T(128)} %bitcast.place_ref, ...), custom_call_target="tpu_custom_call" | custom-call | flops 2415919104 | bytes 1179648 | tf_op jit(solution)/shard_map/slot/pallas_call | solution.py:163
  135.4 2.1 %collective-permute-start.24 = (bf16[2,2,32,512]{3,2,1,0:T(8,128)(2,1)S(1)}, bf16[2,2,32,512]{3,2,1,0:T(8,128)(2,1)S(1)}, u32[]{:S(2)}, u32[]{:S(2)}) collective-permute-start(bf16[2,2,32,512]{3,2,1,0:T(8,128)(2,1)S(1)} %get-tuple-element.55), channel_id=1, source_target_pairs={{0,1},{1,0},{2,3},{3,2},{4,5},{5,4},{6,7},{7,6},{8,9},{9,8},{10,11... | collective-permute-start | bytes 393224 | tf_op jit(solution)/shard_map/ppermute | solution.py:227
  137.5 3.1 %collective-permute-start.25 = (bf16[2,2,32,512]{3,2,1,0:T(8,128)(2,1)S(1)}, bf16[2,2,32,512]{3,2,1,0:T(8,128)(2,1)S(1)}, u32[]{:S(2)}, u32[]{:S(2)}) collective-permute-start(bf16[2,2,32,512]{3,2,1,0:T(8,128)(2,1)S(1)} %get-tuple-element.56), channel_id=1, source_target_pairs={{0,2},{1,3},{2,0},{3,1},{4,6},{5,7},{6,4},{7,5},{8,10},{9,11},{10,... | collective-permute-start | bytes 393224 | tf_op jit(solution)/shard_map/ppermute | solution.py:227
  140.7 3.3 %collective-permute-start.27 = (bf16[2,2,32,512]{3,2,1,0:T(8,128)(2,1)}, bf16[2,2,32,512]{3,2,1,0:T(8,128)(2,1)S(1)}, u32[]{:S(2)}, u32[]{:S(2)}) collective-permute-start(bf16[2,2,32,512]{3,2,1,0:T(8,128)(2,1)} %get-tuple-element.58), channel_id=1, source_target_pairs={{0,4},{1,5},{2,6},{3,7},{4,0},{5,1},{6,2},{7,3},{8,12},{9,13},{10,... | collective-permute-start | bytes 393224 | tf_op jit(solution)/shard_map/ppermute | solution.py:227
  144.3 2.9 %collective-permute-start.29 = (bf16[2,2,32,512]{3,2,1,0:T(8,128)(2,1)S(1)}, bf16[2,2,32,512]{3,2,1,0:T(8,128)(2,1)S(1)}, u32[]{:S(2)}, u32[]{:S(2)}) collective-permute-start(bf16[2,2,32,512]{3,2,1,0:T(8,128)(2,1)S(1)} %get-tuple-element.60), channel_id=1, source_target_pairs={{0,6},{1,7},{2,4},{3,5},{4,2},{5,3},{6,0},{7,1},{8,14},{9,15},{10,... | collective-permute-start | bytes 393224 | tf_op jit(solution)/shard_map/ppermute | solution.py:227
  147.2 2.7 %collective-permute-start.30 = (bf16[2,2,32,512]{3,2,1,0:T(8,128)(2,1)S(1)}, bf16[2,2,32,512]{3,2,1,0:T(8,128)(2,1)S(1)}, u32[]{:S(2)}, u32[]{:S(2)}) collective-permute-start(bf16[2,2,32,512]{3,2,1,0:T(8,128)(2,1)S(1)} %get-tuple-element.61), channel_id=1, source_target_pairs={{0,7},{1,6},{2,5},{3,4},{4,3},{5,2},{6,1},{7,0},{8,15},{9,14},{10,... | collective-permute-start | bytes 393224 | tf_op jit(solution)/shard_map/ppermute | solution.py:227
  150.1 6.3 %collective-permute-done.28.refs_5_ = bf16[2,2,32,512]{3,2,1,0:T(8,128)(2,1)S(1)} collective-permute-done((bf16[2,2,32,512]{3,2,1,0:T(8,128)(2,1)S(1)}, bf16[2,2,32,512]{3,2,1,0:T(8,128)(2,1)S(1)}, u32[]{:S(2)}, u32[]{:S(2)}) %collective-permute-start.28) | collective-permute-done | bytes 131104 | tf_op jit(solution)/shard_map/ppermute | solution.py:227
  156.4 1.4 order.1
  (59 shorter events, 1.5 us)
Async XLA Ops:
  0.6 46.1 %collective-permute-start.2 = (bf16[256,5760]{1,0:T(8,128)(2,1)}, bf16[256,5760]{1,0:T(8,128)(2,1)}, u32[]{:S(2)}, u32[]{:S(2)}) collective-permute-start(bf16[256,5760]{1,0:T(8,128)(2,1)} %refs_0_.21), channel_id=1, source_target_pairs={{0,1},{1,0},{2,3},{3,2},{4,5},{5,4},{6,7},{7,6},{8,9},{9,8},{10,11... | collective-permute-start | bytes 8847368 | tf_op jit(solution)/shard_map/ppermute | solution.py:227
  1.4 46.0 %collective-permute-start.3 = (bf16[256,5760]{1,0:T(8,128)(2,1)}, bf16[256,5760]{1,0:T(8,128)(2,1)}, u32[]{:S(2)}, u32[]{:S(2)}) collective-permute-start(bf16[256,5760]{1,0:T(8,128)(2,1)} %refs_1_.21), channel_id=1, source_target_pairs={{0,1},{1,0},{2,3},{3,2},{4,5},{5,4},{6,7},{7,6},{8,9},{9,8},{10,11... | collective-permute-start | bytes 8847368 | tf_op jit(solution)/shard_map/ppermute | solution.py:227
  1.5 35.1 %copy-start.9 = (s32[2,45]{1,0:T(2,128)S(1)}, s32[2,45]{1,0:T(2,128)}, u32[]{:S(2)}) copy-start(s32[2,45]{1,0:T(2,128)} %own_mask.19) | copy-start | bytes 1084
  1.5 48.8 %copy-start = (bf16[256,5760]{1,0:T(8,128)(2,1)S(1)}, bf16[256,5760]{1,0:T(8,128)(2,1)}, u32[]{:S(2)}) copy-start(bf16[256,5760]{1,0:T(8,128)(2,1)} %refs_0_.21) | copy-start | bytes 8847364
  1.5 48.8 %copy-start.10 = (s32[32]{0:T(128)S(1)}, s32[32]{0:T(128)}, u32[]{:S(2)}) copy-start(s32[32]{0:T(128)} %owner_ref.19) | copy-start | bytes 388
  5.4 15.0 %collective-permute-start.6 = (s16[1168,256]{1,0:T(8,128)(2,1)}, s16[1168,256]{1,0:T(8,128)(2,1)}, u32[]{:S(2)}, u32[]{:S(2)}) collective-permute-start(s16[1168,256]{1,0:T(8,128)(2,1)} %get-tuple-element.33.refs_4_), channel_id=1, source_target_pairs={{0,4},{1,5},{2,6},{3,7},{4,0},{5,1},{6,2},{7,3},{8,12},{9,13},{10,... | collective-permute-start | bytes 1794056 | tf_op jit(solution)/shard_map/ppermute | solution.py:227
  6.6 14.9 %collective-permute-start.5 = (s16[1168,256]{1,0:T(8,128)(2,1)}, s16[1168,256]{1,0:T(8,128)(2,1)S(1)}, u32[]{:S(2)}, u32[]{:S(2)}) collective-permute-start(s16[1168,256]{1,0:T(8,128)(2,1)} %get-tuple-element.33.refs_4_), channel_id=1, source_target_pairs={{0,2},{1,3},{2,0},{3,1},{4,6},{5,7},{6,4},{7,5},{8,10},{9,11},{10,... | collective-permute-start | bytes 1794056 | tf_op jit(solution)/shard_map/ppermute | solution.py:227
  7.8 15.8 %collective-permute-start.9 = (s16[1168,256]{1,0:T(8,128)(2,1)}, s16[1168,256]{1,0:T(8,128)(2,1)S(1)}, u32[]{:S(2)}, u32[]{:S(2)}) collective-permute-start(s16[1168,256]{1,0:T(8,128)(2,1)} %get-tuple-element.35), channel_id=1, source_target_pairs={{0,1},{1,0},{2,3},{3,2},{4,5},{5,4},{6,7},{7,6},{8,9},{9,8},{10,11... | collective-permute-start | bytes 1794056 | tf_op jit(solution)/shard_map/ppermute | solution.py:227
  20.4 14.0 %collective-permute-start.10 = (s16[1168,256]{1,0:T(8,128)(2,1)}, s16[1168,256]{1,0:T(8,128)(2,1)S(1)}, u32[]{:S(2)}, u32[]{:S(2)}) collective-permute-start(s16[1168,256]{1,0:T(8,128)(2,1)} %get-tuple-element.36.refs_5_), channel_id=1, source_target_pairs={{0,2},{1,3},{2,0},{3,1},{4,6},{5,7},{6,4},{7,5},{8,10},{9,11},{10,... | collective-permute-start | bytes 1794056 | tf_op jit(solution)/shard_map/ppermute | solution.py:227
  21.6 0.9 copy-start.5
  22.4 14.1 %collective-permute-start.11 = (s16[1168,256]{1,0:T(8,128)(2,1)}, s16[1168,256]{1,0:T(8,128)(2,1)}, u32[]{:S(2)}, u32[]{:S(2)}) collective-permute-start(s16[1168,256]{1,0:T(8,128)(2,1)} %get-tuple-element.36.refs_5_), channel_id=1, source_target_pairs={{0,4},{1,5},{2,6},{3,7},{4,0},{5,1},{6,2},{7,3},{8,12},{9,13},{10,... | collective-permute-start | bytes 1794056 | tf_op jit(solution)/shard_map/ppermute | solution.py:227
  23.7 10.7 %copy-start.3 = (s16[1168,256]{1,0:T(8,128)(2,1)}, s16[1168,256]{1,0:T(8,128)(2,1)S(1)}, u32[]{:S(2)}) copy-start(s16[1168,256]{1,0:T(8,128)(2,1)S(1)} %collective-permute-done.9.refs_5_) | copy-start | bytes 1794052
  23.7 15.4 %collective-permute-start.15 = (s16[1168,256]{1,0:T(8,128)(2,1)}, s16[1168,256]{1,0:T(8,128)(2,1)}, u32[]{:S(2)}, u32[]{:S(2)}) collective-permute-start(s16[1168,256]{1,0:T(8,128)(2,1)} %collective-permute-done.6.refs_4_), channel_id=1, source_target_pairs={{0,8},{1,9},{2,10},{3,11},{8,16},{9,17},{10,18},{11,19},{12,4},{13... | collective-permute-start | bytes 1794056 | tf_op jit(solution)/shard_map/ppermute | solution.py:227
  34.4 9.8 %collective-permute-start.4 = (s16[1168,256]{1,0:T(8,128)(2,1)}, s16[1168,256]{1,0:T(8,128)(2,1)}, u32[]{:S(2)}, u32[]{:S(2)}) collective-permute-start(s16[1168,256]{1,0:T(8,128)(2,1)} %get-tuple-element.32), channel_id=1, source_target_pairs={{0,1},{1,0},{2,3},{3,2},{4,5},{5,4},{6,7},{7,6},{8,9},{9,8},{10,11... | collective-permute-start | bytes 1794056 | tf_op jit(solution)/shard_map/ppermute | solution.py:227
  36.5 13.7 %copy-start.7 = (s16[1168,256]{1,0:T(8,128)(2,1)S(1)}, s16[1168,256]{1,0:T(8,128)(2,1)}, u32[]{:S(2)}) copy-start(s16[1168,256]{1,0:T(8,128)(2,1)} %get-tuple-element.33.refs_4_) | copy-start | bytes 1794052
  36.5 13.7 %copy-start.8 = (s16[1168,256]{1,0:T(8,128)(2,1)S(1)}, s16[1168,256]{1,0:T(8,128)(2,1)}, u32[]{:S(2)}) copy-start(s16[1168,256]{1,0:T(8,128)(2,1)} %get-tuple-element.36.refs_5_) | copy-start | bytes 1794052
  36.5 6.9 %collective-permute-start.1 = (s32[2,45]{1,0:T(2,128)S(1)}, s32[2,45]{1,0:T(2,128)S(1)}, u32[]{:S(2)}, u32[]{:S(2)}) collective-permute-start(s32[2,45]{1,0:T(2,128)S(1)} %copy-done.9), channel_id=1, source_target_pairs={{0,1},{1,0},{2,3},{3,2},{4,5},{5,4},{6,7},{7,6},{8,9},{9,8},{10,11... | collective-permute-start | bytes 1088 | tf_op jit(solution)/shard_map/ppermute | solution.py:227
  39.0 4.0 %collective-permute-start = (s32[1,5]{1,0:T(1,128)}, s32[1,5]{1,0:T(1,128)S(1)}, u32[]{:S(2)}, u32[]{:S(2)}) collective-permute-start(s32[1,5]{1,0:T(1,128)} %own_ids.19), channel_id=1, source_target_pairs={{0,1},{1,0},{2,3},{3,2},{4,5},{5,4},{6,7},{7,6},{8,9},{9,8},{10,11... | collective-permute-start | bytes 68 | tf_op jit(solution)/shard_map/ppermute | solution.py:227
  41.8 16.6 %copy-start.4 = (s16[1168,256]{1,0:T(8,128)(2,1)S(1)}, s16[1168,256]{1,0:T(8,128)(2,1)}, u32[]{:S(2)}) copy-start(s16[1168,256]{1,0:T(8,128)(2,1)} %copy-done.3) | copy-start | bytes 1794052
  43.1 37.2 %collective-permute-start.12 = (s16[1168,256]{1,0:T(8,128)(2,1)}, s16[1168,256]{1,0:T(8,128)(2,1)S(1)}, u32[]{:S(2)}, u32[]{:S(2)}) collective-permute-start(s16[1168,256]{1,0:T(8,128)(2,1)} %copy-done.3), channel_id=1, source_target_pairs={{0,4},{1,5},{2,6},{3,7},{4,0},{5,1},{6,2},{7,3},{8,12},{9,13},{10,... | collective-permute-start | bytes 1794056 | tf_op jit(solution)/shard_map/ppermute | solution.py:227
  43.4 30.6 %collective-permute-start.14 = (s16[1168,256]{1,0:T(8,128)(2,1)}, s16[1168,256]{1,0:T(8,128)(2,1)S(1)}, u32[]{:S(2)}, u32[]{:S(2)}) collective-permute-start(s16[1168,256]{1,0:T(8,128)(2,1)} %copy-done.3), channel_id=1, source_target_pairs={{0,2},{1,3},{2,0},{3,1},{4,6},{5,7},{6,4},{7,5},{8,10},{9,11},{10,... | collective-permute-start | bytes 1794056 | tf_op jit(solution)/shard_map/ppermute | solution.py:227
  44.3 25.7 %collective-permute-start.16 = (s16[1168,256]{1,0:T(8,128)(2,1)}, s16[1168,256]{1,0:T(8,128)(2,1)S(1)}, u32[]{:S(2)}, u32[]{:S(2)}) collective-permute-start(s16[1168,256]{1,0:T(8,128)(2,1)} %collective-permute-done.11.refs_5_), channel_id=1, source_target_pairs={{0,8},{1,9},{2,10},{3,11},{8,16},{9,17},{10,18},{11,19},{12,4},{13... | collective-permute-start | bytes 1794056 | tf_op jit(solution)/shard_map/ppermute | solution.py:227
  46.7 32.7 %collective-permute-start.21 = (s16[1168,256]{1,0:T(8,128)(2,1)S(1)}, s16[1168,256]{1,0:T(8,128)(2,1)S(1)}, u32[]{:S(2)}, u32[]{:S(2)}) collective-permute-start(s16[1168,256]{1,0:T(8,128)(2,1)S(1)} %collective-permute-done.10.refs_5_), channel_id=1, source_target_pairs={{4,12},{5,13},{10,2},{11,3},{12,20},{13,21},{18,10},{19,11},{20,28... | collective-permute-start | bytes 1794056 | tf_op jit(solution)/shard_map/ppermute | solution.py:227
  47.4 41.0 %collective-permute-start.13 = (s16[1168,256]{1,0:T(8,128)(2,1)}, s16[1168,256]{1,0:T(8,128)(2,1)S(1)}, u32[]{:S(2)}, u32[]{:S(2)}) collective-permute-start(s16[1168,256]{1,0:T(8,128)(2,1)} %collective-permute-done.4.refs_4_), channel_id=1, source_target_pairs={{0,2},{1,3},{2,0},{3,1},{4,6},{5,7},{6,4},{7,5},{8,10},{9,11},{10,... | collective-permute-start | bytes 1794056 | tf_op jit(solution)/shard_map/ppermute | solution.py:227
  50.2 1.8 %copy-start.1 = (bf16[256,5760]{1,0:T(8,128)(2,1)S(1)}, bf16[256,5760]{1,0:T(8,128)(2,1)}, u32[]{:S(2)}) copy-start(bf16[256,5760]{1,0:T(8,128)(2,1)} %refs_1_.21) | copy-start | bytes 8847364
  52.1 0.7 copy-start.11
  58.4 5.4 %copy-start.6 = (s16[1168,256]{1,0:T(8,128)(2,1)S(1)}, s16[1168,256]{1,0:T(8,128)(2,1)}, u32[]{:S(2)}) copy-start(s16[1168,256]{1,0:T(8,128)(2,1)} %copy-done.5) | copy-start | bytes 1794052
  70.0 13.3 %collective-permute-start.7 = (s16[1168,256]{1,0:T(8,128)(2,1)}, s16[1168,256]{1,0:T(8,128)(2,1)S(1)}, u32[]{:S(2)}, u32[]{:S(2)}) collective-permute-start(s16[1168,256]{1,0:T(8,128)(2,1)} %collective-permute-done.4.refs_4_), channel_id=1, source_target_pairs={{0,4},{1,5},{2,6},{3,7},{4,0},{5,1},{6,2},{7,3},{8,12},{9,13},{10,... | collective-permute-start | bytes 1794056 | tf_op jit(solution)/shard_map/ppermute | solution.py:227
  71.4 19.0 %copy-start.2 = (bf16[256,5760]{1,0:T(8,128)(2,1)S(1)}, bf16[256,5760]{1,0:T(8,128)(2,1)}, u32[]{:S(2)}) copy-start(bf16[256,5760]{1,0:T(8,128)(2,1)} %refs_1_.21) | copy-start | bytes 8847364
  71.4 19.0 %copy-start.12 = (s32[1,5]{1,0:T(1,128)S(1)}, s32[1,5]{1,0:T(1,128)}, u32[]{:S(2)}) copy-start(s32[1,5]{1,0:T(1,128)} %own_ids.19) | copy-start | bytes 64
  74.0 46.1 %collective-permute-start.20 = (s16[1168,256]{1,0:T(8,128)(2,1)S(1)}, s16[1168,256]{1,0:T(8,128)(2,1)S(1)}, u32[]{:S(2)}, u32[]{:S(2)}) collective-permute-start(s16[1168,256]{1,0:T(8,128)(2,1)S(1)} %broadcast_select_fusion.1), channel_id=1, source_target_pairs={{0,2},{1,3},{2,0},{3,1},{4,6},{5,7},{6,4},{7,5},{8,10},{9,11},{10,... | collective-permute-start | bytes 1794056 | tf_op jit(solution)/shard_map/ppermute | solution.py:227
  79.4 22.2 %collective-permute-start.18 = (s16[1168,256]{1,0:T(8,128)(2,1)S(1)}, s16[1168,256]{1,0:T(8,128)(2,1)S(1)}, u32[]{:S(2)}, u32[]{:S(2)}) collective-permute-start(s16[1168,256]{1,0:T(8,128)(2,1)S(1)} %collective-permute-done.14.refs_5_), channel_id=1, source_target_pairs={{4,12},{5,13},{10,2},{11,3},{12,20},{13,21},{18,10},{19,11},{20,28... | collective-permute-start | bytes 1794056 | tf_op jit(solution)/shard_map/ppermute | solution.py:227
  80.3 39.9 %collective-permute-start.22 = (s16[1168,256]{1,0:T(8,128)(2,1)S(1)}, s16[1168,256]{1,0:T(8,128)(2,1)S(1)}, u32[]{:S(2)}, u32[]{:S(2)}) collective-permute-start(s16[1168,256]{1,0:T(8,128)(2,1)S(1)} %broadcast_select_fusion), channel_id=1, source_target_pairs={{0,4},{1,5},{2,6},{3,7},{4,0},{5,1},{6,2},{7,3},{8,12},{9,13},{10,... | collective-permute-start | bytes 1794056 | tf_op jit(solution)/shard_map/ppermute | solution.py:227
  83.3 35.6 %collective-permute-start.23 = (s16[1168,256]{1,0:T(8,128)(2,1)S(1)}, s16[1168,256]{1,0:T(8,128)(2,1)S(1)}, u32[]{:S(2)}, u32[]{:S(2)}) collective-permute-start(s16[1168,256]{1,0:T(8,128)(2,1)S(1)} %collective-permute-done.12.refs_5_), channel_id=1, source_target_pairs={{0,8},{1,9},{2,10},{3,11},{8,16},{9,17},{10,18},{11,19},{12,4},{13... | collective-permute-start | bytes 1794056 | tf_op jit(solution)/shard_map/ppermute | solution.py:227
  88.5 28.9 %collective-permute-start.8 = (s16[1168,256]{1,0:T(8,128)(2,1)S(1)}, s16[1168,256]{1,0:T(8,128)(2,1)S(1)}, u32[]{:S(2)}, u32[]{:S(2)}) collective-permute-start(s16[1168,256]{1,0:T(8,128)(2,1)S(1)} %collective-permute-done.7.refs_4_), channel_id=1, source_target_pairs={{0,8},{1,9},{2,10},{3,11},{8,16},{9,17},{10,18},{11,19},{12,4},{13... | collective-permute-start | bytes 1794056 | tf_op jit(solution)/shard_map/ppermute | solution.py:227
  101.8 23.0 %collective-permute-start.19 = (s16[1168,256]{1,0:T(8,128)(2,1)S(1)}, s16[1168,256]{1,0:T(8,128)(2,1)S(1)}, u32[]{:S(2)}, u32[]{:S(2)}) collective-permute-start(s16[1168,256]{1,0:T(8,128)(2,1)S(1)} %broadcast_select_fusion.2), channel_id=1, source_target_pairs={{0,4},{1,5},{2,6},{3,7},{4,0},{5,1},{6,2},{7,3},{8,12},{9,13},{10,... | collective-permute-start | bytes 1794056 | tf_op jit(solution)/shard_map/ppermute | solution.py:227
  117.5 14.0 %collective-permute-start.17 = (s16[1168,256]{1,0:T(8,128)(2,1)S(1)}, s16[1168,256]{1,0:T(8,128)(2,1)S(1)}, u32[]{:S(2)}, u32[]{:S(2)}) collective-permute-start(s16[1168,256]{1,0:T(8,128)(2,1)S(1)} %broadcast_select_fusion.3), channel_id=1, source_target_pairs={{0,2},{1,3},{2,0},{3,1},{4,6},{5,7},{6,4},{7,5},{8,10},{9,11},{10,... | collective-permute-start | bytes 1794056 | tf_op jit(solution)/shard_map/ppermute | solution.py:227
  131.5 18.4 %copy-start.13 = (s32[256]{0:T(256)S(1)}, s32[256]{0:T(256)}, u32[]{:S(2)}) copy-start(s32[256]{0:T(256)} %param.13) | copy-start | bytes 3076
  135.4 8.8 %collective-permute-start.24 = (bf16[2,2,32,512]{3,2,1,0:T(8,128)(2,1)S(1)}, bf16[2,2,32,512]{3,2,1,0:T(8,128)(2,1)S(1)}, u32[]{:S(2)}, u32[]{:S(2)}) collective-permute-start(bf16[2,2,32,512]{3,2,1,0:T(8,128)(2,1)S(1)} %get-tuple-element.55), channel_id=1, source_target_pairs={{0,1},{1,0},{2,3},{3,2},{4,5},{5,4},{6,7},{7,6},{8,9},{9,8},{10,11... | collective-permute-start | bytes 393224 | tf_op jit(solution)/shard_map/ppermute | solution.py:227
  137.5 9.6 %collective-permute-start.25 = (bf16[2,2,32,512]{3,2,1,0:T(8,128)(2,1)S(1)}, bf16[2,2,32,512]{3,2,1,0:T(8,128)(2,1)S(1)}, u32[]{:S(2)}, u32[]{:S(2)}) collective-permute-start(bf16[2,2,32,512]{3,2,1,0:T(8,128)(2,1)S(1)} %get-tuple-element.56), channel_id=1, source_target_pairs={{0,2},{1,3},{2,0},{3,1},{4,6},{5,7},{6,4},{7,5},{8,10},{9,11},{10,... | collective-permute-start | bytes 393224 | tf_op jit(solution)/shard_map/ppermute | solution.py:227
  140.6 9.4 %collective-permute-start.26 = (bf16[2,2,32,512]{3,2,1,0:T(8,128)(2,1)}, bf16[2,2,32,512]{3,2,1,0:T(8,128)(2,1)S(1)}, u32[]{:S(2)}, u32[]{:S(2)}) collective-permute-start(bf16[2,2,32,512]{3,2,1,0:T(8,128)(2,1)} %get-tuple-element.57), channel_id=1, source_target_pairs={{0,3},{1,2},{2,1},{3,0},{4,7},{5,6},{6,5},{7,4},{8,11},{9,10},{10,... | collective-permute-start | bytes 393224 | tf_op jit(solution)/shard_map/ppermute | solution.py:227
  140.7 9.4 %collective-permute-start.27 = (bf16[2,2,32,512]{3,2,1,0:T(8,128)(2,1)}, bf16[2,2,32,512]{3,2,1,0:T(8,128)(2,1)S(1)}, u32[]{:S(2)}, u32[]{:S(2)}) collective-permute-start(bf16[2,2,32,512]{3,2,1,0:T(8,128)(2,1)} %get-tuple-element.58), channel_id=1, source_target_pairs={{0,4},{1,5},{2,6},{3,7},{4,0},{5,1},{6,2},{7,3},{8,12},{9,13},{10,... | collective-permute-start | bytes 393224 | tf_op jit(solution)/shard_map/ppermute | solution.py:227
  144.0 12.4 %collective-permute-start.28 = (bf16[2,2,32,512]{3,2,1,0:T(8,128)(2,1)S(1)}, bf16[2,2,32,512]{3,2,1,0:T(8,128)(2,1)S(1)}, u32[]{:S(2)}, u32[]{:S(2)}) collective-permute-start(bf16[2,2,32,512]{3,2,1,0:T(8,128)(2,1)S(1)} %get-tuple-element.59), channel_id=1, source_target_pairs={{0,5},{1,4},{2,7},{3,6},{4,1},{5,0},{6,3},{7,2},{8,13},{9,12},{10,... | collective-permute-start | bytes 393224 | tf_op jit(solution)/shard_map/ppermute | solution.py:227
  144.3 12.1 %collective-permute-start.29 = (bf16[2,2,32,512]{3,2,1,0:T(8,128)(2,1)S(1)}, bf16[2,2,32,512]{3,2,1,0:T(8,128)(2,1)S(1)}, u32[]{:S(2)}, u32[]{:S(2)}) collective-permute-start(bf16[2,2,32,512]{3,2,1,0:T(8,128)(2,1)S(1)} %get-tuple-element.60), channel_id=1, source_target_pairs={{0,6},{1,7},{2,4},{3,5},{4,2},{5,3},{6,0},{7,1},{8,14},{9,15},{10,... | collective-permute-start | bytes 393224 | tf_op jit(solution)/shard_map/ppermute | solution.py:227
  147.2 9.2 %collective-permute-start.30 = (bf16[2,2,32,512]{3,2,1,0:T(8,128)(2,1)S(1)}, bf16[2,2,32,512]{3,2,1,0:T(8,128)(2,1)S(1)}, u32[]{:S(2)}, u32[]{:S(2)}) collective-permute-start(bf16[2,2,32,512]{3,2,1,0:T(8,128)(2,1)S(1)} %get-tuple-element.61), channel_id=1, source_target_pairs={{0,7},{1,6},{2,5},{3,4},{4,3},{5,2},{6,1},{7,0},{8,15},{9,14},{10,... | collective-permute-start | bytes 393224 | tf_op jit(solution)/shard_map/ppermute | solution.py:227

commit v3 on v2

--- a/solution.py
+++ b/solution.py
@@ -13,11 +13,10 @@
 STEPS = 64.0
 TOP = 32760.0
 CODE_ROWS = 16
-PACK_LIMIT = 60
 VMEM = pl.BlockSpec(memory_space=pltpu.VMEM)
 
 
-def quantize(x_ref, q_ref):
+def quantize(x_ref, q_ref, columns):
     tiles = x_ref.shape[0] // TILE
     codes = []
     for t in range(tiles):
@@ -27,47 +26,56 @@
         code = jnp.ceil(jnp.log2(top) * STEPS + 0.5)
         q = x * (jnp.exp2(code * (-1.0 / STEPS)) * TOP)
         q = jnp.minimum(jnp.maximum(q, -32767.0), 32767.0)
-        q_ref[rows, :] = jnp.round(q).astype(jnp.int32).astype(jnp.int16)
+        q_ref[rows, columns] = jnp.round(q).astype(jnp.int32).astype(jnp.int16)
         codes.append(code.astype(jnp.int32))
     codes.append(jnp.zeros((CODE_ROWS - tiles, x_ref.shape[1]), jnp.int32))
-    q_ref[pl.ds(tiles * TILE, CODE_ROWS), :] = jnp.concatenate(codes, axis=0).astype(jnp.int16)
-
-
-def pack_kernel(place_ref, *refs):
-    for x_ref, q_ref in zip(refs[: len(refs) // 2], refs[len(refs) // 2 :], strict=True):
-        quantize(x_ref, q_ref)
-
-
-def pack(place, mode_blocks):
+    q_ref[pl.ds(tiles * TILE, CODE_ROWS), columns] = jnp.concatenate(codes, axis=0).astype(jnp.int16)
+
+
+def pack_kernel(pieces, place_ref, source, *refs):
+    outs, (held, landed) = refs[-2 - len(pieces) : -2], refs[-2:]
+    steps = outs[0].shape[1] // TILE
+    copies = []
+    for n, piece in enumerate(pieces):
+        for i in range(steps):
+            block = ((place_ref[0] + piece // 2) % 2 * 2 + piece % 2) * steps + i
+            at = pl.multiple_of(block * TILE, TILE)
+            k = n * steps + i
+            copies.append(pltpu.make_async_copy(source.at[:, pl.ds(at, TILE)], held.at[k], landed.at[k]))
+            copies[-1].start()
+    for k, copy in enumerate(copies):
+        copy.wait()
+        quantize(held.at[k], outs[k // steps], pl.ds(k % steps * TILE, TILE))
+
+
+def pack(place, mode_blocks, pieces, grant, *landed):
     rows, modes = mode_blocks.shape
     width = modes // 4
-    steps = width // TILE
-    out = jax.ShapeDtypeStruct((rows + CODE_ROWS, width), jnp.int16)
-
-    def columns(piece):
-        return lambda i, place: (0, (((place[0] + piece // 2) % 2) * 2 + piece % 2) * steps + i)
-
+    tiles = len(pieces) * width // TILE
     return pl.pallas_call(
-        pack_kernel,
+        functools.partial(pack_kernel, pieces),
         grid_spec=pltpu.PrefetchScalarGridSpec(
             num_scalar_prefetch=1,
-            grid=(steps,),
-            in_specs=[pl.BlockSpec((rows, TILE), columns(piece)) for piece in range(4)],
-            out_specs=[pl.BlockSpec((rows + CODE_ROWS, TILE), lambda i, place: (0, i))] * 4,
+            grid=(),
+            in_specs=[pl.BlockSpec(memory_space=pltpu.HBM)] + [pl.BlockSpec(memory_space=pl.ANY)] * len(landed),
+            out_specs=[VMEM] * len(pieces),
+            scratch_shapes=[pltpu.VMEM((tiles, rows, TILE), jnp.float32), pltpu.SemaphoreType.DMA((tiles,))],
         ),
-        out_shape=(out,) * 4,
-        compiler_params=pltpu.CompilerParams(vmem_limit_bytes=PACK_LIMIT << 20),
-        cost_estimate=pl.CostEstimate(flops=rows * modes * 16, bytes_accessed=rows * modes * 6, transcendentals=0),
+        out_shape=[jax.ShapeDtypeStruct((rows + CODE_ROWS, width), jnp.int16)] * len(pieces),
+        compiler_params=pltpu.CompilerParams(vmem_limit_bytes=grant << 20),
+        cost_estimate=pl.CostEstimate(
+            flops=tiles * rows * TILE * 16, bytes_accessed=tiles * rows * TILE * 6, transcendentals=0
+        ),
         name="pack",
-    )(place, *[mode_blocks] * 4)
-
-
-def slot_kernel(away, other, first, last, place_ref, owner_ref, own_ids, other_ids, own_mask, other_mask, *refs):
+    )(place, mode_blocks, *landed)
+
+
+def slot_kernel(away, other, outs, first, last, place_ref, owner_ref, own_ids, other_ids, own_mask, other_mask, *refs):
     own_rows, other_rows = refs[0:2], refs[2:4]
     a_ref, b_ref = refs[4:6]
-    total = refs[6] if last or first else refs[7]
     high, low, left, landed = refs[-4:]
-    outs = refs[7:-4]
+    outs = refs[-4 - outs :][:outs]
+    total = refs[6] if last else outs[0]
     depth = high.shape[0]
     width = a_ref.shape[1]
     tiles = depth // TILE
@@ -129,14 +137,9 @@
                                 (TILE, TILE), left.dtype
                             )
 
-            step = 2 * TILE
-
-            @pl.loop(0, high.shape[1] // step)
-            def _(i):
-                span = pl.ds(pl.multiple_of(i * step, step), step)
-                total[who, :, span] += jnp.dot(left[who], high[:, span], preferred_element_type=jnp.float32) + jnp.dot(
-                    left[who], low[:, span], preferred_element_type=jnp.float32
-                )
+            total[who] += jnp.dot(left[who], high[...], preferred_element_type=jnp.float32) + jnp.dot(
+                left[who], low[...], preferred_element_type=jnp.float32
+            )
 
     if last:
         _, kinds, part, _ = outs[0].shape
@@ -146,11 +149,9 @@
                 span = pl.ds(pl.multiple_of((kind * len(outs) + to) * part, part), part)
                 for who in range(2):
                     out_ref[who, kind] = total[who, span, :].astype(jnp.bfloat16)
-    else:
-        refs[-5][...] = jnp.zeros_like(refs[-5])
-
-
-def add_slot(place, away, other, owner_slot, ids, masks, rows, pieces, total, devices=None):
+
+
+def add_slot(place, away, other, owner_slot, ids, masks, rows, pieces, total, devices=None, hold=()):
     height = rows[0][0].shape[0]
     depth = rows[0][0].shape[1] // ids[0].shape[1]
     width = 2 * pieces[0].shape[1]
@@ -158,15 +159,21 @@
     if last:
         out_shape = [jax.ShapeDtypeStruct((2, 2, height // devices, width), jnp.bfloat16)] * devices
     else:
-        out_shape = [jax.ShapeDtypeStruct((2, 2 * height, width), jnp.float32), jax.ShapeDtypeStruct((8, TILE), jnp.int32)]
-    hbm = pl.BlockSpec(memory_space=pl.ANY)
+        out_shape = [jax.ShapeDtypeStruct((2, 2 * height, width), jnp.float32)]
+    sums = len(out_shape)
+    out_shape += [jax.ShapeDtypeStruct(x.shape, x.dtype) for x in hold]
+    anywhere = pl.BlockSpec(memory_space=pl.ANY)
+    at = 12 if first else 13
+    aliases = {at + n: sums + n for n in range(len(hold))}
+    if not (first or last):
+        aliases[12] = 0
     return pl.pallas_call(
-        functools.partial(slot_kernel, away, other, first, last),
+        functools.partial(slot_kernel, away, other, len(out_shape), first, last),
         grid_spec=pltpu.PrefetchScalarGridSpec(
             num_scalar_prefetch=6,
             grid=(),
-            in_specs=[hbm] * 4 + [VMEM] * (2 if first else 3),
-            out_specs=[VMEM] * len(out_shape),
+            in_specs=[pl.BlockSpec(memory_space=pltpu.HBM)] * 4 + [VMEM] * (2 if first else 3) + [anywhere] * len(hold),
+            out_specs=[VMEM] * sums + [anywhere] * len(hold),
             scratch_shapes=[
                 pltpu.VMEM((depth, width), jnp.bfloat16),
                 pltpu.VMEM((depth, width), jnp.bfloat16),
@@ -175,11 +182,11 @@
             ],
         ),
         out_shape=out_shape,
-        input_output_aliases={} if first or last else {12: 0},
-        compiler_params=pltpu.CompilerParams(vmem_limit_bytes=12 << 20),
-        cost_estimate=pl.CostEstimate(flops=16 * height * depth * width, bytes_accessed=depth * width * 2, transcendentals=0),
+        input_output_aliases=aliases,
+        compiler_params=pltpu.CompilerParams(vmem_limit_bytes=44 << 20),
+        cost_estimate=pl.CostEstimate(flops=4 * height * depth * width, bytes_accessed=depth * width // 2, transcendentals=0),
         name="slot",
-    )(place, owner_slot, *ids, *masks, *rows[0], *rows[1], *pieces, *(() if first else (total,)))
+    )(place, owner_slot, *ids, *masks, *rows[0], *rows[1], *pieces, *(() if first else (total,)), *hold)
 
 
 def order_kernel(place_ref, order_ref, *refs):
@@ -227,7 +234,7 @@
     return lax.ppermute(x, AXES, [(i, t) for i, t in pairs if t is not None and 0 <= t < count])
 
 
-def direct(own, partners, count, index, add):
+def direct(own, count, index, add):
     slots = [(lambda index: 0, own)]
     for chips in range(-(REACH // 2), REACH // 2 + 1):
         if chips:
@@ -239,8 +246,9 @@
     return parts
 
 
-def routed(own, partners, count, index, add):
+def routed(own, count, index, add):
     x, y, z, half, d = {}, {}, {}, {}, {}
+    outer = (index // 4 % 2) == (index // 2 % 2)
 
     def beside(k, *landed):
         x[k] = permute(after(own[k], *landed), count, lambda i: i ^ 2)
@@ -248,16 +256,13 @@
 
     def beyond(k, *landed):
         z[k] = permute(after(y[k], *landed), count, lambda i: i - 8 if i & 4 else i + 8)
-        if k[1] == 1:
-            target = lambda i: None if (i >> 2 ^ i >> 1) & 1 == 0 else (i + 8 if i & 4 else i - 8)
-            half[k] = permute(after(x[k], *landed), count, target)
-
-    def around(k, *landed):
-        outer = (index // 4 % 2) == (index // 2 % 2)
-        if k[1] == 0:
-            d[k] = permute(after(jnp.where(outer, y[k], z[k]), *landed), count, lambda i: i ^ 2)
-        else:
-            d[k] = permute(after(jnp.where(outer, x[k], half[k]), *landed), count, lambda i: i ^ 4)
+
+    def beyond_half(k, *landed):
+        target = lambda i: None if (i >> 2 ^ i >> 1) & 1 == 0 else (i + 8 if i & 4 else i - 8)
+        half[k] = permute(after(x[k], *landed), count, target)
+
+    def around(k):
+        return jnp.where(outer, x[k], half[k]) if k[1] else jnp.where(outer, y[k], z[k])
 
     away = {
         "own": lambda index: 0,
@@ -269,23 +274,25 @@
     oa, ob, pa, pb = (0, 0), (0, 1), (1, 0), (1, 1)
     beside(oa)
     beside(ob)
-    beside(pa, x[oa], y[oa], *partners)
+    beside(pa, x[oa], y[oa], own[pb])
     beyond(oa)
-    add(away["own"], 0, own, x[oa], y[oa])
-    done = add(away["own"], 1, own)
-    beside(pb, x[ob], y[ob], done)
-    beyond(ob)
+    (own[pb],) = add(away["own"], 0, own, hold=(own[pb],))
+    add(away["own"], 1, own)
+    beside(pb, x[ob], y[ob])
+    beyond(ob, z[oa])
     add(away["x"], 0, x)
-    done = add(away["y"], 0, y)
-    around(oa)
-    beyond(pa, done)
-    around(ob)
-    done = add(away["z"], 0, z)
-    beyond(pb, done)
-    add(away["x"], 1, x)
-    done = add(away["y"], 1, y)
-    around(pa, done)
-    around(pb, done)
+    (passed,) = add(away["y"], 0, y, hold=(around(oa),))
+    beyond_half(ob, x[pa], z[oa])
+    beyond(pa)
+    d[oa] = permute(after(passed, z[ob]), count, lambda i: i ^ 2)
+    add(away["z"], 0, z)
+    d[ob] = permute(around(ob), count, lambda i: i ^ 4)
+    beyond_half(pb)
+    beyond(pb)
+    (passed,) = add(away["x"], 1, x, hold=(around(pa),))
+    d[pa] = permute(passed, count, lambda i: i ^ 2)
+    add(away["y"], 1, y)
+    d[pb] = permute(around(pb), count, lambda i: i ^ 4)
     add(away["z"], 1, z)
     add(away["d"], 0, d)
     return add(away["d"], 1, d, last=True)
@@ -300,23 +307,24 @@
     def partner(x):
         return permute(x, count, lambda i: i ^ 1)
 
-    packed = pack(place, mode_blocks)
-    keys = ((0, 0), (0, 1), (1, 0), (1, 1))
-    own = dict(zip(keys, (*packed[:2], *(partner(x) for x in packed[2:])), strict=True))
-    partners = [partner(x) for x in (stiffness, mass_tiles, reader_ids, tile_mask)]
+    partners = [partner(x) for x in (stiffness, mass_tiles)]
+    partners += [partner(after(x, *partners)) for x in (reader_ids, tile_mask)]
+    (first,) = pack(place, mode_blocks, (0,), 60)
+    second, *sent = pack(place, mode_blocks, (1, 2, 3), 48, *partners[:2], first)
+    own = dict(zip(((0, 0), (0, 1), (1, 0), (1, 1)), (first, second, *map(partner, sent)), strict=True))
     rows = ((stiffness, mass_tiles), tuple(partners[:2]))
     ids, masks = (reader_ids, partners[2]), (tile_mask, partners[3])
     total = [None]
 
-    def add(away, other, pieces, *landed, last=False):
+    def add(away, other, pieces, last=False, hold=()):
         pair = (pieces[other, 0], pieces[other, 1])
-        out = add_slot(after(place, *landed), away, other, owner_slot, ids, masks, rows, pair, total[0], devices if last else None)
+        out = add_slot(place, away, other, owner_slot, ids, masks, rows, pair, total[0], devices if last else None, hold)
         if last:
             return out
-        total[0], token = out
-        return token
-
-    parts = (routed if devices == 8 else direct)(own, partners, count, index, add)
+        total[0] = out[0]
+        return out[1:]
+
+    parts = (routed if devices == 8 else direct)(own, count, index, add)
     parts = [permute(x, count, lambda i, by=by: i ^ by) if by else x for by, x in enumerate(parts)]
     return order_rows(place, tree_order, parts)
 

time: 158 us -> 126 us (0.80)
  the two profiles are of different devices: /device:TPU:17 before, /device:TPU:15 now
where the time goes in v3:
time: 126 us
  waiting for transfers between devices  42.9 us (34%)
  Pallas kernels  40.8 us (32%)
  starting transfers between devices  32.8 us (26%)
  local copies, waits for them, and re-layouts  6.43 us (5%)
  other arithmetic  1.72 us (1%)
    ppermute x31, waiting for transfers between devices, permute(): lax.ppermute(x, AXES, [(i, t) for i, t in pairs if t is not None and 0 <=...  42.9 us
    pallas_call x10, Pallas kernels, add_slot(): pl.pallas_call(functools.partial(slot_kernel, away, other, len(out_shape)...  34.2 us
    ppermute x31, starting transfers between devices, permute(): lax.ppermute(x, AXES, [(i, t) for i, t in pairs if t is not None and 0 <=...  32.8 us
    unnamed x28, local copies, waits for them, and re-layouts  6.3 us
    pallas_call x2, Pallas kernels, pack(): pl.pallas_call(functools.partial(pack_kernel, pieces), grid_spec=pltpu.Pr...  5.23 us
  transfers between devices with their start and end apart: 31, of which 12 were waited for; matrix products, arithmetic and copies ran while one was open for 1% of the time, Pallas kernels for 29%

profile of v3, /device:TPU:15, one launch (start us, length us, event | category | flops | bytes accessed | tf_op | source)
XLA Modules:
  0.0 125.7 jit_solution(3262879533256970190)
XLA Ops:
  0.6 0.7 collective-permute-start
  1.5 2.3 %pack.2.refs_2_.refs_4_ = s16[1168,256]{1,0:T(8,128)(2,1)} custom-call(s32[1]{0:T(128)} %bitcast.place_ref, f32[1152,1024]{1,0:T(8,128)} %source.3), custom_call_target="tpu_custom_call" | custom-call | flops 4718592 | bytes 1769472 | tf_op jit(solution)/shard_map/pack/pallas_call | solution.py:55
  4.3 5.7 %collective-permute-done.refs_0_.refs_2_ = bf16[256,5760]{1,0:T(8,128)(2,1)S(1)} collective-permute-done((bf16[256,5760]{1,0:T(8,128)(2,1)}, bf16[256,5760]{1,0:T(8,128)(2,1)S(1)}, u32[]{:S(2)}, u32[]{:S(2)}) %collective-permute-start) | collective-permute-done | bytes 2949152 | tf_op jit(solution)/shard_map/ppermute | solution.py:234
  10.0 0.9 collective-permute-done.1.refs_1_.refs_3_
  10.9 1.1 copy-done.5
  12.1 2.9 %pack.3 = (s16[1168,256]{1,0:T(8,128)(2,1)}, s16[1168,256]{1,0:T(8,128)(2,1)S(1)}, s16[1168,256]{1,0:T(8,128)(2,1)S(1)}) custom-call(s32[1]{0:T(128)} %bitcast.place_ref, f32[1152,1024]{1,0:T(8,128)} %source.3, bf16[256,5760]{1,0:T(8,128)(2,1)S(1)} %collective-permute-done.refs_0_.refs_2_, bf16[256,5760]{1,0:T(8,128)(2,1)} %collective-permute-done.1.refs_1_.refs_3_, ...), custom_call_target="tpu_custom_call" | custom-call | flops 14155776 | bytes 5308416 | tf_op jit(solution)/shard_map/pack/pallas_call | solution.py:55
  15.9 2.9 %collective-permute-done.6.refs_4_ = s16[1168,256]{1,0:T(8,128)(2,1)} collective-permute-done((s16[1168,256]{1,0:T(8,128)(2,1)}, s16[1168,256]{1,0:T(8,128)(2,1)}, u32[]{:S(2)}, u32[]{:S(2)}) %collective-permute-start.6) | collective-permute-done | bytes 598048 | tf_op jit(solution)/shard_map/ppermute | solution.py:234
  19.0 0.8 copy-done.7
  19.8 2.1 %collective-permute-start.12 = (s16[1168,256]{1,0:T(8,128)(2,1)}, s16[1168,256]{1,0:T(8,128)(2,1)S(1)}, u32[]{:S(2)}, u32[]{:S(2)}) collective-permute-start(s16[1168,256]{1,0:T(8,128)(2,1)} %collective-permute-done.6.refs_4_), channel_id=1, source_target_pairs={{0,8},{1,9},{2,10},{3,11},{8,16},{9,17},{10,18},{11,19},{12,4},{13... | collective-permute-start | bytes 1794056 | tf_op jit(solution)/shard_map/ppermute | solution.py:234
  22.3 2.4 %collective-permute-start.2 = (s32[1,5]{1,0:T(1,128)}, s32[1,5]{1,0:T(1,128)S(1)}, u32[]{:S(2)}, u32[]{:S(2)}) collective-permute-start(s32[1,5]{1,0:T(1,128)} %own_ids.19), channel_id=1, source_target_pairs={{0,1},{1,0},{2,3},{3,2},{4,5},{5,4},{6,7},{7,6},{8,9},{9,8},{10,11... | collective-permute-start | bytes 68 | tf_op jit(solution)/shard_map/ppermute | solution.py:234
  24.7 1.0 collective-permute-done.2.other_ids
  26.0 0.8 collective-permute-done.3.other_mask
  26.8 2.8 %collective-permute-start.14 = (s16[1168,256]{1,0:T(8,128)(2,1)}, s16[1168,256]{1,0:T(8,128)(2,1)S(1)}, u32[]{:S(2)}, u32[]{:S(2)}) collective-permute-start(s16[1168,256]{1,0:T(8,128)(2,1)} %collective-permute-done.4.refs_4_), channel_id=1, source_target_pairs={{0,4},{1,5},{2,6},{3,7},{4,0},{5,1},{6,2},{7,3},{8,12},{9,13},{10,... | collective-permute-start | bytes 1794056 | tf_op jit(solution)/shard_map/ppermute | solution.py:234
  29.6 1.8 %copy-done.1 = bf16[256,5760]{1,0:T(8,128)(2,1)S(1)} copy-done((bf16[256,5760]{1,0:T(8,128)(2,1)S(1)}, bf16[256,5760]{1,0:T(8,128)(2,1)}, u32[]{:S(2)}) %copy-start.1) | copy-done | bytes 2949144
  31.5 1.8 %copy-done.3 = bf16[256,5760]{1,0:T(8,128)(2,1)S(1)} copy-done((bf16[256,5760]{1,0:T(8,128)(2,1)S(1)}, bf16[256,5760]{1,0:T(8,128)(2,1)}, u32[]{:S(2)}) %copy-start.3) | copy-done | bytes 2949144
  33.3 0.7 copy-done.11
  34.0 4.4 %slot.10 = (f32[2,512,512]{2,1,0:T(8,128)S(1)}, s16[1168,256]{1,0:T(8,128)(2,1)S(1)}) custom-call(s32[1]{0:T(128)} %bitcast.place_ref, s32[32]{0:T(128)S(1)} %copy-done.10, s32[1,5]{1,0:T(1,128)S(1)} %copy-done.11, s32[1,5]{1,0:T(1,128)S(1)} %collective-permute-done.2.other_ids, s32[2,45]{1,0:T(2,128)S(1)} %copy-done.9, ...), custom_call_target="tpu_custom_call", output_to_operand_aliasing={{1}: (12, {})} | custom-call | flops 603979776 | bytes 294912 | tf_op jit(solution)/shard_map/slot/pallas_call | solution.py:170
  38.4 1.3 %collective-permute-start.11 = (s16[1168,256]{1,0:T(8,128)(2,1)S(1)}, s16[1168,256]{1,0:T(8,128)(2,1)S(1)}, u32[]{:S(2)}, u32[]{:S(2)}) collective-permute-start(s16[1168,256]{1,0:T(8,128)(2,1)S(1)} %get-tuple-element.33.refs_5_), channel_id=1, source_target_pairs={{0,2},{1,3},{2,0},{3,1},{4,6},{5,7},{6,4},{7,5},{8,10},{9,11},{10,... | collective-permute-start | bytes 1794056 | tf_op jit(solution)/shard_map/ppermute | solution.py:234
  39.7 1.7 %collective-permute-start.22 = (s16[1168,256]{1,0:T(8,128)(2,1)S(1)}, s16[1168,256]{1,0:T(8,128)(2,1)S(1)}, u32[]{:S(2)}, u32[]{:S(2)}) collective-permute-start(s16[1168,256]{1,0:T(8,128)(2,1)S(1)} %get-tuple-element.33.refs_5_), channel_id=1, source_target_pairs={{0,4},{1,5},{2,6},{3,7},{4,0},{5,1},{6,2},{7,3},{8,12},{9,13},{10,... | collective-permute-start | bytes 1794056 | tf_op jit(solution)/shard_map/ppermute | solution.py:234
  41.4 2.1 %collective-permute-start.13 = (s16[1168,256]{1,0:T(8,128)(2,1)}, s16[1168,256]{1,0:T(8,128)(2,1)S(1)}, u32[]{:S(2)}, u32[]{:S(2)}) collective-permute-start(s16[1168,256]{1,0:T(8,128)(2,1)} %collective-permute-done.10.refs_5_), channel_id=1, source_target_pairs={{0,8},{1,9},{2,10},{3,11},{8,16},{9,17},{10,18},{11,19},{12,4},{13... | collective-permute-start | bytes 1794056 | tf_op jit(solution)/shard_map/ppermute | solution.py:234
  43.5 0.7 collective-permute-done.8.refs_4_
  44.2 0.7 collective-permute-start.20
  44.9 1.3 broadcast_select_fusion.3.refs_7_
  46.2 5.7 %slot.11.refs_6_ = f32[2,512,512]{2,1,0:T(8,128)S(1)} custom-call(s32[1]{0:T(128)} %bitcast.place_ref, s32[32]{0:T(128)S(1)} %copy-done.10, s32[1,5]{1,0:T(1,128)S(1)} %copy-done.12, s32[1,5]{1,0:T(1,128)S(1)} %collective-permute-done.2.other_ids, s32[2,45]{1,0:T(2,128)S(1)} %copy-done.9, ...), custom_call_target="tpu_custom_call", output_to_operand_aliasing={{}: (12, {})} | custom-call | flops 603979776 | bytes 294912 | tf_op jit(solution)/shard_map/slot/pallas_call | solution.py:170
  52.0 0.7 slot.12.refs_6_
  52.6 4.4 %collective-permute-done.11.refs_5_ = s16[1168,256]{1,0:T(8,128)(2,1)S(1)} collective-permute-done((s16[1168,256]{1,0:T(8,128)(2,1)S(1)}, s16[1168,256]{1,0:T(8,128)(2,1)S(1)}, u32[]{:S(2)}, u32[]{:S(2)}) %collective-permute-start.11) | collective-permute-done | bytes 598048 | tf_op jit(solution)/shard_map/ppermute | solution.py:234
  57.0 0.7 collective-permute-start.17
  57.7 4.7 %slot.13 = (f32[2,512,512]{2,1,0:T(8,128)S(1)}, s16[1168,256]{1,0:T(8,128)(2,1)S(1)}) custom-call(s32[1]{0:T(128)} %bitcast.place_ref, s32[32]{0:T(128)S(1)} %copy-done.10, s32[1,5]{1,0:T(1,128)S(1)} %copy-done.12, s32[1,5]{1,0:T(1,128)S(1)} %collective-permute-done.2.other_ids, ...), custom_call_target="tpu_custom_call", output_to_operand_aliasing={{1}: (13, {}), {0}: (12, {})} | custom-call | flops 603979776 | bytes 294912 | tf_op jit(solution)/shard_map/slot/pallas_call | solution.py:170
  62.5 4.2 %collective-permute-start.19 = (s16[1168,256]{1,0:T(8,128)(2,1)S(1)}, s16[1168,256]{1,0:T(8,128)(2,1)S(1)}, u32[]{:S(2)}, u32[]{:S(2)}) collective-permute-start(s16[1168,256]{1,0:T(8,128)(2,1)S(1)} %get-tuple-element.39), channel_id=1, source_target_pairs={{0,2},{1,3},{2,0},{3,1},{4,6},{5,7},{6,4},{7,5},{8,10},{9,11},{10,... | collective-permute-start | bytes 1794056 | tf_op jit(solution)/shard_map/ppermute | solution.py:234
  66.6 1.9 %collective-permute-start.15 = (s16[1168,256]{1,0:T(8,128)(2,1)S(1)}, s16[1168,256]{1,0:T(8,128)(2,1)S(1)}, u32[]{:S(2)}, u32[]{:S(2)}) collective-permute-start(s16[1168,256]{1,0:T(8,128)(2,1)S(1)} %collective-permute-done.14.refs_4_), channel_id=1, source_target_pairs={{0,8},{1,9},{2,10},{3,11},{8,16},{9,17},{10,18},{11,19},{12,4},{13... | collective-permute-start | bytes 1794056 | tf_op jit(solution)/shard_map/ppermute | solution.py:234
  68.6 1.9 %collective-permute-start.23 = (s16[1168,256]{1,0:T(8,128)(2,1)S(1)}, s16[1168,256]{1,0:T(8,128)(2,1)S(1)}, u32[]{:S(2)}, u32[]{:S(2)}) collective-permute-start(s16[1168,256]{1,0:T(8,128)(2,1)S(1)} %collective-permute-done.22.refs_5_), channel_id=1, source_target_pairs={{0,8},{1,9},{2,10},{3,11},{8,16},{9,17},{10,18},{11,19},{12,4},{13... | collective-permute-start | bytes 1794056 | tf_op jit(solution)/shard_map/ppermute | solution.py:234
  70.5 3.0 %slot.14.refs_6_ = f32[2,512,512]{2,1,0:T(8,128)S(1)} custom-call(s32[1]{0:T(128)} %bitcast.place_ref, s32[32]{0:T(128)S(1)} %copy-done.10, s32[1,5]{1,0:T(1,128)S(1)} %copy-done.12, s32[1,5]{1,0:T(1,128)S(1)} %collective-permute-done.2.other_ids, s32[2,45]{1,0:T(2,128)S(1)} %copy-done.9, ...), custom_call_target="tpu_custom_call", output_to_operand_aliasing={{}: (12, {})} | custom-call | flops 603979776 | bytes 294912 | tf_op jit(solution)/shard_map/slot/pallas_call | solution.py:170
  73.6 1.2 collective-permute-start.21
  75.4 6.8 %collective-permute-done.15.refs_4_ = s16[1168,256]{1,0:T(8,128)(2,1)S(1)} collective-permute-done((s16[1168,256]{1,0:T(8,128)(2,1)S(1)}, s16[1168,256]{1,0:T(8,128)(2,1)S(1)}, u32[]{:S(2)}, u32[]{:S(2)}) %collective-permute-start.15) | collective-permute-done | bytes 598048 | tf_op jit(solution)/shard_map/ppermute | solution.py:234
  82.4 3.0 %slot.15 = (f32[2,512,512]{2,1,0:T(8,128)S(1)}, s16[1168,256]{1,0:T(8,128)(2,1)S(1)}) custom-call(s32[1]{0:T(128)} %bitcast.place_ref, s32[32]{0:T(128)S(1)} %copy-done.10, s32[1,5]{1,0:T(1,128)S(1)} %copy-done.12, s32[1,5]{1,0:T(1,128)S(1)} %collective-permute-done.2.other_ids, ...), custom_call_target="tpu_custom_call", output_to_operand_aliasing={{1}: (13, {}), {0}: (12, {})} | custom-call | flops 603979776 | bytes 294912 | tf_op jit(solution)/shard_map/slot/pallas_call | solution.py:170
  85.5 0.7 slot.16.refs_6_
  86.1 8.9 %collective-permute-done.23.refs_5_ = s16[1168,256]{1,0:T(8,128)(2,1)S(1)} collective-permute-done((s16[1168,256]{1,0:T(8,128)(2,1)S(1)}, s16[1168,256]{1,0:T(8,128)(2,1)S(1)}, u32[]{:S(2)}, u32[]{:S(2)}) %collective-permute-start.23) | collective-permute-done | bytes 598048 | tf_op jit(solution)/shard_map/ppermute | solution.py:234
  95.1 3.6 %slot.17.refs_6_ = f32[2,512,512]{2,1,0:T(8,128)S(1)} custom-call(s32[1]{0:T(128)} %bitcast.place_ref, s32[32]{0:T(128)S(1)} %copy-done.10, s32[1,5]{1,0:T(1,128)S(1)} %copy-done.12, s32[1,5]{1,0:T(1,128)S(1)} %collective-permute-done.2.other_ids, s32[2,45]{1,0:T(2,128)S(1)} %copy-done.9, ...), custom_call_target="tpu_custom_call", output_to_operand_aliasing={{}: (12, {})} | custom-call | flops 603979776 | bytes 294912 | tf_op jit(solution)/shard_map/slot/pallas_call | solution.py:170
  98.7 4.9 %slot.18.refs_6_ = f32[2,512,512]{2,1,0:T(8,128)S(1)} custom-call(s32[1]{0:T(128)} %bitcast.place_ref, s32[32]{0:T(128)S(1)} %copy-done.10, s32[1,5]{1,0:T(1,128)S(1)} %copy-done.12, s32[1,5]{1,0:T(1,128)S(1)} %collective-permute-done.2.other_ids, s32[2,45]{1,0:T(2,128)S(1)} %copy-done.9, ...), custom_call_target="tpu_custom_call", output_to_operand_aliasing={{}: (12, {})} | custom-call | flops 603979776 | bytes 294912 | tf_op jit(solution)/shard_map/slot/pallas_call | solution.py:170
  103.6 3.6 %slot.19 = (bf16[2,2,32,512]{3,2,1,0:T(8,128)(2,1)S(1)}, bf16[2,2,32,512]{3,2,1,0:T(8,128)(2,1)S(1)}, bf16[2,2,32,512]{3,2,1,0:T(8,128)(2,1)S(1)}, bf16[2,2,32,5...) custom-call(s32[1]{0:T(128)} %bitcast.place_ref, ...), custom_call_target="tpu_custom_call" | custom-call | flops 603979776 | bytes 294912 | tf_op jit(solution)/shard_map/slot/pallas_call | solution.py:170
  107.3 1.7 %collective-permute-start.24 = (bf16[2,2,32,512]{3,2,1,0:T(8,128)(2,1)S(1)}, bf16[2,2,32,512]{3,2,1,0:T(8,128)(2,1)S(1)}, u32[]{:S(2)}, u32[]{:S(2)}) collective-permute-start(bf16[2,2,32,512]{3,2,1,0:T(8,128)(2,1)S(1)} %get-tuple-element.43), channel_id=1, source_target_pairs={{0,1},{1,0},{2,3},{3,2},{4,5},{5,4},{6,7},{7,6},{8,9},{9,8},{10,11... | collective-permute-start | bytes 393224 | tf_op jit(solution)/shard_map/ppermute | solution.py:234
  109.0 1.7 %collective-permute-start.26 = (bf16[2,2,32,512]{3,2,1,0:T(8,128)(2,1)S(1)}, bf16[2,2,32,512]{3,2,1,0:T(8,128)(2,1)S(1)}, u32[]{:S(2)}, u32[]{:S(2)}) collective-permute-start(bf16[2,2,32,512]{3,2,1,0:T(8,128)(2,1)S(1)} %get-tuple-element.45), channel_id=1, source_target_pairs={{0,3},{1,2},{2,1},{3,0},{4,7},{5,6},{6,5},{7,4},{8,11},{9,10},{10,... | collective-permute-start | bytes 393224 | tf_op jit(solution)/shard_map/ppermute | solution.py:234
  110.7 1.8 %collective-permute-start.28 = (bf16[2,2,32,512]{3,2,1,0:T(8,128)(2,1)S(1)}, bf16[2,2,32,512]{3,2,1,0:T(8,128)(2,1)S(1)}, u32[]{:S(2)}, u32[]{:S(2)}) collective-permute-start(bf16[2,2,32,512]{3,2,1,0:T(8,128)(2,1)S(1)} %get-tuple-element.47), channel_id=1, source_target_pairs={{0,5},{1,4},{2,7},{3,6},{4,1},{5,0},{6,3},{7,2},{8,13},{9,12},{10,... | collective-permute-start | bytes 393224 | tf_op jit(solution)/shard_map/ppermute | solution.py:234
  112.5 1.5 %collective-permute-done.25.refs_2_ = bf16[2,2,32,512]{3,2,1,0:T(8,128)(2,1)S(1)} collective-permute-done((bf16[2,2,32,512]{3,2,1,0:T(8,128)(2,1)S(1)}, bf16[2,2,32,512]{3,2,1,0:T(8,128)(2,1)S(1)}, u32[]{:S(2)}, u32[]{:S(2)}) %collective-permute-start.25) | collective-permute-done | bytes 131104 | tf_op jit(solution)/shard_map/ppermute | solution.py:234
  114.0 1.0 collective-permute-start.30
  115.2 2.5 %collective-permute-done.26.refs_3_ = bf16[2,2,32,512]{3,2,1,0:T(8,128)(2,1)S(1)} collective-permute-done((bf16[2,2,32,512]{3,2,1,0:T(8,128)(2,1)S(1)}, bf16[2,2,32,512]{3,2,1,0:T(8,128)(2,1)S(1)}, u32[]{:S(2)}, u32[]{:S(2)}) %collective-permute-start.26) | collective-permute-done | bytes 131104 | tf_op jit(solution)/shard_map/ppermute | solution.py:234
  117.7 6.6 %collective-permute-done.28.refs_5_ = bf16[2,2,32,512]{3,2,1,0:T(8,128)(2,1)S(1)} collective-permute-done((bf16[2,2,32,512]{3,2,1,0:T(8,128)(2,1)S(1)}, bf16[2,2,32,512]{3,2,1,0:T(8,128)(2,1)S(1)}, u32[]{:S(2)}, u32[]{:S(2)}) %collective-permute-start.28) | collective-permute-done | bytes 131104 | tf_op jit(solution)/shard_map/ppermute | solution.py:234
  124.3 1.4 %order.1 = (bf16[256,1024]{1,0:T(8,128)(2,1)}, bf16[256,1024]{1,0:T(8,128)(2,1)}) custom-call(s32[1]{0:T(128)} %bitcast.place_ref, s32[256,1]{1,0:T(8,128)S(1)} %copy.20.order_ref, bf16[2,2,32,512]{3,2,1,0:T(8,128)(2,1)S(1)} %get-tuple-element.42.refs_0_, bf16[2,2,32,512]{3,2,1,0:T(8,128)(2,1)S(1)} %collective-permute-done.24.refs_1_, ...), custom_call_target="tpu_custom_call" | custom-call | tf_op jit(solution)/shard_map/order/pallas_call | solution.py:217
  (60 shorter events, 3.6 us)
Async XLA Ops:
  0.6 9.4 %collective-permute-start = (bf16[256,5760]{1,0:T(8,128)(2,1)}, bf16[256,5760]{1,0:T(8,128)(2,1)S(1)}, u32[]{:S(2)}, u32[]{:S(2)}) collective-permute-start(bf16[256,5760]{1,0:T(8,128)(2,1)} %refs_0_.19), channel_id=1, source_target_pairs={{0,1},{1,0},{2,3},{3,2},{4,5},{5,4},{6,7},{7,6},{8,9},{9,8},{10,11... | collective-permute-start | bytes 8847368 | tf_op jit(solution)/shard_map/ppermute | solution.py:234
  1.4 9.6 %collective-permute-start.1 = (bf16[256,5760]{1,0:T(8,128)(2,1)}, bf16[256,5760]{1,0:T(8,128)(2,1)}, u32[]{:S(2)}, u32[]{:S(2)}) collective-permute-start(bf16[256,5760]{1,0:T(8,128)(2,1)} %refs_1_.19), channel_id=1, source_target_pairs={{0,1},{1,0},{2,3},{3,2},{4,5},{5,4},{6,7},{7,6},{8,9},{9,8},{10,11... | collective-permute-start | bytes 8847368 | tf_op jit(solution)/shard_map/ppermute | solution.py:234
  1.5 24.2 %copy-start.9 = (s32[2,45]{1,0:T(2,128)S(1)}, s32[2,45]{1,0:T(2,128)}, u32[]{:S(2)}) copy-start(s32[2,45]{1,0:T(2,128)} %own_mask.19) | copy-start | bytes 1084
  1.5 28.2 %copy-start.10 = (s32[32]{0:T(128)S(1)}, s32[32]{0:T(128)}, u32[]{:S(2)}) copy-start(s32[32]{0:T(128)} %owner_ref.19) | copy-start | bytes 388
  3.8 15.0 %collective-permute-start.6 = (s16[1168,256]{1,0:T(8,128)(2,1)}, s16[1168,256]{1,0:T(8,128)(2,1)}, u32[]{:S(2)}, u32[]{:S(2)}) collective-permute-start(s16[1168,256]{1,0:T(8,128)(2,1)} %pack.2.refs_2_.refs_4_), channel_id=1, source_target_pairs={{0,4},{1,5},{2,6},{3,7},{4,0},{5,1},{6,2},{7,3},{8,12},{9,13},{10,... | collective-permute-start | bytes 1794056 | tf_op jit(solution)/shard_map/ppermute | solution.py:234
  4.0 15.0 %collective-permute-start.5 = (s16[1168,256]{1,0:T(8,128)(2,1)}, s16[1168,256]{1,0:T(8,128)(2,1)S(1)}, u32[]{:S(2)}, u32[]{:S(2)}) collective-permute-start(s16[1168,256]{1,0:T(8,128)(2,1)} %pack.2.refs_2_.refs_4_), channel_id=1, source_target_pairs={{0,2},{1,3},{2,0},{3,1},{4,6},{5,7},{6,4},{7,5},{8,10},{9,11},{10,... | collective-permute-start | bytes 1794056 | tf_op jit(solution)/shard_map/ppermute | solution.py:234
  10.0 5.0 %copy-start = (bf16[256,5760]{1,0:T(8,128)(2,1)}, bf16[256,5760]{1,0:T(8,128)(2,1)S(1)}, u32[]{:S(2)}) copy-start(bf16[256,5760]{1,0:T(8,128)(2,1)S(1)} %collective-permute-done.refs_0_.refs_2_) | copy-start | bytes 8847364
  10.9 1.1 copy-start.5
  12.1 17.6 %copy-start.6 = (s16[1168,256]{1,0:T(8,128)(2,1)S(1)}, s16[1168,256]{1,0:T(8,128)(2,1)}, u32[]{:S(2)}) copy-start(s16[1168,256]{1,0:T(8,128)(2,1)} %pack.2.refs_2_.refs_4_) | copy-start | bytes 1794052
  15.0 6.9 %collective-permute-start.4 = (s16[1168,256]{1,0:T(8,128)(2,1)S(1)}, s16[1168,256]{1,0:T(8,128)(2,1)}, u32[]{:S(2)}, u32[]{:S(2)}) collective-permute-start(s16[1168,256]{1,0:T(8,128)(2,1)S(1)} %get-tuple-element.28), channel_id=1, source_target_pairs={{0,1},{1,0},{2,3},{3,2},{4,5},{5,4},{6,7},{7,6},{8,9},{9,8},{10,11... | collective-permute-start | bytes 1794056 | tf_op jit(solution)/shard_map/ppermute | solution.py:234
  15.5 6.5 %collective-permute-start.7 = (s16[1168,256]{1,0:T(8,128)(2,1)S(1)}, s16[1168,256]{1,0:T(8,128)(2,1)S(1)}, u32[]{:S(2)}, u32[]{:S(2)}) collective-permute-start(s16[1168,256]{1,0:T(8,128)(2,1)S(1)} %get-tuple-element.29), channel_id=1, source_target_pairs={{0,1},{1,0},{2,3},{3,2},{4,5},{5,4},{6,7},{7,6},{8,9},{9,8},{10,11... | collective-permute-start | bytes 1794056 | tf_op jit(solution)/shard_map/ppermute | solution.py:234
  15.6 22.8 %collective-permute-start.9 = (s16[1168,256]{1,0:T(8,128)(2,1)}, s16[1168,256]{1,0:T(8,128)(2,1)S(1)}, u32[]{:S(2)}, u32[]{:S(2)}) collective-permute-start(s16[1168,256]{1,0:T(8,128)(2,1)} %get-tuple-element.31.refs_5_), channel_id=1, source_target_pairs={{0,2},{1,3},{2,0},{3,1},{4,6},{5,7},{6,4},{7,5},{8,10},{9,11},{10,... | collective-permute-start | bytes 1794056 | tf_op jit(solution)/shard_map/ppermute | solution.py:234
  18.8 19.6 %collective-permute-start.10 = (s16[1168,256]{1,0:T(8,128)(2,1)}, s16[1168,256]{1,0:T(8,128)(2,1)}, u32[]{:S(2)}, u32[]{:S(2)}) collective-permute-start(s16[1168,256]{1,0:T(8,128)(2,1)} %get-tuple-element.31.refs_5_), channel_id=1, source_target_pairs={{0,4},{1,5},{2,6},{3,7},{4,0},{5,1},{6,2},{7,3},{8,12},{9,13},{10,... | collective-permute-start | bytes 1794056 | tf_op jit(solution)/shard_map/ppermute | solution.py:234
  19.0 0.8 copy-start.7
  19.8 21.5 %collective-permute-start.12 = (s16[1168,256]{1,0:T(8,128)(2,1)}, s16[1168,256]{1,0:T(8,128)(2,1)S(1)}, u32[]{:S(2)}, u32[]{:S(2)}) collective-permute-start(s16[1168,256]{1,0:T(8,128)(2,1)} %collective-permute-done.6.refs_4_), channel_id=1, source_target_pairs={{0,8},{1,9},{2,10},{3,11},{8,16},{9,17},{10,18},{11,19},{12,4},{13... | collective-permute-start | bytes 1794056 | tf_op jit(solution)/shard_map/ppermute | solution.py:234
  21.9 22.3 %collective-permute-start.8 = (s16[1168,256]{1,0:T(8,128)(2,1)}, s16[1168,256]{1,0:T(8,128)(2,1)S(1)}, u32[]{:S(2)}, u32[]{:S(2)}) collective-permute-start(s16[1168,256]{1,0:T(8,128)(2,1)} %collective-permute-done.4.refs_4_), channel_id=1, source_target_pairs={{0,2},{1,3},{2,0},{3,1},{4,6},{5,7},{6,4},{7,5},{8,10},{9,11},{10,... | collective-permute-start | bytes 1794056 | tf_op jit(solution)/shard_map/ppermute | solution.py:234
  22.3 3.4 %collective-permute-start.2 = (s32[1,5]{1,0:T(1,128)}, s32[1,5]{1,0:T(1,128)S(1)}, u32[]{:S(2)}, u32[]{:S(2)}) collective-permute-start(s32[1,5]{1,0:T(1,128)} %own_ids.19), channel_id=1, source_target_pairs={{0,1},{1,0},{2,3},{3,2},{4,5},{5,4},{6,7},{7,6},{8,9},{9,8},{10,11... | collective-permute-start | bytes 68 | tf_op jit(solution)/shard_map/ppermute | solution.py:234
  25.7 1.1 collective-permute-start.3
  26.0 20.2 %copy-start.12 = (s32[1,5]{1,0:T(1,128)S(1)}, s32[1,5]{1,0:T(1,128)}, u32[]{:S(2)}) copy-start(s32[1,5]{1,0:T(1,128)} %own_ids.19) | copy-start | bytes 64
  26.8 39.8 %collective-permute-start.14 = (s16[1168,256]{1,0:T(8,128)(2,1)}, s16[1168,256]{1,0:T(8,128)(2,1)S(1)}, u32[]{:S(2)}, u32[]{:S(2)}) collective-permute-start(s16[1168,256]{1,0:T(8,128)(2,1)} %collective-permute-done.4.refs_4_), channel_id=1, source_target_pairs={{0,4},{1,5},{2,6},{3,7},{4,0},{5,1},{6,2},{7,3},{8,12},{9,13},{10,... | collective-permute-start | bytes 1794056 | tf_op jit(solution)/shard_map/ppermute | solution.py:234
  29.6 1.8 %copy-start.1 = (bf16[256,5760]{1,0:T(8,128)(2,1)S(1)}, bf16[256,5760]{1,0:T(8,128)(2,1)}, u32[]{:S(2)}) copy-start(bf16[256,5760]{1,0:T(8,128)(2,1)} %refs_0_.19) | copy-start | bytes 8847364
  31.5 1.8 %copy-start.3 = (bf16[256,5760]{1,0:T(8,128)(2,1)S(1)}, bf16[256,5760]{1,0:T(8,128)(2,1)}, u32[]{:S(2)}) copy-start(bf16[256,5760]{1,0:T(8,128)(2,1)} %refs_1_.19) | copy-start | bytes 8847364
  33.3 0.7 copy-start.11
  34.0 12.2 %copy-start.2 = (bf16[256,5760]{1,0:T(8,128)(2,1)S(1)}, bf16[256,5760]{1,0:T(8,128)(2,1)}, u32[]{:S(2)}) copy-start(bf16[256,5760]{1,0:T(8,128)(2,1)} %refs_0_.19) | copy-start | bytes 8847364
  34.0 12.2 %copy-start.4 = (bf16[256,5760]{1,0:T(8,128)(2,1)S(1)}, bf16[256,5760]{1,0:T(8,128)(2,1)}, u32[]{:S(2)}) copy-start(bf16[256,5760]{1,0:T(8,128)(2,1)} %refs_1_.19) | copy-start | bytes 8847364
  38.4 18.6 %collective-permute-start.11 = (s16[1168,256]{1,0:T(8,128)(2,1)S(1)}, s16[1168,256]{1,0:T(8,128)(2,1)S(1)}, u32[]{:S(2)}, u32[]{:S(2)}) collective-permute-start(s16[1168,256]{1,0:T(8,128)(2,1)S(1)} %get-tuple-element.33.refs_5_), channel_id=1, source_target_pairs={{0,2},{1,3},{2,0},{3,1},{4,6},{5,7},{6,4},{7,5},{8,10},{9,11},{10,... | collective-permute-start | bytes 1794056 | tf_op jit(solution)/shard_map/ppermute | solution.py:234
  39.7 28.9 %collective-permute-start.22 = (s16[1168,256]{1,0:T(8,128)(2,1)S(1)}, s16[1168,256]{1,0:T(8,128)(2,1)S(1)}, u32[]{:S(2)}, u32[]{:S(2)}) collective-permute-start(s16[1168,256]{1,0:T(8,128)(2,1)S(1)} %get-tuple-element.33.refs_5_), channel_id=1, source_target_pairs={{0,4},{1,5},{2,6},{3,7},{4,0},{5,1},{6,2},{7,3},{8,12},{9,13},{10,... | collective-permute-start | bytes 1794056 | tf_op jit(solution)/shard_map/ppermute | solution.py:234
  41.4 21.1 %collective-permute-start.13 = (s16[1168,256]{1,0:T(8,128)(2,1)}, s16[1168,256]{1,0:T(8,128)(2,1)S(1)}, u32[]{:S(2)}, u32[]{:S(2)}) collective-permute-start(s16[1168,256]{1,0:T(8,128)(2,1)} %collective-permute-done.10.refs_5_), channel_id=1, source_target_pairs={{0,8},{1,9},{2,10},{3,11},{8,16},{9,17},{10,18},{11,19},{12,4},{13... | collective-permute-start | bytes 1794056 | tf_op jit(solution)/shard_map/ppermute | solution.py:234
  44.2 29.3 %collective-permute-start.20 = (s16[1168,256]{1,0:T(8,128)(2,1)S(1)}, s16[1168,256]{1,0:T(8,128)(2,1)S(1)}, u32[]{:S(2)}, u32[]{:S(2)}) collective-permute-start(s16[1168,256]{1,0:T(8,128)(2,1)S(1)} %collective-permute-done.9.refs_5_), channel_id=1, source_target_pairs={{4,12},{5,13},{10,2},{11,3},{12,20},{13,21},{18,10},{19,11},{20,28... | collective-permute-start | bytes 1794056 | tf_op jit(solution)/shard_map/ppermute | solution.py:234
  46.2 5.7 %copy-start.8 = (s16[1168,256]{1,0:T(8,128)(2,1)S(1)}, s16[1168,256]{1,0:T(8,128)(2,1)}, u32[]{:S(2)}) copy-start(s16[1168,256]{1,0:T(8,128)(2,1)} %copy-done.7) | copy-start | bytes 1794052
  57.0 17.8 %collective-permute-start.17 = (s16[1168,256]{1,0:T(8,128)(2,1)S(1)}, s16[1168,256]{1,0:T(8,128)(2,1)S(1)}, u32[]{:S(2)}, u32[]{:S(2)}) collective-permute-start(s16[1168,256]{1,0:T(8,128)(2,1)S(1)} %collective-permute-done.11.refs_5_), channel_id=1, source_target_pairs={{4,12},{5,13},{10,2},{11,3},{12,20},{13,21},{18,10},{19,11},{20,28... | collective-permute-start | bytes 1794056 | tf_op jit(solution)/shard_map/ppermute | solution.py:234
  62.5 36.2 %collective-permute-start.19 = (s16[1168,256]{1,0:T(8,128)(2,1)S(1)}, s16[1168,256]{1,0:T(8,128)(2,1)S(1)}, u32[]{:S(2)}, u32[]{:S(2)}) collective-permute-start(s16[1168,256]{1,0:T(8,128)(2,1)S(1)} %get-tuple-element.39), channel_id=1, source_target_pairs={{0,2},{1,3},{2,0},{3,1},{4,6},{5,7},{6,4},{7,5},{8,10},{9,11},{10,... | collective-permute-start | bytes 1794056 | tf_op jit(solution)/shard_map/ppermute | solution.py:234
  66.6 15.6 %collective-permute-start.15 = (s16[1168,256]{1,0:T(8,128)(2,1)S(1)}, s16[1168,256]{1,0:T(8,128)(2,1)S(1)}, u32[]{:S(2)}, u32[]{:S(2)}) collective-permute-start(s16[1168,256]{1,0:T(8,128)(2,1)S(1)} %collective-permute-done.14.refs_4_), channel_id=1, source_target_pairs={{0,8},{1,9},{2,10},{3,11},{8,16},{9,17},{10,18},{11,19},{12,4},{13... | collective-permute-start | bytes 1794056 | tf_op jit(solution)/shard_map/ppermute | solution.py:234
  68.6 26.5 %collective-permute-start.23 = (s16[1168,256]{1,0:T(8,128)(2,1)S(1)}, s16[1168,256]{1,0:T(8,128)(2,1)S(1)}, u32[]{:S(2)}, u32[]{:S(2)}) collective-permute-start(s16[1168,256]{1,0:T(8,128)(2,1)S(1)} %collective-permute-done.22.refs_5_), channel_id=1, source_target_pairs={{0,8},{1,9},{2,10},{3,11},{8,16},{9,17},{10,18},{11,19},{12,4},{13... | collective-permute-start | bytes 1794056 | tf_op jit(solution)/shard_map/ppermute | solution.py:234
  73.6 25.0 %collective-permute-start.21 = (s16[1168,256]{1,0:T(8,128)(2,1)S(1)}, s16[1168,256]{1,0:T(8,128)(2,1)S(1)}, u32[]{:S(2)}, u32[]{:S(2)}) collective-permute-start(s16[1168,256]{1,0:T(8,128)(2,1)S(1)} %broadcast_select_fusion), channel_id=1, source_target_pairs={{0,4},{1,5},{2,6},{3,7},{4,0},{5,1},{6,2},{7,3},{8,12},{9,13},{10,... | collective-permute-start | bytes 1794056 | tf_op jit(solution)/shard_map/ppermute | solution.py:234
  75.0 28.6 %collective-permute-start.18 = (s16[1168,256]{1,0:T(8,128)(2,1)S(1)}, s16[1168,256]{1,0:T(8,128)(2,1)S(1)}, u32[]{:S(2)}, u32[]{:S(2)}) collective-permute-start(s16[1168,256]{1,0:T(8,128)(2,1)S(1)} %broadcast_select_fusion.1), channel_id=1, source_target_pairs={{0,4},{1,5},{2,6},{3,7},{4,0},{5,1},{6,2},{7,3},{8,12},{9,13},{10,... | collective-permute-start | bytes 1794056 | tf_op jit(solution)/shard_map/ppermute | solution.py:234
  85.4 18.2 %collective-permute-start.16 = (s16[1168,256]{1,0:T(8,128)(2,1)S(1)}, s16[1168,256]{1,0:T(8,128)(2,1)S(1)}, u32[]{:S(2)}, u32[]{:S(2)}) collective-permute-start(s16[1168,256]{1,0:T(8,128)(2,1)S(1)} %get-tuple-element.37), channel_id=1, source_target_pairs={{0,2},{1,3},{2,0},{3,1},{4,6},{5,7},{6,4},{7,5},{8,10},{9,11},{10,... | collective-permute-start | bytes 1794056 | tf_op jit(solution)/shard_map/ppermute | solution.py:234
  103.6 11.5 %copy-start.13 = (s32[256]{0:T(256)S(1)}, s32[256]{0:T(256)}, u32[]{:S(2)}) copy-start(s32[256]{0:T(256)} %param.13) | copy-start | bytes 3076
  107.3 5.2 %collective-permute-start.24 = (bf16[2,2,32,512]{3,2,1,0:T(8,128)(2,1)S(1)}, bf16[2,2,32,512]{3,2,1,0:T(8,128)(2,1)S(1)}, u32[]{:S(2)}, u32[]{:S(2)}) collective-permute-start(bf16[2,2,32,512]{3,2,1,0:T(8,128)(2,1)S(1)} %get-tuple-element.43), channel_id=1, source_target_pairs={{0,1},{1,0},{2,3},{3,2},{4,5},{5,4},{6,7},{7,6},{8,9},{9,8},{10,11... | collective-permute-start | bytes 393224 | tf_op jit(solution)/shard_map/ppermute | solution.py:234
  109.0 5.1 %collective-permute-start.25 = (bf16[2,2,32,512]{3,2,1,0:T(8,128)(2,1)S(1)}, bf16[2,2,32,512]{3,2,1,0:T(8,128)(2,1)S(1)}, u32[]{:S(2)}, u32[]{:S(2)}) collective-permute-start(bf16[2,2,32,512]{3,2,1,0:T(8,128)(2,1)S(1)} %get-tuple-element.44), channel_id=1, source_target_pairs={{0,2},{1,3},{2,0},{3,1},{4,6},{5,7},{6,4},{7,5},{8,10},{9,11},{10,... | collective-permute-start | bytes 393224 | tf_op jit(solution)/shard_map/ppermute | solution.py:234
  109.0 8.8 %collective-permute-start.26 = (bf16[2,2,32,512]{3,2,1,0:T(8,128)(2,1)S(1)}, bf16[2,2,32,512]{3,2,1,0:T(8,128)(2,1)S(1)}, u32[]{:S(2)}, u32[]{:S(2)}) collective-permute-start(bf16[2,2,32,512]{3,2,1,0:T(8,128)(2,1)S(1)} %get-tuple-element.45), channel_id=1, source_target_pairs={{0,3},{1,2},{2,1},{3,0},{4,7},{5,6},{6,5},{7,4},{8,11},{9,10},{10,... | collective-permute-start | bytes 393224 | tf_op jit(solution)/shard_map/ppermute | solution.py:234
  110.7 7.1 %collective-permute-start.27 = (bf16[2,2,32,512]{3,2,1,0:T(8,128)(2,1)S(1)}, bf16[2,2,32,512]{3,2,1,0:T(8,128)(2,1)S(1)}, u32[]{:S(2)}, u32[]{:S(2)}) collective-permute-start(bf16[2,2,32,512]{3,2,1,0:T(8,128)(2,1)S(1)} %get-tuple-element.46), channel_id=1, source_target_pairs={{0,4},{1,5},{2,6},{3,7},{4,0},{5,1},{6,2},{7,3},{8,12},{9,13},{10,... | collective-permute-start | bytes 393224 | tf_op jit(solution)/shard_map/ppermute | solution.py:234
  110.7 13.6 %collective-permute-start.28 = (bf16[2,2,32,512]{3,2,1,0:T(8,128)(2,1)S(1)}, bf16[2,2,32,512]{3,2,1,0:T(8,128)(2,1)S(1)}, u32[]{:S(2)}, u32[]{:S(2)}) collective-permute-start(bf16[2,2,32,512]{3,2,1,0:T(8,128)(2,1)S(1)} %get-tuple-element.47), channel_id=1, source_target_pairs={{0,5},{1,4},{2,7},{3,6},{4,1},{5,0},{6,3},{7,2},{8,13},{9,12},{10,... | collective-permute-start | bytes 393224 | tf_op jit(solution)/shard_map/ppermute | solution.py:234
  112.5 11.8 %collective-permute-start.29 = (bf16[2,2,32,512]{3,2,1,0:T(8,128)(2,1)S(1)}, bf16[2,2,32,512]{3,2,1,0:T(8,128)(2,1)S(1)}, u32[]{:S(2)}, u32[]{:S(2)}) collective-permute-start(bf16[2,2,32,512]{3,2,1,0:T(8,128)(2,1)S(1)} %get-tuple-element.48), channel_id=1, source_target_pairs={{0,6},{1,7},{2,4},{3,5},{4,2},{5,3},{6,0},{7,1},{8,14},{9,15},{10,... | collective-permute-start | bytes 393224 | tf_op jit(solution)/shard_map/ppermute | solution.py:234
  114.0 10.3 %collective-permute-start.30 = (bf16[2,2,32,512]{3,2,1,0:T(8,128)(2,1)S(1)}, bf16[2,2,32,512]{3,2,1,0:T(8,128)(2,1)S(1)}, u32[]{:S(2)}, u32[]{:S(2)}) collective-permute-start(bf16[2,2,32,512]{3,2,1,0:T(8,128)(2,1)S(1)} %get-tuple-element.49), channel_id=1, source_target_pairs={{0,7},{1,6},{2,5},{3,4},{4,3},{5,2},{6,1},{7,0},{8,15},{9,14},{10,... | collective-permute-start | bytes 393224 | tf_op jit(solution)/shard_map/ppermute | solution.py:234

commit v4 on v3

--- a/solution.py
+++ b/solution.py
@@ -325,7 +325,9 @@
         return out[1:]
 
     parts = (routed if devices == 8 else direct)(own, count, index, add)
-    parts = [permute(x, count, lambda i, by=by: i ^ by) if by else x for by, x in enumerate(parts)]
+    parts = list(parts)
+    for by in sorted(range(1, devices), key=lambda by: (-bin(by >> 1).count("1"), -by)):
+        parts[by] = permute(parts[by], count, lambda i, by=by: i ^ by)
     return order_rows(place, tree_order, parts)
 
 

time: 126 us -> 127 us (level); the launches traced: 126 us -> 125 us
  waiting for transfers between devices: 42.9 us -> 38.6 us
  starting transfers between devices: 32.8 us -> 35.8 us
    ppermute x31, waiting for transfers between devices: 42.9 us -> 38.6 us  [permute(): lax.ppermute(x, AXES, [(i, t) for i, t in pairs if t is not None and 0 <=...]
    ppermute x31, starting transfers between devices: 32.8 us -> 35.8 us  [permute(): lax.ppermute(x, AXES, [(i, t) for i, t in pairs if t is not None and 0 <=...]
  transfers between devices with their start and end apart: 31 -> 31, of which waited for: 12 -> 13; matrix products, arithmetic and copies ran while one was open for 1% -> 1% of each run, Pallas kernels for 29% -> 29%
where the time goes in v4:
time: 127 us; the launch traced here: 125 us
  Pallas kernels  41 us (32%)
  waiting for transfers between devices  38.6 us (30%)
  starting transfers between devices  35.8 us (28%)
  local copies, waits for them, and re-layouts  6.43 us (5%)
  other arithmetic  1.72 us (1%)
    ppermute x31, waiting for transfers between devices, permute(): lax.ppermute(x, AXES, [(i, t) for i, t in pairs if t is not None and 0 <=...  38.6 us
    ppermute x31, starting transfers between devices, permute(): lax.ppermute(x, AXES, [(i, t) for i, t in pairs if t is not None and 0 <=...  35.8 us
    pallas_call x10, Pallas kernels, add_slot(): pl.pallas_call(functools.partial(slot_kernel, away, other, len(out_shape)...  34.4 us
    unnamed x28, local copies, waits for them, and re-layouts  6.3 us
    pallas_call x2, Pallas kernels, pack(): pl.pallas_call(functools.partial(pack_kernel, pieces), grid_spec=pltpu.Pr...  5.23 us
  transfers between devices with their start and end apart: 31, of which 13 were waited for; matrix products, arithmetic and copies ran while one was open for 1% of the time, Pallas kernels for 29%

profile of v4, /device:TPU:15, one launch (start us, length us, event | category | flops | bytes accessed | tf_op | source)
XLA Modules:
  0.0 124.5 jit_solution(3262879533256970190)
XLA Ops:
  0.6 0.7 collective-permute-start
  1.5 2.3 %pack.2.refs_2_.refs_4_ = s16[1168,256]{1,0:T(8,128)(2,1)} custom-call(s32[1]{0:T(128)} %bitcast.place_ref, f32[1152,1024]{1,0:T(8,128)} %source.3), custom_call_target="tpu_custom_call" | custom-call | flops 4718592 | bytes 1769472 | tf_op jit(solution)/shard_map/pack/pallas_call | solution.py:55
  4.3 5.7 %collective-permute-done.refs_0_.refs_2_ = bf16[256,5760]{1,0:T(8,128)(2,1)S(1)} collective-permute-done((bf16[256,5760]{1,0:T(8,128)(2,1)}, bf16[256,5760]{1,0:T(8,128)(2,1)S(1)}, u32[]{:S(2)}, u32[]{:S(2)}) %collective-permute-start) | collective-permute-done | bytes 2949152 | tf_op jit(solution)/shard_map/ppermute | solution.py:234
  10.0 0.9 collective-permute-done.1.refs_1_.refs_3_
  10.9 1.1 copy-done.5
  12.1 2.9 %pack.3 = (s16[1168,256]{1,0:T(8,128)(2,1)}, s16[1168,256]{1,0:T(8,128)(2,1)S(1)}, s16[1168,256]{1,0:T(8,128)(2,1)S(1)}) custom-call(s32[1]{0:T(128)} %bitcast.place_ref, f32[1152,1024]{1,0:T(8,128)} %source.3, bf16[256,5760]{1,0:T(8,128)(2,1)S(1)} %collective-permute-done.refs_0_.refs_2_, bf16[256,5760]{1,0:T(8,128)(2,1)} %collective-permute-done.1.refs_1_.refs_3_, ...), custom_call_target="tpu_custom_call" | custom-call | flops 14155776 | bytes 5308416 | tf_op jit(solution)/shard_map/pack/pallas_call | solution.py:55
  15.9 2.9 %collective-permute-done.6.refs_4_ = s16[1168,256]{1,0:T(8,128)(2,1)} collective-permute-done((s16[1168,256]{1,0:T(8,128)(2,1)}, s16[1168,256]{1,0:T(8,128)(2,1)}, u32[]{:S(2)}, u32[]{:S(2)}) %collective-permute-start.6) | collective-permute-done | bytes 598048 | tf_op jit(solution)/shard_map/ppermute | solution.py:234
  19.0 0.8 copy-done.7
  19.8 2.1 %collective-permute-start.12 = (s16[1168,256]{1,0:T(8,128)(2,1)}, s16[1168,256]{1,0:T(8,128)(2,1)S(1)}, u32[]{:S(2)}, u32[]{:S(2)}) collective-permute-start(s16[1168,256]{1,0:T(8,128)(2,1)} %collective-permute-done.6.refs_4_), channel_id=1, source_target_pairs={{0,8},{1,9},{2,10},{3,11},{8,16},{9,17},{10,18},{11,19},{12,4},{13... | collective-permute-start | bytes 1794056 | tf_op jit(solution)/shard_map/ppermute | solution.py:234
  22.3 2.4 %collective-permute-start.2 = (s32[1,5]{1,0:T(1,128)}, s32[1,5]{1,0:T(1,128)S(1)}, u32[]{:S(2)}, u32[]{:S(2)}) collective-permute-start(s32[1,5]{1,0:T(1,128)} %own_ids.19), channel_id=1, source_target_pairs={{0,1},{1,0},{2,3},{3,2},{4,5},{5,4},{6,7},{7,6},{8,9},{9,8},{10,11... | collective-permute-start | bytes 68 | tf_op jit(solution)/shard_map/ppermute | solution.py:234
  24.7 1.0 collective-permute-done.2.other_ids
  26.0 0.8 collective-permute-done.3.other_mask
  26.8 2.8 %collective-permute-start.14 = (s16[1168,256]{1,0:T(8,128)(2,1)}, s16[1168,256]{1,0:T(8,128)(2,1)S(1)}, u32[]{:S(2)}, u32[]{:S(2)}) collective-permute-start(s16[1168,256]{1,0:T(8,128)(2,1)} %collective-permute-done.4.refs_4_), channel_id=1, source_target_pairs={{0,4},{1,5},{2,6},{3,7},{4,0},{5,1},{6,2},{7,3},{8,12},{9,13},{10,... | collective-permute-start | bytes 1794056 | tf_op jit(solution)/shard_map/ppermute | solution.py:234
  29.6 1.8 %copy-done.1 = bf16[256,5760]{1,0:T(8,128)(2,1)S(1)} copy-done((bf16[256,5760]{1,0:T(8,128)(2,1)S(1)}, bf16[256,5760]{1,0:T(8,128)(2,1)}, u32[]{:S(2)}) %copy-start.1) | copy-done | bytes 2949144
  31.5 1.8 %copy-done.3 = bf16[256,5760]{1,0:T(8,128)(2,1)S(1)} copy-done((bf16[256,5760]{1,0:T(8,128)(2,1)S(1)}, bf16[256,5760]{1,0:T(8,128)(2,1)}, u32[]{:S(2)}) %copy-start.3) | copy-done | bytes 2949144
  33.3 0.7 copy-done.11
  34.0 4.4 %slot.10 = (f32[2,512,512]{2,1,0:T(8,128)S(1)}, s16[1168,256]{1,0:T(8,128)(2,1)S(1)}) custom-call(s32[1]{0:T(128)} %bitcast.place_ref, s32[32]{0:T(128)S(1)} %copy-done.10, s32[1,5]{1,0:T(1,128)S(1)} %copy-done.11, s32[1,5]{1,0:T(1,128)S(1)} %collective-permute-done.2.other_ids, s32[2,45]{1,0:T(2,128)S(1)} %copy-done.9, ...), custom_call_target="tpu_custom_call", output_to_operand_aliasing={{1}: (12, {})} | custom-call | flops 603979776 | bytes 294912 | tf_op jit(solution)/shard_map/slot/pallas_call | solution.py:170
  38.4 1.3 %collective-permute-start.11 = (s16[1168,256]{1,0:T(8,128)(2,1)S(1)}, s16[1168,256]{1,0:T(8,128)(2,1)S(1)}, u32[]{:S(2)}, u32[]{:S(2)}) collective-permute-start(s16[1168,256]{1,0:T(8,128)(2,1)S(1)} %get-tuple-element.33.refs_5_), channel_id=1, source_target_pairs={{0,2},{1,3},{2,0},{3,1},{4,6},{5,7},{6,4},{7,5},{8,10},{9,11},{10,... | collective-permute-start | bytes 1794056 | tf_op jit(solution)/shard_map/ppermute | solution.py:234
  39.6 1.7 %collective-permute-start.22 = (s16[1168,256]{1,0:T(8,128)(2,1)S(1)}, s16[1168,256]{1,0:T(8,128)(2,1)S(1)}, u32[]{:S(2)}, u32[]{:S(2)}) collective-permute-start(s16[1168,256]{1,0:T(8,128)(2,1)S(1)} %get-tuple-element.33.refs_5_), channel_id=1, source_target_pairs={{0,4},{1,5},{2,6},{3,7},{4,0},{5,1},{6,2},{7,3},{8,12},{9,13},{10,... | collective-permute-start | bytes 1794056 | tf_op jit(solution)/shard_map/ppermute | solution.py:234
  41.4 2.1 %collective-permute-start.13 = (s16[1168,256]{1,0:T(8,128)(2,1)}, s16[1168,256]{1,0:T(8,128)(2,1)S(1)}, u32[]{:S(2)}, u32[]{:S(2)}) collective-permute-start(s16[1168,256]{1,0:T(8,128)(2,1)} %collective-permute-done.10.refs_5_), channel_id=1, source_target_pairs={{0,8},{1,9},{2,10},{3,11},{8,16},{9,17},{10,18},{11,19},{12,4},{13... | collective-permute-start | bytes 1794056 | tf_op jit(solution)/shard_map/ppermute | solution.py:234
  43.5 0.7 collective-permute-done.8.refs_4_
  44.2 0.7 collective-permute-start.20
  44.9 1.3 %broadcast_select_fusion.3.refs_7_ = s16[1168,256]{1,0:T(8,128)(2,1)S(1)} fusion(s16[1168,256]{1,0:T(8,128)(2,1)} %collective-permute-done.6.refs_4_, s16[1168,256]{1,0:T(8,128)(2,1)S(1)} %collective-permute-done.12.refs_4_, pred[]{:T(512)S(6)} %eq.6), kind=kLoop, calls=%fused_computation.3 | loop fusion | flops 299008 | bytes 1794049 | tf_op jit(solution)/shard_map/jit(_where)/select_n | solution.py:265
  46.2 4.5 %slot.11.refs_6_ = f32[2,512,512]{2,1,0:T(8,128)S(1)} custom-call(s32[1]{0:T(128)} %bitcast.place_ref, s32[32]{0:T(128)S(1)} %copy-done.10, s32[1,5]{1,0:T(1,128)S(1)} %copy-done.12, s32[1,5]{1,0:T(1,128)S(1)} %collective-permute-done.2.other_ids, s32[2,45]{1,0:T(2,128)S(1)} %copy-done.9, ...), custom_call_target="tpu_custom_call", output_to_operand_aliasing={{}: (12, {})} | custom-call | flops 603979776 | bytes 294912 | tf_op jit(solution)/shard_map/slot/pallas_call | solution.py:170
  50.7 4.7 %slot.12.refs_6_ = f32[2,512,512]{2,1,0:T(8,128)S(1)} custom-call(s32[1]{0:T(128)} %bitcast.place_ref, s32[32]{0:T(128)S(1)} %copy-done.10, s32[1,5]{1,0:T(1,128)S(1)} %copy-done.12, s32[1,5]{1,0:T(1,128)S(1)} %collective-permute-done.2.other_ids, s32[2,45]{1,0:T(2,128)S(1)} %copy-done.9, ...), custom_call_target="tpu_custom_call", output_to_operand_aliasing={{}: (12, {})} | custom-call | flops 603979776 | bytes 294912 | tf_op jit(solution)/shard_map/slot/pallas_call | solution.py:170
  55.4 1.6 %collective-permute-done.11.refs_5_ = s16[1168,256]{1,0:T(8,128)(2,1)S(1)} collective-permute-done((s16[1168,256]{1,0:T(8,128)(2,1)S(1)}, s16[1168,256]{1,0:T(8,128)(2,1)S(1)}, u32[]{:S(2)}, u32[]{:S(2)}) %collective-permute-start.11) | collective-permute-done | bytes 598048 | tf_op jit(solution)/shard_map/ppermute | solution.py:234
  57.0 0.7 collective-permute-start.17
  57.7 4.4 %slot.13 = (f32[2,512,512]{2,1,0:T(8,128)S(1)}, s16[1168,256]{1,0:T(8,128)(2,1)S(1)}) custom-call(s32[1]{0:T(128)} %bitcast.place_ref, s32[32]{0:T(128)S(1)} %copy-done.10, s32[1,5]{1,0:T(1,128)S(1)} %copy-done.12, s32[1,5]{1,0:T(1,128)S(1)} %collective-permute-done.2.other_ids, ...), custom_call_target="tpu_custom_call", output_to_operand_aliasing={{1}: (13, {}), {0}: (12, {})} | custom-call | flops 603979776 | bytes 294912 | tf_op jit(solution)/shard_map/slot/pallas_call | solution.py:170
  62.1 3.3 %collective-permute-start.19 = (s16[1168,256]{1,0:T(8,128)(2,1)S(1)}, s16[1168,256]{1,0:T(8,128)(2,1)S(1)}, u32[]{:S(2)}, u32[]{:S(2)}) collective-permute-start(s16[1168,256]{1,0:T(8,128)(2,1)S(1)} %get-tuple-element.39), channel_id=1, source_target_pairs={{0,2},{1,3},{2,0},{3,1},{4,6},{5,7},{6,4},{7,5},{8,10},{9,11},{10,... | collective-permute-start | bytes 1794056 | tf_op jit(solution)/shard_map/ppermute | solution.py:234
  65.4 3.1 %collective-permute-start.15 = (s16[1168,256]{1,0:T(8,128)(2,1)S(1)}, s16[1168,256]{1,0:T(8,128)(2,1)S(1)}, u32[]{:S(2)}, u32[]{:S(2)}) collective-permute-start(s16[1168,256]{1,0:T(8,128)(2,1)S(1)} %collective-permute-done.14.refs_4_), channel_id=1, source_target_pairs={{0,8},{1,9},{2,10},{3,11},{8,16},{9,17},{10,18},{11,19},{12,4},{13... | collective-permute-start | bytes 1794056 | tf_op jit(solution)/shard_map/ppermute | solution.py:234
  68.5 1.9 %collective-permute-start.23 = (s16[1168,256]{1,0:T(8,128)(2,1)S(1)}, s16[1168,256]{1,0:T(8,128)(2,1)S(1)}, u32[]{:S(2)}, u32[]{:S(2)}) collective-permute-start(s16[1168,256]{1,0:T(8,128)(2,1)S(1)} %collective-permute-done.22.refs_5_), channel_id=1, source_target_pairs={{0,8},{1,9},{2,10},{3,11},{8,16},{9,17},{10,18},{11,19},{12,4},{13... | collective-permute-start | bytes 1794056 | tf_op jit(solution)/shard_map/ppermute | solution.py:234
  70.5 0.7 slot.14.refs_6_
  71.3 4.9 %collective-permute-start.21 = (s16[1168,256]{1,0:T(8,128)(2,1)S(1)}, s16[1168,256]{1,0:T(8,128)(2,1)S(1)}, u32[]{:S(2)}, u32[]{:S(2)}) collective-permute-start(s16[1168,256]{1,0:T(8,128)(2,1)S(1)} %broadcast_select_fusion), channel_id=1, source_target_pairs={{0,4},{1,5},{2,6},{3,7},{4,0},{5,1},{6,2},{7,3},{8,12},{9,13},{10,... | collective-permute-start | bytes 1794056 | tf_op jit(solution)/shard_map/ppermute | solution.py:234
  76.5 7.4 %collective-permute-done.15.refs_4_ = s16[1168,256]{1,0:T(8,128)(2,1)S(1)} collective-permute-done((s16[1168,256]{1,0:T(8,128)(2,1)S(1)}, s16[1168,256]{1,0:T(8,128)(2,1)S(1)}, u32[]{:S(2)}, u32[]{:S(2)}) %collective-permute-start.15) | collective-permute-done | bytes 598048 | tf_op jit(solution)/shard_map/ppermute | solution.py:234
  84.0 4.7 %slot.15 = (f32[2,512,512]{2,1,0:T(8,128)S(1)}, s16[1168,256]{1,0:T(8,128)(2,1)S(1)}) custom-call(s32[1]{0:T(128)} %bitcast.place_ref, s32[32]{0:T(128)S(1)} %copy-done.10, s32[1,5]{1,0:T(1,128)S(1)} %copy-done.12, s32[1,5]{1,0:T(1,128)S(1)} %collective-permute-done.2.other_ids, ...), custom_call_target="tpu_custom_call", output_to_operand_aliasing={{1}: (13, {}), {0}: (12, {})} | custom-call | flops 603979776 | bytes 294912 | tf_op jit(solution)/shard_map/slot/pallas_call | solution.py:170
  88.8 0.7 slot.16.refs_6_
  89.5 6.6 %collective-permute-done.23.refs_5_ = s16[1168,256]{1,0:T(8,128)(2,1)S(1)} collective-permute-done((s16[1168,256]{1,0:T(8,128)(2,1)S(1)}, s16[1168,256]{1,0:T(8,128)(2,1)S(1)}, u32[]{:S(2)}, u32[]{:S(2)}) %collective-permute-start.23) | collective-permute-done | bytes 598048 | tf_op jit(solution)/shard_map/ppermute | solution.py:234
  96.1 3.6 %slot.17.refs_6_ = f32[2,512,512]{2,1,0:T(8,128)S(1)} custom-call(s32[1]{0:T(128)} %bitcast.place_ref, s32[32]{0:T(128)S(1)} %copy-done.10, s32[1,5]{1,0:T(1,128)S(1)} %copy-done.12, s32[1,5]{1,0:T(1,128)S(1)} %collective-permute-done.2.other_ids, s32[2,45]{1,0:T(2,128)S(1)} %copy-done.9, ...), custom_call_target="tpu_custom_call", output_to_operand_aliasing={{}: (12, {})} | custom-call | flops 603979776 | bytes 294912 | tf_op jit(solution)/shard_map/slot/pallas_call | solution.py:170
  99.7 3.2 %slot.18.refs_6_ = f32[2,512,512]{2,1,0:T(8,128)S(1)} custom-call(s32[1]{0:T(128)} %bitcast.place_ref, s32[32]{0:T(128)S(1)} %copy-done.10, s32[1,5]{1,0:T(1,128)S(1)} %copy-done.12, s32[1,5]{1,0:T(1,128)S(1)} %collective-permute-done.2.other_ids, s32[2,45]{1,0:T(2,128)S(1)} %copy-done.9, ...), custom_call_target="tpu_custom_call", output_to_operand_aliasing={{}: (12, {})} | custom-call | flops 603979776 | bytes 294912 | tf_op jit(solution)/shard_map/slot/pallas_call | solution.py:170
  102.9 0.7 collective-permute-done.16.refs_4_
  103.7 3.6 %slot.19 = (bf16[2,2,32,512]{3,2,1,0:T(8,128)(2,1)S(1)}, bf16[2,2,32,512]{3,2,1,0:T(8,128)(2,1)S(1)}, bf16[2,2,32,512]{3,2,1,0:T(8,128)(2,1)S(1)}, bf16[2,2,32,5...) custom-call(s32[1]{0:T(128)} %bitcast.place_ref, ...), custom_call_target="tpu_custom_call" | custom-call | flops 603979776 | bytes 294912 | tf_op jit(solution)/shard_map/slot/pallas_call | solution.py:170
  107.8 1.7 %collective-permute-start.26 = (bf16[2,2,32,512]{3,2,1,0:T(8,128)(2,1)S(1)}, bf16[2,2,32,512]{3,2,1,0:T(8,128)(2,1)S(1)}, u32[]{:S(2)}, u32[]{:S(2)}) collective-permute-start(bf16[2,2,32,512]{3,2,1,0:T(8,128)(2,1)S(1)} %get-tuple-element.45), channel_id=1, source_target_pairs={{0,3},{1,2},{2,1},{3,0},{4,7},{5,6},{6,5},{7,4},{8,11},{9,10},{10,... | collective-permute-start | bytes 393224 | tf_op jit(solution)/shard_map/ppermute | solution.py:234
  110.1 1.2 collective-permute-start.28
  111.6 1.3 %collective-permute-done.25.refs_2_ = bf16[2,2,32,512]{3,2,1,0:T(8,128)(2,1)S(1)} collective-permute-done((bf16[2,2,32,512]{3,2,1,0:T(8,128)(2,1)S(1)}, bf16[2,2,32,512]{3,2,1,0:T(8,128)(2,1)S(1)}, u32[]{:S(2)}, u32[]{:S(2)}) %collective-permute-start.25) | collective-permute-done | bytes 131104 | tf_op jit(solution)/shard_map/ppermute | solution.py:234
  112.9 1.2 collective-permute-start.30
  114.3 2.3 %collective-permute-done.26.refs_3_ = bf16[2,2,32,512]{3,2,1,0:T(8,128)(2,1)S(1)} collective-permute-done((bf16[2,2,32,512]{3,2,1,0:T(8,128)(2,1)S(1)}, bf16[2,2,32,512]{3,2,1,0:T(8,128)(2,1)S(1)}, u32[]{:S(2)}, u32[]{:S(2)}) %collective-permute-start.26) | collective-permute-done | bytes 131104 | tf_op jit(solution)/shard_map/ppermute | solution.py:234
  116.6 6.6 %collective-permute-done.28.refs_5_ = bf16[2,2,32,512]{3,2,1,0:T(8,128)(2,1)S(1)} collective-permute-done((bf16[2,2,32,512]{3,2,1,0:T(8,128)(2,1)S(1)}, bf16[2,2,32,512]{3,2,1,0:T(8,128)(2,1)S(1)}, u32[]{:S(2)}, u32[]{:S(2)}) %collective-permute-start.28) | collective-permute-done | bytes 131104 | tf_op jit(solution)/shard_map/ppermute | solution.py:234
  123.2 1.4 %order.1 = (bf16[256,1024]{1,0:T(8,128)(2,1)}, bf16[256,1024]{1,0:T(8,128)(2,1)}) custom-call(s32[1]{0:T(128)} %bitcast.place_ref, s32[256,1]{1,0:T(8,128)S(1)} %copy.20.order_ref, bf16[2,2,32,512]{3,2,1,0:T(8,128)(2,1)S(1)} %get-tuple-element.42.refs_0_, bf16[2,2,32,512]{3,2,1,0:T(8,128)(2,1)S(1)} %collective-permute-done.24.refs_1_, ...), custom_call_target="tpu_custom_call" | custom-call | tf_op jit(solution)/shard_map/order/pallas_call | solution.py:217
  (60 shorter events, 4.7 us)
Async XLA Ops:
  0.6 9.4 %collective-permute-start = (bf16[256,5760]{1,0:T(8,128)(2,1)}, bf16[256,5760]{1,0:T(8,128)(2,1)S(1)}, u32[]{:S(2)}, u32[]{:S(2)}) collective-permute-start(bf16[256,5760]{1,0:T(8,128)(2,1)} %refs_0_.19), channel_id=1, source_target_pairs={{0,1},{1,0},{2,3},{3,2},{4,5},{5,4},{6,7},{7,6},{8,9},{9,8},{10,11... | collective-permute-start | bytes 8847368 | tf_op jit(solution)/shard_map/ppermute | solution.py:234
  1.4 9.6 %collective-permute-start.1 = (bf16[256,5760]{1,0:T(8,128)(2,1)}, bf16[256,5760]{1,0:T(8,128)(2,1)}, u32[]{:S(2)}, u32[]{:S(2)}) collective-permute-start(bf16[256,5760]{1,0:T(8,128)(2,1)} %refs_1_.19), channel_id=1, source_target_pairs={{0,1},{1,0},{2,3},{3,2},{4,5},{5,4},{6,7},{7,6},{8,9},{9,8},{10,11... | collective-permute-start | bytes 8847368 | tf_op jit(solution)/shard_map/ppermute | solution.py:234
  1.5 24.2 %copy-start.9 = (s32[2,45]{1,0:T(2,128)S(1)}, s32[2,45]{1,0:T(2,128)}, u32[]{:S(2)}) copy-start(s32[2,45]{1,0:T(2,128)} %own_mask.19) | copy-start | bytes 1084
  1.5 28.2 %copy-start.10 = (s32[32]{0:T(128)S(1)}, s32[32]{0:T(128)}, u32[]{:S(2)}) copy-start(s32[32]{0:T(128)} %owner_ref.19) | copy-start | bytes 388
  3.8 15.0 %collective-permute-start.6 = (s16[1168,256]{1,0:T(8,128)(2,1)}, s16[1168,256]{1,0:T(8,128)(2,1)}, u32[]{:S(2)}, u32[]{:S(2)}) collective-permute-start(s16[1168,256]{1,0:T(8,128)(2,1)} %pack.2.refs_2_.refs_4_), channel_id=1, source_target_pairs={{0,4},{1,5},{2,6},{3,7},{4,0},{5,1},{6,2},{7,3},{8,12},{9,13},{10,... | collective-permute-start | bytes 1794056 | tf_op jit(solution)/shard_map/ppermute | solution.py:234
  4.0 15.0 %collective-permute-start.5 = (s16[1168,256]{1,0:T(8,128)(2,1)}, s16[1168,256]{1,0:T(8,128)(2,1)S(1)}, u32[]{:S(2)}, u32[]{:S(2)}) collective-permute-start(s16[1168,256]{1,0:T(8,128)(2,1)} %pack.2.refs_2_.refs_4_), channel_id=1, source_target_pairs={{0,2},{1,3},{2,0},{3,1},{4,6},{5,7},{6,4},{7,5},{8,10},{9,11},{10,... | collective-permute-start | bytes 1794056 | tf_op jit(solution)/shard_map/ppermute | solution.py:234
  10.0 5.0 %copy-start = (bf16[256,5760]{1,0:T(8,128)(2,1)}, bf16[256,5760]{1,0:T(8,128)(2,1)S(1)}, u32[]{:S(2)}) copy-start(bf16[256,5760]{1,0:T(8,128)(2,1)S(1)} %collective-permute-done.refs_0_.refs_2_) | copy-start | bytes 8847364
  10.9 1.1 copy-start.5
  12.1 17.6 %copy-start.6 = (s16[1168,256]{1,0:T(8,128)(2,1)S(1)}, s16[1168,256]{1,0:T(8,128)(2,1)}, u32[]{:S(2)}) copy-start(s16[1168,256]{1,0:T(8,128)(2,1)} %pack.2.refs_2_.refs_4_) | copy-start | bytes 1794052
  15.0 6.9 %collective-permute-start.4 = (s16[1168,256]{1,0:T(8,128)(2,1)S(1)}, s16[1168,256]{1,0:T(8,128)(2,1)}, u32[]{:S(2)}, u32[]{:S(2)}) collective-permute-start(s16[1168,256]{1,0:T(8,128)(2,1)S(1)} %get-tuple-element.28), channel_id=1, source_target_pairs={{0,1},{1,0},{2,3},{3,2},{4,5},{5,4},{6,7},{7,6},{8,9},{9,8},{10,11... | collective-permute-start | bytes 1794056 | tf_op jit(solution)/shard_map/ppermute | solution.py:234
  15.5 6.5 %collective-permute-start.7 = (s16[1168,256]{1,0:T(8,128)(2,1)S(1)}, s16[1168,256]{1,0:T(8,128)(2,1)S(1)}, u32[]{:S(2)}, u32[]{:S(2)}) collective-permute-start(s16[1168,256]{1,0:T(8,128)(2,1)S(1)} %get-tuple-element.29), channel_id=1, source_target_pairs={{0,1},{1,0},{2,3},{3,2},{4,5},{5,4},{6,7},{7,6},{8,9},{9,8},{10,11... | collective-permute-start | bytes 1794056 | tf_op jit(solution)/shard_map/ppermute | solution.py:234
  15.6 22.8 %collective-permute-start.9 = (s16[1168,256]{1,0:T(8,128)(2,1)}, s16[1168,256]{1,0:T(8,128)(2,1)S(1)}, u32[]{:S(2)}, u32[]{:S(2)}) collective-permute-start(s16[1168,256]{1,0:T(8,128)(2,1)} %get-tuple-element.31.refs_5_), channel_id=1, source_target_pairs={{0,2},{1,3},{2,0},{3,1},{4,6},{5,7},{6,4},{7,5},{8,10},{9,11},{10,... | collective-permute-start | bytes 1794056 | tf_op jit(solution)/shard_map/ppermute | solution.py:234
  18.8 19.6 %collective-permute-start.10 = (s16[1168,256]{1,0:T(8,128)(2,1)}, s16[1168,256]{1,0:T(8,128)(2,1)}, u32[]{:S(2)}, u32[]{:S(2)}) collective-permute-start(s16[1168,256]{1,0:T(8,128)(2,1)} %get-tuple-element.31.refs_5_), channel_id=1, source_target_pairs={{0,4},{1,5},{2,6},{3,7},{4,0},{5,1},{6,2},{7,3},{8,12},{9,13},{10,... | collective-permute-start | bytes 1794056 | tf_op jit(solution)/shard_map/ppermute | solution.py:234
  19.0 0.8 copy-start.7
  19.8 21.5 %collective-permute-start.12 = (s16[1168,256]{1,0:T(8,128)(2,1)}, s16[1168,256]{1,0:T(8,128)(2,1)S(1)}, u32[]{:S(2)}, u32[]{:S(2)}) collective-permute-start(s16[1168,256]{1,0:T(8,128)(2,1)} %collective-permute-done.6.refs_4_), channel_id=1, source_target_pairs={{0,8},{1,9},{2,10},{3,11},{8,16},{9,17},{10,18},{11,19},{12,4},{13... | collective-permute-start | bytes 1794056 | tf_op jit(solution)/shard_map/ppermute | solution.py:234
  21.9 22.3 %collective-permute-start.8 = (s16[1168,256]{1,0:T(8,128)(2,1)}, s16[1168,256]{1,0:T(8,128)(2,1)S(1)}, u32[]{:S(2)}, u32[]{:S(2)}) collective-permute-start(s16[1168,256]{1,0:T(8,128)(2,1)} %collective-permute-done.4.refs_4_), channel_id=1, source_target_pairs={{0,2},{1,3},{2,0},{3,1},{4,6},{5,7},{6,4},{7,5},{8,10},{9,11},{10,... | collective-permute-start | bytes 1794056 | tf_op jit(solution)/shard_map/ppermute | solution.py:234
  22.3 3.4 %collective-permute-start.2 = (s32[1,5]{1,0:T(1,128)}, s32[1,5]{1,0:T(1,128)S(1)}, u32[]{:S(2)}, u32[]{:S(2)}) collective-permute-start(s32[1,5]{1,0:T(1,128)} %own_ids.19), channel_id=1, source_target_pairs={{0,1},{1,0},{2,3},{3,2},{4,5},{5,4},{6,7},{7,6},{8,9},{9,8},{10,11... | collective-permute-start | bytes 68 | tf_op jit(solution)/shard_map/ppermute | solution.py:234
  25.7 1.1 collective-permute-start.3
  26.0 20.2 %copy-start.12 = (s32[1,5]{1,0:T(1,128)S(1)}, s32[1,5]{1,0:T(1,128)}, u32[]{:S(2)}) copy-start(s32[1,5]{1,0:T(1,128)} %own_ids.19) | copy-start | bytes 64
  26.8 38.5 %collective-permute-start.14 = (s16[1168,256]{1,0:T(8,128)(2,1)}, s16[1168,256]{1,0:T(8,128)(2,1)S(1)}, u32[]{:S(2)}, u32[]{:S(2)}) collective-permute-start(s16[1168,256]{1,0:T(8,128)(2,1)} %collective-permute-done.4.refs_4_), channel_id=1, source_target_pairs={{0,4},{1,5},{2,6},{3,7},{4,0},{5,1},{6,2},{7,3},{8,12},{9,13},{10,... | collective-permute-start | bytes 1794056 | tf_op jit(solution)/shard_map/ppermute | solution.py:234
  29.6 1.8 %copy-start.1 = (bf16[256,5760]{1,0:T(8,128)(2,1)S(1)}, bf16[256,5760]{1,0:T(8,128)(2,1)}, u32[]{:S(2)}) copy-start(bf16[256,5760]{1,0:T(8,128)(2,1)} %refs_0_.19) | copy-start | bytes 8847364
  31.5 1.8 %copy-start.3 = (bf16[256,5760]{1,0:T(8,128)(2,1)S(1)}, bf16[256,5760]{1,0:T(8,128)(2,1)}, u32[]{:S(2)}) copy-start(bf16[256,5760]{1,0:T(8,128)(2,1)} %refs_1_.19) | copy-start | bytes 8847364
  33.3 0.7 copy-start.11
  34.0 12.2 %copy-start.2 = (bf16[256,5760]{1,0:T(8,128)(2,1)S(1)}, bf16[256,5760]{1,0:T(8,128)(2,1)}, u32[]{:S(2)}) copy-start(bf16[256,5760]{1,0:T(8,128)(2,1)} %refs_0_.19) | copy-start | bytes 8847364
  34.0 12.2 %copy-start.4 = (bf16[256,5760]{1,0:T(8,128)(2,1)S(1)}, bf16[256,5760]{1,0:T(8,128)(2,1)}, u32[]{:S(2)}) copy-start(bf16[256,5760]{1,0:T(8,128)(2,1)} %refs_1_.19) | copy-start | bytes 8847364
  38.4 18.7 %collective-permute-start.11 = (s16[1168,256]{1,0:T(8,128)(2,1)S(1)}, s16[1168,256]{1,0:T(8,128)(2,1)S(1)}, u32[]{:S(2)}, u32[]{:S(2)}) collective-permute-start(s16[1168,256]{1,0:T(8,128)(2,1)S(1)} %get-tuple-element.33.refs_5_), channel_id=1, source_target_pairs={{0,2},{1,3},{2,0},{3,1},{4,6},{5,7},{6,4},{7,5},{8,10},{9,11},{10,... | collective-permute-start | bytes 1794056 | tf_op jit(solution)/shard_map/ppermute | solution.py:234
  39.6 28.9 %collective-permute-start.22 = (s16[1168,256]{1,0:T(8,128)(2,1)S(1)}, s16[1168,256]{1,0:T(8,128)(2,1)S(1)}, u32[]{:S(2)}, u32[]{:S(2)}) collective-permute-start(s16[1168,256]{1,0:T(8,128)(2,1)S(1)} %get-tuple-element.33.refs_5_), channel_id=1, source_target_pairs={{0,4},{1,5},{2,6},{3,7},{4,0},{5,1},{6,2},{7,3},{8,12},{9,13},{10,... | collective-permute-start | bytes 1794056 | tf_op jit(solution)/shard_map/ppermute | solution.py:234
  41.4 20.7 %collective-permute-start.13 = (s16[1168,256]{1,0:T(8,128)(2,1)}, s16[1168,256]{1,0:T(8,128)(2,1)S(1)}, u32[]{:S(2)}, u32[]{:S(2)}) collective-permute-start(s16[1168,256]{1,0:T(8,128)(2,1)} %collective-permute-done.10.refs_5_), channel_id=1, source_target_pairs={{0,8},{1,9},{2,10},{3,11},{8,16},{9,17},{10,18},{11,19},{12,4},{13... | collective-permute-start | bytes 1794056 | tf_op jit(solution)/shard_map/ppermute | solution.py:234
  44.2 26.9 %collective-permute-start.20 = (s16[1168,256]{1,0:T(8,128)(2,1)S(1)}, s16[1168,256]{1,0:T(8,128)(2,1)S(1)}, u32[]{:S(2)}, u32[]{:S(2)}) collective-permute-start(s16[1168,256]{1,0:T(8,128)(2,1)S(1)} %collective-permute-done.9.refs_5_), channel_id=1, source_target_pairs={{4,12},{5,13},{10,2},{11,3},{12,20},{13,21},{18,10},{19,11},{20,28... | collective-permute-start | bytes 1794056 | tf_op jit(solution)/shard_map/ppermute | solution.py:234
  46.2 4.5 %copy-start.8 = (s16[1168,256]{1,0:T(8,128)(2,1)S(1)}, s16[1168,256]{1,0:T(8,128)(2,1)}, u32[]{:S(2)}) copy-start(s16[1168,256]{1,0:T(8,128)(2,1)} %copy-done.7) | copy-start | bytes 1794052
  57.0 19.2 %collective-permute-start.17 = (s16[1168,256]{1,0:T(8,128)(2,1)S(1)}, s16[1168,256]{1,0:T(8,128)(2,1)S(1)}, u32[]{:S(2)}, u32[]{:S(2)}) collective-permute-start(s16[1168,256]{1,0:T(8,128)(2,1)S(1)} %collective-permute-done.11.refs_5_), channel_id=1, source_target_pairs={{4,12},{5,13},{10,2},{11,3},{12,20},{13,21},{18,10},{19,11},{20,28... | collective-permute-start | bytes 1794056 | tf_op jit(solution)/shard_map/ppermute | solution.py:234
  62.1 37.6 %collective-permute-start.19 = (s16[1168,256]{1,0:T(8,128)(2,1)S(1)}, s16[1168,256]{1,0:T(8,128)(2,1)S(1)}, u32[]{:S(2)}, u32[]{:S(2)}) collective-permute-start(s16[1168,256]{1,0:T(8,128)(2,1)S(1)} %get-tuple-element.39), channel_id=1, source_target_pairs={{0,2},{1,3},{2,0},{3,1},{4,6},{5,7},{6,4},{7,5},{8,10},{9,11},{10,... | collective-permute-start | bytes 1794056 | tf_op jit(solution)/shard_map/ppermute | solution.py:234
  65.4 18.5 %collective-permute-start.15 = (s16[1168,256]{1,0:T(8,128)(2,1)S(1)}, s16[1168,256]{1,0:T(8,128)(2,1)S(1)}, u32[]{:S(2)}, u32[]{:S(2)}) collective-permute-start(s16[1168,256]{1,0:T(8,128)(2,1)S(1)} %collective-permute-done.14.refs_4_), channel_id=1, source_target_pairs={{0,8},{1,9},{2,10},{3,11},{8,16},{9,17},{10,18},{11,19},{12,4},{13... | collective-permute-start | bytes 1794056 | tf_op jit(solution)/shard_map/ppermute | solution.py:234
  68.5 27.6 %collective-permute-start.23 = (s16[1168,256]{1,0:T(8,128)(2,1)S(1)}, s16[1168,256]{1,0:T(8,128)(2,1)S(1)}, u32[]{:S(2)}, u32[]{:S(2)}) collective-permute-start(s16[1168,256]{1,0:T(8,128)(2,1)S(1)} %collective-permute-done.22.refs_5_), channel_id=1, source_target_pairs={{0,8},{1,9},{2,10},{3,11},{8,16},{9,17},{10,18},{11,19},{12,4},{13... | collective-permute-start | bytes 1794056 | tf_op jit(solution)/shard_map/ppermute | solution.py:234
  71.3 28.4 %collective-permute-start.21 = (s16[1168,256]{1,0:T(8,128)(2,1)S(1)}, s16[1168,256]{1,0:T(8,128)(2,1)S(1)}, u32[]{:S(2)}, u32[]{:S(2)}) collective-permute-start(s16[1168,256]{1,0:T(8,128)(2,1)S(1)} %broadcast_select_fusion), channel_id=1, source_target_pairs={{0,4},{1,5},{2,6},{3,7},{4,0},{5,1},{6,2},{7,3},{8,12},{9,13},{10,... | collective-permute-start | bytes 1794056 | tf_op jit(solution)/shard_map/ppermute | solution.py:234
  76.4 26.6 %collective-permute-start.18 = (s16[1168,256]{1,0:T(8,128)(2,1)S(1)}, s16[1168,256]{1,0:T(8,128)(2,1)S(1)}, u32[]{:S(2)}, u32[]{:S(2)}) collective-permute-start(s16[1168,256]{1,0:T(8,128)(2,1)S(1)} %broadcast_select_fusion.1), channel_id=1, source_target_pairs={{0,4},{1,5},{2,6},{3,7},{4,0},{5,1},{6,2},{7,3},{8,12},{9,13},{10,... | collective-permute-start | bytes 1794056 | tf_op jit(solution)/shard_map/ppermute | solution.py:234
  88.7 15.0 %collective-permute-start.16 = (s16[1168,256]{1,0:T(8,128)(2,1)S(1)}, s16[1168,256]{1,0:T(8,128)(2,1)S(1)}, u32[]{:S(2)}, u32[]{:S(2)}) collective-permute-start(s16[1168,256]{1,0:T(8,128)(2,1)S(1)} %get-tuple-element.37), channel_id=1, source_target_pairs={{0,2},{1,3},{2,0},{3,1},{4,6},{5,7},{6,4},{7,5},{8,10},{9,11},{10,... | collective-permute-start | bytes 1794056 | tf_op jit(solution)/shard_map/ppermute | solution.py:234
  102.9 11.2 %copy-start.13 = (s32[256]{0:T(256)S(1)}, s32[256]{0:T(256)}, u32[]{:S(2)}) copy-start(s32[256]{0:T(256)} %param.13) | copy-start | bytes 3076
  107.3 4.0 %collective-permute-start.24 = (bf16[2,2,32,512]{3,2,1,0:T(8,128)(2,1)S(1)}, bf16[2,2,32,512]{3,2,1,0:T(8,128)(2,1)S(1)}, u32[]{:S(2)}, u32[]{:S(2)}) collective-permute-start(bf16[2,2,32,512]{3,2,1,0:T(8,128)(2,1)S(1)} %get-tuple-element.43), channel_id=1, source_target_pairs={{0,1},{1,0},{2,3},{3,2},{4,5},{5,4},{6,7},{7,6},{8,9},{9,8},{10,11... | collective-permute-start | bytes 393224 | tf_op jit(solution)/shard_map/ppermute | solution.py:234
  107.8 5.1 %collective-permute-start.25 = (bf16[2,2,32,512]{3,2,1,0:T(8,128)(2,1)S(1)}, bf16[2,2,32,512]{3,2,1,0:T(8,128)(2,1)S(1)}, u32[]{:S(2)}, u32[]{:S(2)}) collective-permute-start(bf16[2,2,32,512]{3,2,1,0:T(8,128)(2,1)S(1)} %get-tuple-element.44), channel_id=1, source_target_pairs={{0,2},{1,3},{2,0},{3,1},{4,6},{5,7},{6,4},{7,5},{8,10},{9,11},{10,... | collective-permute-start | bytes 393224 | tf_op jit(solution)/shard_map/ppermute | solution.py:234
  107.8 8.8 %collective-permute-start.26 = (bf16[2,2,32,512]{3,2,1,0:T(8,128)(2,1)S(1)}, bf16[2,2,32,512]{3,2,1,0:T(8,128)(2,1)S(1)}, u32[]{:S(2)}, u32[]{:S(2)}) collective-permute-start(bf16[2,2,32,512]{3,2,1,0:T(8,128)(2,1)S(1)} %get-tuple-element.45), channel_id=1, source_target_pairs={{0,3},{1,2},{2,1},{3,0},{4,7},{5,6},{6,5},{7,4},{8,11},{9,10},{10,... | collective-permute-start | bytes 393224 | tf_op jit(solution)/shard_map/ppermute | solution.py:234
  109.5 7.1 %collective-permute-start.27 = (bf16[2,2,32,512]{3,2,1,0:T(8,128)(2,1)S(1)}, bf16[2,2,32,512]{3,2,1,0:T(8,128)(2,1)S(1)}, u32[]{:S(2)}, u32[]{:S(2)}) collective-permute-start(bf16[2,2,32,512]{3,2,1,0:T(8,128)(2,1)S(1)} %get-tuple-element.46), channel_id=1, source_target_pairs={{0,4},{1,5},{2,6},{3,7},{4,0},{5,1},{6,2},{7,3},{8,12},{9,13},{10,... | collective-permute-start | bytes 393224 | tf_op jit(solution)/shard_map/ppermute | solution.py:234
  110.1 13.0 %collective-permute-start.28 = (bf16[2,2,32,512]{3,2,1,0:T(8,128)(2,1)S(1)}, bf16[2,2,32,512]{3,2,1,0:T(8,128)(2,1)S(1)}, u32[]{:S(2)}, u32[]{:S(2)}) collective-permute-start(bf16[2,2,32,512]{3,2,1,0:T(8,128)(2,1)S(1)} %get-tuple-element.47), channel_id=1, source_target_pairs={{0,5},{1,4},{2,7},{3,6},{4,1},{5,0},{6,3},{7,2},{8,13},{9,12},{10,... | collective-permute-start | bytes 393224 | tf_op jit(solution)/shard_map/ppermute | solution.py:234
  111.3 11.9 %collective-permute-start.29 = (bf16[2,2,32,512]{3,2,1,0:T(8,128)(2,1)S(1)}, bf16[2,2,32,512]{3,2,1,0:T(8,128)(2,1)S(1)}, u32[]{:S(2)}, u32[]{:S(2)}) collective-permute-start(bf16[2,2,32,512]{3,2,1,0:T(8,128)(2,1)S(1)} %get-tuple-element.48), channel_id=1, source_target_pairs={{0,6},{1,7},{2,4},{3,5},{4,2},{5,3},{6,0},{7,1},{8,14},{9,15},{10,... | collective-permute-start | bytes 393224 | tf_op jit(solution)/shard_map/ppermute | solution.py:234
  112.9 10.3 %collective-permute-start.30 = (bf16[2,2,32,512]{3,2,1,0:T(8,128)(2,1)S(1)}, bf16[2,2,32,512]{3,2,1,0:T(8,128)(2,1)S(1)}, u32[]{:S(2)}, u32[]{:S(2)}) collective-permute-start(bf16[2,2,32,512]{3,2,1,0:T(8,128)(2,1)S(1)} %get-tuple-element.49), channel_id=1, source_target_pairs={{0,7},{1,6},{2,5},{3,4},{4,3},{5,2},{6,1},{7,0},{8,15},{9,14},{10,... | collective-permute-start | bytes 393224 | tf_op jit(solution)/shard_map/ppermute | solution.py:234
